TPU v7x, 32 devices: a whole 2x2x4 slice. The times are simulated.
32 devices in a mesh: fsdp: 8 (over y, x, core), tp: 4 (over z).
Axes of the slice: x: 2, y: 2, z: 4, core: 2. Of those that a mesh axis runs over, the one named last changes fastest.
Arguments:
- hidden_in: bfloat16 [2, 8, 1024, 2048], P(None, 'fsdp', 'tp'), may hold values from -6 to 6
- segment_ids: int32 [2, 8, 1024], P(None, 'fsdp'), may hold values from 0 to 15, never falling along the last dimension, each value on 1 to 512 neighbouring positions
- cotangent: bfloat16 [2, 8, 1024, 2048], P(None, 'fsdp', 'tp'), may hold values from -6 to 6
- norm_gain: float32 [2048], replicated, may hold values from 0.5 to 1.5
- proj_gate: bfloat16 [2048, 4096], P('fsdp', 'tp'), may hold values from -0.125 to 0.125
- proj_value: bfloat16 [2048, 4096], P('fsdp', 'tp'), may hold values from -0.125 to 0.125
- proj_state: bfloat16 [2048, 256], P('fsdp'), may hold values from -0.125 to 0.125
- proj_step: bfloat16 [2048, 64], P('fsdp', 'tp'), may hold values from -0.125 to 0.125
- conv_value: float32 [4, 4096], P(None, 'tp'), may hold values from -3 to 3
- conv_value_bias: float32 [4096], P('tp'), may hold values from -3 to 3
- conv_state: float32 [4, 256], replicated, may hold values from -3 to 3
- conv_state_bias: float32 [256], replicated, may hold values from -3 to 3
- step_bias: float32 [64], P('tp'), may hold values from -7 to -3
- decay_log: float32 [64], P('tp'), may hold values from -1.5 to 1.5
- skip_gain: float32 [64], P('tp'), may hold values from 0.5 to 1.5
- gate_gain: float32 [4096], P('tp'), may hold values from 0.25 to 1.75
- proj_out: bfloat16 [4096, 2048], P('tp', 'fsdp'), may hold values from -0.09375 to 0.09375
Outputs:
- block_out: bfloat16 [2, 8, 1024, 2048], P(None, 'fsdp', 'tp')
- grad_hidden: bfloat16 [2, 8, 1024, 2048], P(None, 'fsdp', 'tp')
- grad_norm_gain: float32 [2048], replicated
- grad_proj_gate: float32 [2048, 4096], P('fsdp', 'tp')
- grad_proj_value: float32 [2048, 4096], P('fsdp', 'tp')
- grad_proj_state: float32 [2048, 256], P('fsdp')
- grad_proj_step: float32 [2048, 64], P('fsdp', 'tp')
- grad_conv_value: float32 [4, 4096], P(None, 'tp')
- grad_conv_value_bias: float32 [4096], P('tp')
- grad_conv_state: float32 [4, 256], replicated
- grad_conv_state_bias: float32 [256], replicated
- grad_step_bias: float32 [64], P('tp')
- grad_decay_log: float32 [64], P('tp')
- grad_skip_gain: float32 [64], P('tp')
- grad_gate_gain: float32 [4096], P('tp')
- grad_proj_out: float32 [4096, 2048], P('tp', 'fsdp')
Inputs may be any that keep to these rules, and one draw needn't show every extreme that they name: `segment_ids`: ids of the documents packed in each sequence, from 0 and never falling; a document starts where the id changes; each sequence holds 16 documents, one of exactly 512 tokens.
All inputs are finite; a program needn't handle non-finite values.
Results may differ from a plain program's by a relative error of at most 0.019.
Values may be sent and summed in bfloat16 or wider, within the bound.
A program may use at most 96 MiB of HBM per device.

v0:
```python
from functools import partial

import jax
import jax.numpy as jnp
from jax import lax
from jax.sharding import PartitionSpec as P

HEAD_DIM = 64
STATE = 128
CONV = 4
GROUP = 256
LENGTH = 1024
INNER = 4096


EPSILON = 1e-05
PRECISE = lax.Precision.HIGHEST


def matmul(former, latter):
    return jnp.dot(former, latter, preferred_element_type=jnp.float32)


def contract_first(former, latter):
    return lax.dot_general(
        former, latter, (((0,), (0,)), ((), ())), preferred_element_type=jnp.float32
    )


def contract_last(former, latter):
    return lax.dot_general(
        former, latter, (((1,), (1,)), ((), ())), preferred_element_type=jnp.float32
    )


def silu_slope(values):
    sig_value = jax.nn.sigmoid(values)
    return sig_value * (1.0 + values * (1.0 - sig_value))


def shift_down(values, offset):
    return jnp.pad(values, ((offset, 0), (0, 0)))[: values.shape[0]]


def shift_up(values, offset):
    return jnp.pad(values, ((0, offset), (0, 0)))[offset:]


def document_masks(seg_row):
    doc_masks = []
    for offset in range(CONV):
        before = jnp.pad(seg_row, (offset, 0), constant_values=-1)[: seg_row.shape[0]]
        doc_masks.append((before == seg_row).astype(jnp.float32)[:, None])
    return doc_masks


def conv_apply(values, kernel, bias, doc_masks):
    summed = bias[None, :] + kernel[0][None, :] * values
    for offset in range(1, CONV):
        summed = summed + kernel[offset][None, :] * shift_down(values, offset) * doc_masks[offset]
    return summed


def conv_grad(grad_conv, values, kernel, doc_masks):
    masked = [grad_conv * doc_masks[offset] for offset in range(CONV)]
    grad_kernel = jnp.stack(
        [jnp.sum(masked[offset] * shift_down(values, offset), axis=0) for offset in range(CONV)]
    )
    grad_values = masked[0] * kernel[0][None, :]
    for offset in range(1, CONV):
        grad_values = grad_values + shift_up(masked[offset], offset) * kernel[offset][None, :]
    return (grad_values, grad_kernel, jnp.sum(grad_conv, axis=0))


def group_parts(decay_rate, x_values, b_values, c_values, step_size, seg_row, previous):
    positions = jnp.arange(seg_row.shape[0])
    cumulated = jnp.cumsum(step_size * decay_rate[None, :], axis=0)
    final_cum = cumulated[-1]
    within = (positions[:, None] >= positions[None, :]) & (seg_row[:, None] == seg_row[None, :])
    within_f = within.astype(jnp.float32)[None]
    decays = (
        jnp.exp(jnp.where(within[None], cumulated.T[:, :, None] - cumulated.T[:, None, :], 0.0))
        * within_f
    )
    inner_cb = contract_last(c_values, b_values)
    step_cols = step_size.T[:, None, :]
    mixing = (inner_cb[None] * decays * step_cols).astype(jnp.bfloat16)
    entering = jnp.exp(cumulated) * (seg_row == previous).astype(jnp.float32)[:, None]
    entry_low = (entering.T[:, :, None] * c_values.astype(jnp.float32)[None]).astype(jnp.bfloat16)
    at_end = (seg_row == seg_row[-1]).astype(jnp.float32)[:, None]
    fading = jnp.exp(final_cum[None, :] - cumulated) * at_end
    weights = fading * step_size
    weighted = (weights[:, :, None] * x_values.astype(jnp.float32)).astype(jnp.bfloat16)
    retain = jnp.exp(final_cum) * (seg_row[-1] == previous).astype(jnp.float32)
    return (
        decays,
        inner_cb,
        step_cols,
        mixing,
        entering,
        entry_low,
        fading,
        weights,
        weighted,
        retain,
    )


def group_forward(decay_rate, hidden, piece):
    x_values, b_values, c_values, step_size, seg_row, previous = piece
    parts = group_parts(decay_rate, x_values, b_values, c_values, step_size, seg_row, previous)
    mixing, entry_low, weighted, retain = (parts[3], parts[5], parts[8], parts[9])
    intra = jnp.einsum("hts,shp->thp", mixing, x_values, preferred_element_type=jnp.float32)
    carried = jnp.einsum(
        "htn,hnp->thp", entry_low, hidden.astype(jnp.bfloat16), preferred_element_type=jnp.float32
    )
    own_state = jnp.einsum("sn,shp->hnp", b_values, weighted, preferred_element_type=jnp.float32)
    return (retain[:, None, None] * hidden + own_state, (intra + carried, hidden))


def group_backward(decay_rate, grad_next, piece):
    x_values, b_values, c_values, step_size, seg_row, previous, hidden, grad_out = piece
    decays, inner_cb, step_cols, mixing, entering, entry_low, fading, weights, weighted, retain = (
        group_parts(decay_rate, x_values, b_values, c_values, step_size, seg_row, previous)
    )
    grad_own = grad_next.astype(jnp.bfloat16)
    grad_weighted = jnp.einsum(
        "sn,hnp->shp", b_values, grad_own, preferred_element_type=jnp.float32
    )
    grad_bvals = jnp.einsum("shp,hnp->sn", weighted, grad_own, preferred_element_type=jnp.float32)
    grad_hidden = retain[:, None, None] * grad_next + jnp.einsum(
        "htn,thp->hnp", entry_low, grad_out, preferred_element_type=jnp.float32
    )
    grad_entry = jnp.einsum(
        "thp,hnp->htn", grad_out, hidden.astype(jnp.bfloat16), preferred_element_type=jnp.float32
    )
    grad_mixing = jnp.einsum("thp,shp->hts", grad_out, x_values, preferred_element_type=jnp.float32)
    grad_xvals = jnp.einsum("hts,thp->shp", mixing, grad_out, preferred_element_type=jnp.float32)
    through = grad_mixing * inner_cb[None] * decays
    spread = through * step_cols
    grad_inner = jnp.sum(grad_mixing * decays * step_cols, axis=0).astype(jnp.bfloat16)
    c_float = c_values.astype(jnp.float32)
    grad_cvals = matmul(grad_inner, b_values) + jnp.einsum(
        "th,htn->tn", entering, grad_entry, precision=PRECISE
    )
    grad_bvals = grad_bvals + contract_first(grad_inner, c_values)
    grad_entering = jnp.einsum("tn,htn->th", c_float, grad_entry, precision=PRECISE)
    grad_weights = jnp.sum(x_values.astype(jnp.float32) * grad_weighted, axis=2)
    grad_xvals = grad_xvals + weights[:, :, None] * grad_weighted
    grad_cums = (
        (jnp.sum(spread, axis=2) - jnp.sum(spread, axis=1)).T
        + grad_entering * entering
        - grad_weights * weights
    )
    grad_final = jnp.sum(grad_weights * weights, axis=0) + retain * jnp.sum(
        hidden * grad_next, axis=(1, 2)
    )
    final_row = (jnp.arange(seg_row.shape[0]) == seg_row.shape[0] - 1).astype(jnp.float32)[:, None]
    grad_cums = grad_cums + final_row * grad_final[None, :]
    grad_rate = lax.cumsum(grad_cums, axis=0, reverse=True)
    grad_step = jnp.sum(through, axis=1).T + grad_weights * fading + grad_rate * decay_rate[None, :]
    grad_decay = jnp.sum(grad_rate * step_size, axis=0)
    return (grad_hidden, (grad_xvals, grad_bvals, grad_cvals, grad_step, grad_decay))


def local(
    hidden_in,
    segment_ids,
    cotangent,
    norm_gain,
    proj_gate,
    proj_value,
    proj_state,
    proj_step,
    conv_value,
    conv_value_bias,
    conv_state,
    conv_state_bias,
    step_bias,
    decay_log,
    skip_gain,
    gate_gain,
    proj_out,
):
    heads_here = step_bias.shape[0]
    inner_here = proj_gate.shape[1]
    rows_here = hidden_in.shape[2]
    group_count = LENGTH // GROUP
    decay_rate = -jnp.exp(decay_log)
    leader = (lax.axis_index("tp") == 0).astype(jnp.float32)

    def micro_step(carry, micro_item):
        big_sums, small_sums, gain_sum = carry
        rows_in, seg_row, cotan_rows = micro_item
        gate_w, value_w, state_w, step_w, out_w = (
            lax.all_gather(proj_gate, "fsdp", axis=0, tiled=True),
            lax.all_gather(proj_value, "fsdp", axis=0, tiled=True),
            lax.all_gather(proj_state, "fsdp", axis=0, tiled=True),
            lax.all_gather(proj_step, "fsdp", axis=0, tiled=True),
            lax.all_gather(proj_out, "fsdp", axis=1, tiled=True),
        )
        rows_float = rows_in.astype(jnp.float32)
        inv_root = lax.rsqrt(jnp.mean(rows_float * rows_float, axis=-1, keepdims=True) + EPSILON)
        normed = rows_float * inv_root
        input_rows = (normed * norm_gain[None, :]).astype(jnp.bfloat16)
        inputs = lax.all_gather(input_rows, "tp", axis=0, tiled=True)
        gate_raw = matmul(inputs, gate_w)
        value_raw = matmul(inputs, value_w)
        state_raw = matmul(inputs, state_w)
        step_raw = matmul(inputs, step_w)
        doc_masks = document_masks(seg_row)
        value_conv = conv_apply(value_raw, conv_value, conv_value_bias, doc_masks)
        state_conv = conv_apply(state_raw, conv_state, conv_state_bias, doc_masks)
        x_values = jax.nn.silu(value_conv).astype(jnp.bfloat16)
        bc_values = jax.nn.silu(state_conv).astype(jnp.bfloat16)
        b_values = bc_values[:, :STATE]
        c_values = bc_values[:, STATE:]
        step_in = step_raw + step_bias[None, :]
        step_size = jax.nn.softplus(step_in)
        previous = jnp.concatenate(
            [jnp.full((1,), -1, seg_row.dtype), seg_row[GROUP - 1 : -1 : GROUP]]
        )
        head_view = x_values.reshape(LENGTH, heads_here, HEAD_DIM)
        pieces = (
            head_view.reshape(group_count, GROUP, heads_here, HEAD_DIM),
            b_values.reshape(group_count, GROUP, STATE),
            c_values.reshape(group_count, GROUP, STATE),
            step_size.reshape(group_count, GROUP, heads_here),
            seg_row.reshape(group_count, GROUP),
            previous,
        )
        start_state = jnp.zeros((heads_here, STATE, HEAD_DIM), jnp.float32)
        _, (scanned, kept_states) = lax.scan(
            partial(group_forward, decay_rate), start_state, pieces
        )
        scanned = scanned.reshape(LENGTH, heads_here, HEAD_DIM)
        mixed = (scanned + skip_gain[None, :, None] * head_view).reshape(LENGTH, inner_here)
        gate_act = jax.nn.silu(gate_raw)
        gated = mixed * gate_act
        square_sum = lax.psum(jnp.sum(gated * gated, axis=-1), "tp")
        scaling = lax.rsqrt(square_sum / INNER + EPSILON)[:, None]
        branch = (gated * scaling * gate_gain[None, :]).astype(jnp.bfloat16)
        produced = lax.psum_scatter(
            matmul(branch, out_w).astype(jnp.bfloat16), "tp", scatter_dimension=0, tiled=True
        ).astype(jnp.float32)
        block_rows = (rows_float + produced).astype(jnp.bfloat16)
        cotan_all = lax.all_gather(cotan_rows, "tp", axis=0, tiled=True)
        grad_out_w = contract_first(branch, cotan_all)
        grad_branch = contract_last(cotan_all, out_w)
        grad_gate_gain = jnp.sum(grad_branch * gated * scaling, axis=0)
        grad_scaled = grad_branch * gate_gain[None, :]
        inner_dot = lax.psum(jnp.sum(grad_scaled * gated, axis=-1), "tp")
        grad_gated = scaling * grad_scaled - gated * scaling**3 * (inner_dot / INNER)[:, None]
        grad_mixed = grad_gated * gate_act
        grad_gate_raw = grad_gated * mixed * silu_slope(gate_raw)
        grad_heads = grad_mixed.reshape(LENGTH, heads_here, HEAD_DIM)
        grad_skip = jnp.sum(grad_heads * head_view, axis=(0, 2))
        grad_scan = grad_heads.astype(jnp.bfloat16)
        back_pieces = pieces + (
            kept_states,
            grad_scan.reshape(group_count, GROUP, heads_here, HEAD_DIM),
        )
        _, (grad_xchunks, grad_bchunks, grad_cchunks, grad_stepchunks, grad_decays) = lax.scan(
            partial(group_backward, decay_rate),
            jnp.zeros_like(start_state),
            back_pieces,
            reverse=True,
        )
        grad_xvals = (
            grad_xchunks.reshape(LENGTH, heads_here, HEAD_DIM)
            + skip_gain[None, :, None] * grad_heads
        )
        state_part = jnp.concatenate(
            [grad_bchunks.reshape(LENGTH, STATE), grad_cchunks.reshape(LENGTH, STATE)], axis=1
        )
        grad_bcvals = lax.psum(state_part.astype(jnp.bfloat16), "tp").astype(jnp.float32)
        grad_value_conv = grad_xvals.reshape(LENGTH, inner_here) * silu_slope(value_conv)
        grad_value_raw, grad_conv_value, grad_conv_value_bias = conv_grad(
            grad_value_conv, value_raw, conv_value, doc_masks
        )
        grad_state_conv = grad_bcvals * silu_slope(state_conv)
        grad_state_raw, grad_conv_state, grad_conv_state_bias = conv_grad(
            grad_state_conv, state_raw, conv_state, doc_masks
        )
        grad_step_in = grad_stepchunks.reshape(LENGTH, heads_here) * jax.nn.sigmoid(step_in)
        grad_step_bias = jnp.sum(grad_step_in, axis=0)
        grad_decay_log = jnp.sum(grad_decays, axis=0) * decay_rate
        low_gate = grad_gate_raw.astype(jnp.bfloat16)
        low_value = grad_value_raw.astype(jnp.bfloat16)
        low_state = grad_state_raw.astype(jnp.bfloat16)
        low_step = grad_step_in.astype(jnp.bfloat16)
        big_grads = (
            contract_first(inputs, low_gate),
            contract_first(inputs, low_value),
            contract_first(inputs, low_state),
            contract_first(inputs, low_step),
            grad_out_w,
        )

        def rows_of(values):
            return lax.slice_in_dim(values, 0, rows_here * lax.axis_size("tp"), axis=0)

        summed = contract_last(rows_of(low_gate), gate_w) + contract_last(
            rows_of(low_value), value_w
        )
        summed = summed + contract_last(rows_of(low_step), step_w)
        grad_inputs = lax.psum_scatter(
            (summed + leader * contract_last(rows_of(low_state), state_w)).astype(jnp.bfloat16),
            "tp",
            scatter_dimension=0,
            tiled=True,
        ).astype(jnp.float32)
        grad_norm_gain = jnp.sum(grad_inputs * normed, axis=0)
        grad_normed = grad_inputs * norm_gain[None, :]
        grad_rows = inv_root * grad_normed - rows_float * inv_root**3 * jnp.mean(
            grad_normed * rows_float, axis=-1, keepdims=True
        )
        grad_hidden_rows = (cotan_rows.astype(jnp.float32) + grad_rows).astype(jnp.bfloat16)
        big_grads = (
            lax.psum_scatter(big_grads[0], "fsdp", scatter_dimension=0, tiled=True),
            lax.psum_scatter(big_grads[1], "fsdp", scatter_dimension=0, tiled=True),
            lax.psum_scatter(big_grads[2], "fsdp", scatter_dimension=0, tiled=True),
            lax.psum_scatter(big_grads[3], "fsdp", scatter_dimension=0, tiled=True),
            lax.psum_scatter(big_grads[4], "fsdp", scatter_dimension=1, tiled=True),
        )
        big_sums = tuple((former + latter for former, latter in zip(big_sums, big_grads)))
        small_grads = (
            grad_conv_value,
            grad_conv_value_bias,
            grad_conv_state,
            grad_conv_state_bias,
            grad_step_bias,
            grad_decay_log,
            grad_skip,
            grad_gate_gain,
        )
        small_sums = tuple((former + latter for former, latter in zip(small_sums, small_grads)))
        return ((big_sums, small_sums, gain_sum + grad_norm_gain), (block_rows, grad_hidden_rows))

    big_start = (
        jnp.zeros(proj_gate.shape, jnp.float32),
        jnp.zeros(proj_value.shape, jnp.float32),
        jnp.zeros(proj_state.shape, jnp.float32),
        jnp.zeros(proj_step.shape, jnp.float32),
        jnp.zeros(proj_out.shape, jnp.float32),
    )
    small_start = (
        jnp.zeros(conv_value.shape, jnp.float32),
        jnp.zeros(conv_value_bias.shape, jnp.float32),
        jnp.zeros(conv_state.shape, jnp.float32),
        jnp.zeros(conv_state_bias.shape, jnp.float32),
        jnp.zeros(step_bias.shape, jnp.float32),
        jnp.zeros(decay_log.shape, jnp.float32),
        jnp.zeros(skip_gain.shape, jnp.float32),
        jnp.zeros(gate_gain.shape, jnp.float32),
    )
    gain_start = jnp.zeros(norm_gain.shape, jnp.float32)
    (big_sums, small_sums, gain_sum), (block_rows, grad_hidden_rows) = lax.scan(
        micro_step,
        (big_start, small_start, gain_start),
        (hidden_in[:, 0], segment_ids[:, 0], cotangent[:, 0]),
    )
    small_total = lax.psum(
        (
            small_sums[0],
            small_sums[1],
            small_sums[2],
            small_sums[3],
            small_sums[4],
            small_sums[5],
            small_sums[6],
            small_sums[7],
        ),
        "fsdp",
    )
    gain_total = lax.psum(gain_sum, ("fsdp", "tp"))
    return (
        block_rows[:, None],
        grad_hidden_rows[:, None],
        gain_total,
        big_sums[0],
        big_sums[1],
        big_sums[2],
        big_sums[3],
        small_total[0],
        small_total[1],
        small_total[2],
        small_total[3],
        small_total[4],
        small_total[5],
        small_total[6],
        small_total[7],
        big_sums[4],
    )


def solution(mesh):
    in_specs = (
        P(None, "fsdp", "tp", None),
        P(None, "fsdp", None),
        P(None, "fsdp", "tp", None),
        P(),
        P("fsdp", "tp"),
        P("fsdp", "tp"),
        P("fsdp", None),
        P("fsdp", "tp"),
        P(None, "tp"),
        P("tp"),
        P(),
        P(),
        P("tp"),
        P("tp"),
        P("tp"),
        P("tp"),
        P("tp", "fsdp"),
    )
    out_specs = (
        P(None, "fsdp", "tp", None),
        P(None, "fsdp", "tp", None),
        P(),
        P("fsdp", "tp"),
        P("fsdp", "tp"),
        P("fsdp", None),
        P("fsdp", "tp"),
        P(None, "tp"),
        P("tp"),
        P(),
        P(),
        P("tp"),
        P("tp"),
        P("tp"),
        P("tp"),
        P("tp", "fsdp"),
    )
    return jax.shard_map(local, mesh=mesh, in_specs=in_specs, out_specs=out_specs, check_vma=False)
```

profile of v0, /device:TPU:0, one launch (start us, length us, event | category | flops | bytes accessed | tf_op | source)
XLA Modules:
  0.0 2286.8 jit_solution(2784296955852652867)
XLA Ops:
  9.8 2206.1 %while.144 = (s32[]{:T(128)}, f32[256,1024]{1,0:T(8,128)}, f32[256,1024]{1,0:T(8,128)}, f32[256,256]{1,0:T(8,128)}, f32[256,16]{0,1:T(8,128)}, /*index=5*/f32[10...) while((s32[]{:T(128)}, f32[256,1024]{1,0:T(8,128)}, ...), condition=%wide.region_49.50_spmd.clone, body=%wide.region_0.49_spmd.clone.sunk | while | flops 43134263296 | bytes 859342272 | solution.py:358
  21.4 10.5 all_gather.77
  39.0 82.4 %all-gather.11.cloned.1.call-done = bf16[1024,2048]{1,0:T(8,128)(2,1)} async-done(((bf16[256,2048]{1,0:T(8,128)(2,1)}), bf16[1024,2048]{1,0:T(8,128)(2,1)}) %all-gather.11.cloned.1.call-update) | async-done | bytes 4194320 | tf_op jit(solution)/shard_map/while/body/eval_jaxpr/all_gather | solution.py:206
  130.5 28.0 %all-gather.13.cloned.1.call-done = bf16[2048,1024]{1,0:T(8,128)(2,1)} async-done(((bf16[256,1024]{1,0:T(8,128)(2,1)}), bf16[2048,1024]{1,0:T(8,128)(2,1)}) %all-gather.13.cloned.1.call-update) | async-done | bytes 4194320 | tf_op jit(solution)/shard_map/while/body/eval_jaxpr/all_gather | solution.py:197
  158.6 7.5 fusion.338
  175.1 5.8 copy.240
  183.4 68.5 %while.145 = (s32[]{:T(128)}, f32[16,128,64]{1,2,0:T(8,128)S(1)}, f32[4,256,16,64]{1,3,2,0:T(8,128)}, f32[4,16,128,64]{2,3,1,0:T(8,128)}, f32[4,256,16]{1,0,2:T(...) while((s32[]{:T(128)}, f32[16,128,64]{1,2,0:T(8,128)S(1)}, ...), condition=%wide.region_5.5_spmd.clone, body=%wide.region_2.4_spmd.clone.sunk | while | flops 295105600 | bytes 8877419 | solution.py:233
  251.9 8.2 copy.241
  260.1 8.3 reshape.621
  268.4 12.8 multiply_reduce_fusion.19
  281.3 11.8 psum.117
  293.1 23.9 %all-gather.19.cloned.1.call-done = bf16[1024,2048]{1,0:T(8,128)(2,1)} async-done(((bf16[1024,256]{1,0:T(8,128)(2,1)}), bf16[1024,2048]{1,0:T(8,128)(2,1)}) %all-gather.19.cloned.1.call-update) | async-done | bytes 4194320 | tf_op jit(solution)/shard_map/while/body/eval_jaxpr/all_gather | solution.py:200
  317.1 11.9 multiply_reduce_fusion.20
  329.0 11.7 psum.118
  340.7 9.2 fusion.343
  366.3 242.1 %while.146 = (s32[]{:T(128)}, f32[16,128,64]{1,2,0:T(8,128)S(1)}, f32[4,256,16,64]{1,3,2,0:T(8,128)}, bf16[4,256,128]{2,1,0:T(8,128)(2,1)}, bf16[4,256,128]{2,1,...) while((s32[]{:T(128)}, f32[16,128,64]{1,2,0:T(8,128)S(1)}, ...), condition=%wide.region_24.24_spmd.clone, body=%wide.region_11.23_spmd.clone.sunk | while | flops 624150208 | bytes 43844252 | solution.py:263
  610.4 8.2 copy.243
  618.6 7.7 reshape.623
  626.5 17.3 fusion.345
  645.4 8.5 fusion.346
  662.7 7.2 fusion.358
  669.8 6.7 fusion.357
  676.5 8.9 add_convert_fusion.2
  686.1 10.0 convolution_convert_fusion.2
  696.4 10.9 fusion.347
  707.4 11.4 fusion.353
  719.1 9.1 fusion.344
  731.8 74.4 %reduce-scatter.18.cloned.1.call-done = bf16[256,2048]{1,0:T(8,128)(2,1)} async-done(((bf16[1024,2048]{1,0:T(8,128)(2,1)}), bf16[256,2048]{1,0:T(8,128)(2,1)}) %reduce-scatter.18.cloned.1.call-update) | async-done | bytes 1048592 | tf_op jit(solution)/shard_map/while/body/eval_jaxpr/reduce_scatter | solution.py:307
  808.5 77.3 %reduce-scatter.20.cloned.1.call-done = bf16[256,2048]{1,0:T(8,128)(2,1)} async-done(((bf16[1024,2048]{1,0:T(8,128)(2,1)}), bf16[256,2048]{1,0:T(8,128)(2,1)}) %reduce-scatter.20.cloned.1.call-update) | async-done | bytes 1048592 | tf_op jit(solution)/shard_map/while/body/eval_jaxpr/reduce_scatter | solution.py:243
  890.0 71.3 %reduce-scatter.10.cloned.1.call-done = f32[256,1024]{1,0:T(8,128)} async-done(((f32[2048,1024]{1,0:T(8,128)}), f32[256,1024]{1,0:T(8,128)}) %reduce-scatter.10.cloned.1.call-update) | async-done | bytes 1048592 | tf_op jit(solution)/shard_map/while/body/eval_jaxpr/reduce_scatter | solution.py:321
  963.0 73.2 %reduce-scatter.16.cloned.1.call-done = f32[1024,256]{1,0:T(8,128)} async-done(((f32[1024,2048]{1,0:T(8,128)}), f32[1024,256]{1,0:T(8,128)}) %reduce-scatter.16.cloned.1.call-update) | async-done | bytes 1048592 | tf_op jit(solution)/shard_map/while/body/eval_jaxpr/reduce_scatter | solution.py:324
  1038.5 72.3 %reduce-scatter.8.cloned.1.call-done = f32[256,1024]{1,0:T(8,128)} async-done(((f32[2048,1024]{1,0:T(8,128)}), f32[256,1024]{1,0:T(8,128)}) %reduce-scatter.8.cloned.1.call-update) | async-done | bytes 1048592 | tf_op jit(solution)/shard_map/while/body/eval_jaxpr/reduce_scatter | solution.py:320
  1124.8 8.9 all_gather.77
  1139.6 82.2 %all-gather.11.cloned.1.call-done = bf16[1024,2048]{1,0:T(8,128)(2,1)} async-done(((bf16[256,2048]{1,0:T(8,128)(2,1)}), bf16[1024,2048]{1,0:T(8,128)(2,1)}) %all-gather.11.cloned.1.call-update) | async-done | bytes 4194320 | tf_op jit(solution)/shard_map/while/body/eval_jaxpr/all_gather | solution.py:206
  1231.0 27.9 %all-gather.13.cloned.1.call-done = bf16[2048,1024]{1,0:T(8,128)(2,1)} async-done(((bf16[256,1024]{1,0:T(8,128)(2,1)}), bf16[2048,1024]{1,0:T(8,128)(2,1)}) %all-gather.13.cloned.1.call-update) | async-done | bytes 4194320 | tf_op jit(solution)/shard_map/while/body/eval_jaxpr/all_gather | solution.py:197
  1258.8 7.5 fusion.338
  1283.7 68.5 %while.145 = (s32[]{:T(128)}, f32[16,128,64]{1,2,0:T(8,128)S(1)}, f32[4,256,16,64]{1,3,2,0:T(8,128)}, f32[4,16,128,64]{2,3,1,0:T(8,128)}, f32[4,256,16]{1,0,2:T(...) while((s32[]{:T(128)}, f32[16,128,64]{1,2,0:T(8,128)S(1)}, ...), condition=%wide.region_5.5_spmd.clone, body=%wide.region_2.4_spmd.clone.sunk | while | flops 295105600 | bytes 8877419 | solution.py:233
  1352.2 8.2 copy.241
  1360.3 7.9 reshape.621
  1368.3 12.8 multiply_reduce_fusion.19
  1381.1 11.8 psum.117
  1393.0 24.5 %all-gather.19.cloned.1.call-done = bf16[1024,2048]{1,0:T(8,128)(2,1)} async-done(((bf16[1024,256]{1,0:T(8,128)(2,1)}), bf16[1024,2048]{1,0:T(8,128)(2,1)}) %all-gather.19.cloned.1.call-update) | async-done | bytes 4194320 | tf_op jit(solution)/shard_map/while/body/eval_jaxpr/all_gather | solution.py:200
  1417.5 11.9 multiply_reduce_fusion.20
  1429.4 11.7 psum.118
  1441.1 9.2 fusion.343
  1466.7 242.3 %while.146 = (s32[]{:T(128)}, f32[16,128,64]{1,2,0:T(8,128)S(1)}, f32[4,256,16,64]{1,3,2,0:T(8,128)}, bf16[4,256,128]{2,1,0:T(8,128)(2,1)}, bf16[4,256,128]{2,1,...) while((s32[]{:T(128)}, f32[16,128,64]{1,2,0:T(8,128)S(1)}, ...), condition=%wide.region_24.24_spmd.clone, body=%wide.region_11.23_spmd.clone.sunk | while | flops 624150208 | bytes 43844252 | solution.py:263
  1711.0 8.2 copy.243
  1719.2 7.7 reshape.623
  1727.1 17.3 fusion.345
  1746.1 8.5 fusion.346
  1763.3 6.9 fusion.358
  1770.2 6.7 fusion.357
  1776.9 8.9 add_convert_fusion.2
  1786.5 10.0 convolution_convert_fusion.2
  1796.8 11.0 fusion.347
  1807.8 11.4 fusion.353
  1819.6 9.1 fusion.344
  1832.3 74.5 %reduce-scatter.18.cloned.1.call-done = bf16[256,2048]{1,0:T(8,128)(2,1)} async-done(((bf16[1024,2048]{1,0:T(8,128)(2,1)}), bf16[256,2048]{1,0:T(8,128)(2,1)}) %reduce-scatter.18.cloned.1.call-update) | async-done | bytes 1048592 | tf_op jit(solution)/shard_map/while/body/eval_jaxpr/reduce_scatter | solution.py:307
  1909.1 77.3 %reduce-scatter.20.cloned.1.call-done = bf16[256,2048]{1,0:T(8,128)(2,1)} async-done(((bf16[1024,2048]{1,0:T(8,128)(2,1)}), bf16[256,2048]{1,0:T(8,128)(2,1)}) %reduce-scatter.20.cloned.1.call-update) | async-done | bytes 1048592 | tf_op jit(solution)/shard_map/while/body/eval_jaxpr/reduce_scatter | solution.py:243
  1990.5 71.4 %reduce-scatter.10.cloned.1.call-done = f32[256,1024]{1,0:T(8,128)} async-done(((f32[2048,1024]{1,0:T(8,128)}), f32[256,1024]{1,0:T(8,128)}) %reduce-scatter.10.cloned.1.call-update) | async-done | bytes 1048592 | tf_op jit(solution)/shard_map/while/body/eval_jaxpr/reduce_scatter | solution.py:321
  2063.5 73.0 %reduce-scatter.16.cloned.1.call-done = f32[1024,256]{1,0:T(8,128)} async-done(((f32[1024,2048]{1,0:T(8,128)}), f32[1024,256]{1,0:T(8,128)}) %reduce-scatter.16.cloned.1.call-update) | async-done | bytes 1048592 | tf_op jit(solution)/shard_map/while/body/eval_jaxpr/reduce_scatter | solution.py:324
  2139.2 72.1 %reduce-scatter.8.cloned.1.call-done = f32[256,1024]{1,0:T(8,128)} async-done(((f32[2048,1024]{1,0:T(8,128)}), f32[256,1024]{1,0:T(8,128)}) %reduce-scatter.8.cloned.1.call-update) | async-done | bytes 1048592 | tf_op jit(solution)/shard_map/while/body/eval_jaxpr/reduce_scatter | solution.py:320
  2215.8 24.4 %all-reduce.15 = (f32[4,1024]{1,0:T(4,128)}, f32[1024]{0:T(1024)}, f32[4,256]{1,0:T(4,128)}, f32[256]{0:T(256)}, f32[16]{0:T(128)}, /*index=5*/f32[16]{0:T(128)}, f32[16]{0:T(128)}, f32[1024]{0:T(1024)}) all-reduce(f32[4,1024]{1,0:T(4,128)} %get-tuple-element.1138, ...), channel_id=1, replica_groups=mesh['fsdp'=8,'tp'=4] {'fsdp'}, use_global_device_ids=true, to_apply=%region_51.52 | all-reduce | flops 7472 | bytes 59776 | tf_op jit(solution)/shard_map/psum | solution.py:363
  2240.2 39.6 %psum.102 = f32[2048]{0:T(1024)} all-reduce(f32[2048]{0:T(1024)} %get-tuple-element.1133), channel_id=1, replica_groups=mesh['fsdp'=8,'tp'=4] {'fsdp','tp'}, use_global_device_ids=true, to_apply=%region_50.51 | all-reduce | flops 2048 | bytes 16384 | tf_op jit(solution)/shard_map/psum | solution.py:376
  (1431 shorter events, 774.1 us)
Async XLA Ops:
  10.1 29.0 %all-gather.15.cloned.1.call-start = ((), (), s32[]{:S(2)}) async-start(), calls=%async_computation.9 | async-start | bytes 1179648 | tf_op jit(solution)/shard_map/while/body/eval_jaxpr/all_gather | solution.py:198
  10.8 110.6 %all-gather.11.cloned.1.call-start = ((), (), s32[]{:S(2)}) async-start(), calls=%async_computation.7 | async-start | bytes 5242880 | tf_op jit(solution)/shard_map/while/body/eval_jaxpr/all_gather | solution.py:206
  16.1 142.4 %all-gather.13.cloned.1.call-start = ((), (), s32[]{:S(2)}) async-start(), calls=%async_computation.8 | async-start | bytes 4718592 | tf_op jit(solution)/shard_map/while/body/eval_jaxpr/all_gather | solution.py:197
  16.9 251.5 %all-gather.17.cloned.1.call-start = ((), (), s32[]{:S(2)}) async-start(), calls=%async_computation.10 | async-start | bytes 4718592 | tf_op jit(solution)/shard_map/while/body/eval_jaxpr/all_gather | solution.py:196
  17.5 275.6 %all-gather.21.cloned.1.call-start = ((), (), s32[]{:S(2)}) async-start(), calls=%async_computation.12 | async-start | bytes 5242880 | tf_op jit(solution)/shard_map/while/body/eval_jaxpr/all_gather | solution.py:247
  18.6 298.4 %all-gather.19.cloned.1.call-start = ((), (), s32[]{:S(2)}) async-start(), calls=%async_computation.11 | async-start | bytes 4718592 | tf_op jit(solution)/shard_map/while/body/eval_jaxpr/all_gather | solution.py:200
  19.2 634.8 %all-reduce.18.cloned.1.call-start = ((), (), s32[]{:S(2)}) async-start(), calls=%async_computation.15 | async-start | bytes 1048576 | tf_op jit(solution)/shard_map/while/body/eval_jaxpr/psum | solution.py:276
  21.2 144.9 %copy-start.45 = (f32[1024]{0:T(1024)}, f32[1024]{0:T(1024)S(1)}, u32[]{:S(2)}) copy-start(f32[1024]{0:T(1024)S(1)} %get-tuple-element.2259) | copy-start | bytes 12292 | tf_op jit(solution)/shard_map/while
  21.2 144.9 %copy-start.47 = (f32[1024]{0:T(1024)}, f32[1024]{0:T(1024)S(1)}, u32[]{:S(2)}) copy-start(f32[1024]{0:T(1024)S(1)} %get-tuple-element.2257) | copy-start | bytes 12292 | tf_op jit(solution)/shard_map/while
  21.2 144.9 %copy-start.49 = (f32[1024]{0:T(1024)}, f32[1024]{0:T(1024)S(1)}, u32[]{:S(2)}) copy-start(f32[1024]{0:T(1024)S(1)} %get-tuple-element.2255) | copy-start | bytes 12292 | tf_op jit(solution)/shard_map/while
  21.3 144.8 %copy-start.55 = (f32[1,1024]{1,0:T(1,128)}, f32[1,1024]{1,0:T(1,128)S(1)}, u32[]{:S(2)}) copy-start(f32[1,1024]{1,0:T(1,128)S(1)} %get-tuple-element.2261) | copy-start | bytes 12292 | tf_op jit(solution)/shard_map/while
  32.7 307.9 %copy-start.53 = (f32[1024]{0:T(1024)}, f32[1024]{0:T(1024)S(1)}, u32[]{:S(2)}) copy-start(f32[1024]{0:T(1024)S(1)} %mul.2480) | copy-start | bytes 12292 | tf_op jit(solution)/shard_map/while
  610.3 119.6 %reduce-scatter.14.cloned.1.call-start = ((), (), s32[]{:S(2)}) async-start(), calls=%async_computation.17 | async-start | bytes 147456 | tf_op jit(solution)/shard_map/while/body/eval_jaxpr/reduce_scatter | solution.py:323
  645.3 85.5 %reduce-scatter.12.cloned.1.call-start = ((), (), s32[]{:S(2)}) async-start(), calls=%async_computation.16 | async-start | bytes 2359296 | tf_op jit(solution)/shard_map/while/body/eval_jaxpr/reduce_scatter | solution.py:322
  659.8 146.5 %reduce-scatter.18.cloned.1.call-start = ((), (), s32[]{:S(2)}) async-start(), calls=%async_computation.19 | async-start | bytes 5242880 | tf_op jit(solution)/shard_map/while/body/eval_jaxpr/reduce_scatter | solution.py:307
  685.5 200.4 %reduce-scatter.20.cloned.1.call-start = ((), (), s32[]{:S(2)}) async-start(), calls=%async_computation.20 | async-start | bytes 5242880 | tf_op jit(solution)/shard_map/while/body/eval_jaxpr/reduce_scatter | solution.py:243
  696.2 265.2 %reduce-scatter.10.cloned.1.call-start = ((), (), s32[]{:S(2)}) async-start(), calls=%async_computation.14 | async-start | bytes 9437184 | tf_op jit(solution)/shard_map/while/body/eval_jaxpr/reduce_scatter | solution.py:321
  707.4 328.8 %reduce-scatter.16.cloned.1.call-start = ((), (), s32[]{:S(2)}) async-start(), calls=%async_computation.18 | async-start | bytes 9437184 | tf_op jit(solution)/shard_map/while/body/eval_jaxpr/reduce_scatter | solution.py:324
  718.8 391.9 %reduce-scatter.8.cloned.1.call-start = ((), (), s32[]{:S(2)}) async-start(), calls=%async_computation.13 | async-start | bytes 9437184 | tf_op jit(solution)/shard_map/while/body/eval_jaxpr/reduce_scatter | solution.py:320
  728.4 157.5 %copy-start.90 = (f32[256]{0:T(256)S(1)}, f32[256]{0:T(256)}, u32[]{:S(2)}) copy-start(f32[256]{0:T(256)} %get-tuple-element.2317) | copy-start | bytes 3076 | tf_op jit(solution)/shard_map/while
  729.1 160.8 %copy-start.98 = (f32[16]{0:T(128)}, f32[16]{0:T(128)S(1)}, u32[]{:S(2)}) copy-start(f32[16]{0:T(128)S(1)} %fusion.355) | copy-start | bytes 196 | tf_op jit(solution)/shard_map/while
  729.8 160.2 %copy-start.100 = (f32[16]{0:T(128)}, f32[16]{0:T(128)S(1)}, u32[]{:S(2)}) copy-start(f32[16]{0:T(128)S(1)} %get-tuple-element.2587) | copy-start | bytes 196 | tf_op jit(solution)/shard_map/while
  729.8 160.2 %copy-start.102 = (f32[16]{0:T(128)}, f32[16]{0:T(128)S(1)}, u32[]{:S(2)}) copy-start(f32[16]{0:T(128)S(1)} %get-tuple-element.2588) | copy-start | bytes 196 | tf_op jit(solution)/shard_map/while
  729.8 160.1 %copy-start.86 = (f32[1024]{0:T(1024)}, f32[1024]{0:T(1024)S(1)}, u32[]{:S(2)}) copy-start(f32[1024]{0:T(1024)S(1)} %select_add_fusion.23) | copy-start | bytes 12292 | tf_op jit(solution)/shard_map/while
  729.8 160.1 %copy-start.84 = (f32[1024]{0:T(1024)}, f32[1024]{0:T(1024)S(1)}, u32[]{:S(2)}) copy-start(f32[1024]{0:T(1024)S(1)} %select_add_fusion.25) | copy-start | bytes 12292 | tf_op jit(solution)/shard_map/while
  729.9 160.1 %copy-start.64 = (f32[4,1024]{1,0:T(4,128)}, f32[4,1024]{1,0:T(4,128)S(1)}, u32[]{:S(2)}) copy-start(f32[4,1024]{1,0:T(4,128)S(1)} %maximum_add_fusion.4) | copy-start | bytes 49156 | tf_op jit(solution)/shard_map/while
  730.7 159.3 %copy-start.69 = (f32[256,16]{0,1:T(8,128)}, f32[256,16]{0,1:T(8,128)S(1)}, u32[]{:S(2)}) copy-start(f32[256,16]{0,1:T(8,128)S(1)} %select_add_fusion.21) | copy-start | bytes 49156 | tf_op jit(solution)/shard_map/while
  730.7 159.3 %copy-start.95 = (f32[256]{0:T(256)}, f32[256]{0:T(256)S(1)}, u32[]{:S(2)}) copy-start(f32[256]{0:T(256)S(1)} %select_add_fusion.24) | copy-start | bytes 3076 | tf_op jit(solution)/shard_map/while
  730.7 159.2 %copy-start.88 = (f32[4,256]{1,0:T(4,128)}, f32[4,256]{1,0:T(4,128)S(1)}, u32[]{:S(2)}) copy-start(f32[4,256]{1,0:T(4,128)S(1)} %maximum_add_fusion.5) | copy-start | bytes 12292 | tf_op jit(solution)/shard_map/while
  731.8 158.2 %copy-start.40 = (f32[256,256]{1,0:T(8,128)}, f32[256,256]{1,0:T(8,128)S(1)}, u32[]{:S(2)}) copy-start(f32[256,256]{1,0:T(8,128)S(1)} %select_add_fusion.20) | copy-start | bytes 786436 | tf_op jit(solution)/shard_map/while
  731.8 229.5 %copy-start.27 = (f32[256,1024]{1,0:T(8,128)S(1)}, f32[256,1024]{1,0:T(8,128)}, u32[]{:S(2)}) copy-start(f32[256,1024]{1,0:T(8,128)} %get-tuple-element.2531) | copy-start | bytes 3145732 | tf_op jit(solution)/shard_map/while
  808.5 154.4 %copy-start.72 = (f32[2048]{0:T(1024)}, f32[2048]{0:T(1024)S(1)}, u32[]{:S(2)}) copy-start(f32[2048]{0:T(1024)S(1)} %select_add_fusion.26) | copy-start | bytes 24580 | tf_op jit(solution)/shard_map/while
  890.0 220.7 %copy-start.25 = (f32[256,1024]{1,0:T(8,128)S(1)}, f32[256,1024]{1,0:T(8,128)}, u32[]{:S(2)}) copy-start(f32[256,1024]{1,0:T(8,128)} %get-tuple-element.2530) | copy-start | bytes 3145732 | tf_op jit(solution)/shard_map/while
  962.9 149.4 %copy-start.28 = (f32[256,1024]{1,0:T(8,128)}, f32[256,1024]{1,0:T(8,128)S(1)}, u32[]{:S(2)}) copy-start(f32[256,1024]{1,0:T(8,128)S(1)} %select_add_fusion.19) | copy-start | bytes 3145732 | tf_op jit(solution)/shard_map/while
  1113.7 25.9 %all-gather.15.cloned.1.call-start = ((), (), s32[]{:S(2)}) async-start(), calls=%async_computation.9 | async-start | bytes 1179648 | tf_op jit(solution)/shard_map/while/body/eval_jaxpr/all_gather | solution.py:198
  1114.3 107.5 %all-gather.11.cloned.1.call-start = ((), (), s32[]{:S(2)}) async-start(), calls=%async_computation.7 | async-start | bytes 5242880 | tf_op jit(solution)/shard_map/while/body/eval_jaxpr/all_gather | solution.py:206
  1119.6 139.2 %all-gather.13.cloned.1.call-start = ((), (), s32[]{:S(2)}) async-start(), calls=%async_computation.8 | async-start | bytes 4718592 | tf_op jit(solution)/shard_map/while/body/eval_jaxpr/all_gather | solution.py:197
  1120.2 248.1 %all-gather.17.cloned.1.call-start = ((), (), s32[]{:S(2)}) async-start(), calls=%async_computation.10 | async-start | bytes 4718592 | tf_op jit(solution)/shard_map/while/body/eval_jaxpr/all_gather | solution.py:196
  1120.8 272.2 %all-gather.21.cloned.1.call-start = ((), (), s32[]{:S(2)}) async-start(), calls=%async_computation.12 | async-start | bytes 5242880 | tf_op jit(solution)/shard_map/while/body/eval_jaxpr/all_gather | solution.py:247
  1121.9 295.5 %all-gather.19.cloned.1.call-start = ((), (), s32[]{:S(2)}) async-start(), calls=%async_computation.11 | async-start | bytes 4718592 | tf_op jit(solution)/shard_map/while/body/eval_jaxpr/all_gather | solution.py:200
  1122.5 632.1 %all-reduce.18.cloned.1.call-start = ((), (), s32[]{:S(2)}) async-start(), calls=%async_computation.15 | async-start | bytes 1048576 | tf_op jit(solution)/shard_map/while/body/eval_jaxpr/psum | solution.py:276
  1134.5 306.6 %copy-start.53 = (f32[1024]{0:T(1024)}, f32[1024]{0:T(1024)S(1)}, u32[]{:S(2)}) copy-start(f32[1024]{0:T(1024)S(1)} %mul.2480) | copy-start | bytes 12292 | tf_op jit(solution)/shard_map/while
  1711.0 119.4 %reduce-scatter.14.cloned.1.call-start = ((), (), s32[]{:S(2)}) async-start(), calls=%async_computation.17 | async-start | bytes 147456 | tf_op jit(solution)/shard_map/while/body/eval_jaxpr/reduce_scatter | solution.py:323
  1746.0 85.3 %reduce-scatter.12.cloned.1.call-start = ((), (), s32[]{:S(2)}) async-start(), calls=%async_computation.16 | async-start | bytes 2359296 | tf_op jit(solution)/shard_map/while/body/eval_jaxpr/reduce_scatter | solution.py:322
  1760.4 146.4 %reduce-scatter.18.cloned.1.call-start = ((), (), s32[]{:S(2)}) async-start(), calls=%async_computation.19 | async-start | bytes 5242880 | tf_op jit(solution)/shard_map/while/body/eval_jaxpr/reduce_scatter | solution.py:307
  1785.9 200.5 %reduce-scatter.20.cloned.1.call-start = ((), (), s32[]{:S(2)}) async-start(), calls=%async_computation.20 | async-start | bytes 5242880 | tf_op jit(solution)/shard_map/while/body/eval_jaxpr/reduce_scatter | solution.py:243
  1796.6 265.4 %reduce-scatter.10.cloned.1.call-start = ((), (), s32[]{:S(2)}) async-start(), calls=%async_computation.14 | async-start | bytes 9437184 | tf_op jit(solution)/shard_map/while/body/eval_jaxpr/reduce_scatter | solution.py:321
  1807.8 328.8 %reduce-scatter.16.cloned.1.call-start = ((), (), s32[]{:S(2)}) async-start(), calls=%async_computation.18 | async-start | bytes 9437184 | tf_op jit(solution)/shard_map/while/body/eval_jaxpr/reduce_scatter | solution.py:324
  1819.3 392.1 %reduce-scatter.8.cloned.1.call-start = ((), (), s32[]{:S(2)}) async-start(), calls=%async_computation.13 | async-start | bytes 9437184 | tf_op jit(solution)/shard_map/while/body/eval_jaxpr/reduce_scatter | solution.py:320
  1828.8 157.5 %copy-start.90 = (f32[256]{0:T(256)S(1)}, f32[256]{0:T(256)}, u32[]{:S(2)}) copy-start(f32[256]{0:T(256)} %get-tuple-element.2317) | copy-start | bytes 3076 | tf_op jit(solution)/shard_map/while
  1829.6 160.8 %copy-start.98 = (f32[16]{0:T(128)}, f32[16]{0:T(128)S(1)}, u32[]{:S(2)}) copy-start(f32[16]{0:T(128)S(1)} %fusion.355) | copy-start | bytes 196 | tf_op jit(solution)/shard_map/while
  1830.2 160.2 %copy-start.100 = (f32[16]{0:T(128)}, f32[16]{0:T(128)S(1)}, u32[]{:S(2)}) copy-start(f32[16]{0:T(128)S(1)} %get-tuple-element.2587) | copy-start | bytes 196 | tf_op jit(solution)/shard_map/while
  1830.3 160.2 %copy-start.102 = (f32[16]{0:T(128)}, f32[16]{0:T(128)S(1)}, u32[]{:S(2)}) copy-start(f32[16]{0:T(128)S(1)} %get-tuple-element.2588) | copy-start | bytes 196 | tf_op jit(solution)/shard_map/while
  1830.3 160.2 %copy-start.86 = (f32[1024]{0:T(1024)}, f32[1024]{0:T(1024)S(1)}, u32[]{:S(2)}) copy-start(f32[1024]{0:T(1024)S(1)} %select_add_fusion.23) | copy-start | bytes 12292 | tf_op jit(solution)/shard_map/while
  1830.3 160.1 %copy-start.84 = (f32[1024]{0:T(1024)}, f32[1024]{0:T(1024)S(1)}, u32[]{:S(2)}) copy-start(f32[1024]{0:T(1024)S(1)} %select_add_fusion.25) | copy-start | bytes 12292 | tf_op jit(solution)/shard_map/while
  1830.4 160.1 %copy-start.64 = (f32[4,1024]{1,0:T(4,128)}, f32[4,1024]{1,0:T(4,128)S(1)}, u32[]{:S(2)}) copy-start(f32[4,1024]{1,0:T(4,128)S(1)} %maximum_add_fusion.4) | copy-start | bytes 49156 | tf_op jit(solution)/shard_map/while
  1831.2 159.3 %copy-start.69 = (f32[256,16]{0,1:T(8,128)}, f32[256,16]{0,1:T(8,128)S(1)}, u32[]{:S(2)}) copy-start(f32[256,16]{0,1:T(8,128)S(1)} %select_add_fusion.21) | copy-start | bytes 49156 | tf_op jit(solution)/shard_map/while
  1831.2 159.3 %copy-start.95 = (f32[256]{0:T(256)}, f32[256]{0:T(256)S(1)}, u32[]{:S(2)}) copy-start(f32[256]{0:T(256)S(1)} %select_add_fusion.24) | copy-start | bytes 3076 | tf_op jit(solution)/shard_map/while
  1831.2 159.3 %copy-start.88 = (f32[4,256]{1,0:T(4,128)}, f32[4,256]{1,0:T(4,128)S(1)}, u32[]{:S(2)}) copy-start(f32[4,256]{1,0:T(4,128)S(1)} %maximum_add_fusion.5) | copy-start | bytes 12292 | tf_op jit(solution)/shard_map/while
  1832.3 158.2 %copy-start.40 = (f32[256,256]{1,0:T(8,128)}, f32[256,256]{1,0:T(8,128)S(1)}, u32[]{:S(2)}) copy-start(f32[256,256]{1,0:T(8,128)S(1)} %select_add_fusion.20) | copy-start | bytes 786436 | tf_op jit(solution)/shard_map/while
  1832.3 229.6 %copy-start.27 = (f32[256,1024]{1,0:T(8,128)S(1)}, f32[256,1024]{1,0:T(8,128)}, u32[]{:S(2)}) copy-start(f32[256,1024]{1,0:T(8,128)} %get-tuple-element.2531) | copy-start | bytes 3145732 | tf_op jit(solution)/shard_map/while
  1909.1 154.4 %copy-start.72 = (f32[2048]{0:T(1024)}, f32[2048]{0:T(1024)S(1)}, u32[]{:S(2)}) copy-start(f32[2048]{0:T(1024)S(1)} %select_add_fusion.26) | copy-start | bytes 24580 | tf_op jit(solution)/shard_map/while
  1990.5 220.8 %copy-start.25 = (f32[256,1024]{1,0:T(8,128)S(1)}, f32[256,1024]{1,0:T(8,128)}, u32[]{:S(2)}) copy-start(f32[256,1024]{1,0:T(8,128)} %get-tuple-element.2530) | copy-start | bytes 3145732 | tf_op jit(solution)/shard_map/while
  2063.5 149.4 %copy-start.28 = (f32[256,1024]{1,0:T(8,128)}, f32[256,1024]{1,0:T(8,128)S(1)}, u32[]{:S(2)}) copy-start(f32[256,1024]{1,0:T(8,128)S(1)} %select_add_fusion.19) | copy-start | bytes 3145732 | tf_op jit(solution)/shard_map/while
  (278 other events, 5127.4 us)
Sparse Core Ops, SparseCore 0:
  12.8 26.1 all-gather.14
  40.6 80.7 all-gather.10
  123.3 35.2 all-gather.12
  160.3 36.7 all-gather.16
  198.5 80.7 all-gather.20
  281.1 35.9 all-gather.18
  610.5 35.4 all-reduce.17
  649.3 33.3 reduce-scatter.13
  685.9 41.2 reduce-scatter.11
  729.4 76.7 reduce-scatter.17
  808.5 77.2 reduce-scatter.19
  889.5 71.7 reduce-scatter.9
  964.8 71.2 reduce-scatter.15
  1039.4 71.2 reduce-scatter.7
  1116.1 23.4 all-gather.14
  1141.0 80.7 all-gather.10
  1223.6 35.2 all-gather.12
  1260.6 36.7 all-gather.16
  1298.9 80.7 all-gather.20
  1381.5 35.9 all-gather.18
  1711.1 35.5 all-reduce.17
  1750.0 33.1 reduce-scatter.13
  1786.5 41.2 reduce-scatter.11
  1830.0 76.7 reduce-scatter.17
  1909.1 77.2 reduce-scatter.19
  1990.1 71.8 reduce-scatter.9
  2065.2 71.2 reduce-scatter.15
  2140.0 71.2 reduce-scatter.7
where the time goes:
time: 2300 us; the launch traced here: 2290 us
  waiting for transfers between devices  1020 us (44%)
  matrix products  472 us (21%)
  local copies, waits for them, and re-layouts  315 us (14%)
  other arithmetic  303 us (13%)
  blocking collectives  130 us (6%)
  loops' own time  29.4 us (1%)
    all_gather x2, waiting for transfers between devices, micro_step(): inputs = lax.all_gather(input_rows, 'tp', axis=0, tiled=True)  165 us
    reduce_scatter x2, waiting for transfers between devices, micro_step(): lax.psum_scatter(matmul(branch, out_w).astype(jnp.bfloat16), 'tp', scatte...  155 us
    reduce_scatter x2, waiting for transfers between devices, micro_step(): lax.psum_scatter((summed + leader * contract_last(rows_of(low_state), sta...  149 us
    reduce_scatter x2, waiting for transfers between devices, micro_step(): lax.psum_scatter(big_grads[4], 'fsdp', scatter_dimension=1, tiled=True)  146 us
    reduce_scatter x2, waiting for transfers between devices, micro_step(): lax.psum_scatter(big_grads[0], 'fsdp', scatter_dimension=0, tiled=True)  144 us
    reduce_scatter x2, waiting for transfers between devices, micro_step(): lax.psum_scatter(big_grads[1], 'fsdp', scatter_dimension=0, tiled=True)  143 us
    dot_general x26, matrix products, contract_last(): lax.dot_general(former, latter, (((1,), (1,)), ((), ())), preferred_eleme...  88.6 us
    dot_general x18, matrix products, matmul(): return jnp.dot(former, latter, preferred_element_type=jnp.float32)  85.2 us
  transfers between devices with their start and end apart: 28, of which 18 were waited for; matrix products, arithmetic and copies ran while one was open for 23% of the time, Pallas kernels for 0%

commit v1 on v0

v1 whole, which is shorter than its diff:
```python
from functools import partial

import jax
import jax.numpy as jnp
from jax import lax
from jax.experimental import pallas as pl
from jax.experimental.pallas import tpu as pltpu
from jax.sharding import PartitionSpec as P

HEAD_DIM = 64
STATE = 128
CONV = 4
GROUP = 256
HALF = GROUP // 2
BLOCK = 256
PER_BLOCK = BLOCK // HEAD_DIM
HALO = 8
INNER = 4096
EPSILON = 1e-05
PRECISE = lax.Precision.HIGHEST
F32 = jnp.float32
BF16 = jnp.bfloat16


def mm(former, latter, precision=None):
    return jnp.dot(former, latter, preferred_element_type=F32, precision=precision)


def mm_nt(former, latter):
    return lax.dot_general(
        former, latter, (((1,), (1,)), ((), ())), preferred_element_type=F32
    )


def mm_tn(former, latter):
    return lax.dot_general(
        former, latter, (((0,), (0,)), ((), ())), preferred_element_type=F32
    )


def iota(shape, axis):
    return lax.broadcasted_iota(jnp.int32, shape, axis)


def expand(columns):
    rows = columns.shape[0]
    lane = iota((rows, 128), 1)
    parts = []
    for pair in range(PER_BLOCK // 2):
        former = jnp.broadcast_to(columns[:, 2 * pair : 2 * pair + 1], (rows, 128))
        latter = jnp.broadcast_to(columns[:, 2 * pair + 1 : 2 * pair + 2], (rows, 128))
        parts.append(jnp.where(lane < HEAD_DIM, former, latter))
    return jnp.concatenate(parts, axis=1)


def lane_mask(head):
    lane = iota((1, BLOCK), 1)
    return ((lane // HEAD_DIM) == head).astype(F32).astype(BF16)


def spread(ref, values, blocks):
    for block in range(blocks):
        shift = (128 - PER_BLOCK * block) % 128
        ref[block] = pltpu.roll(values, shift, 1) if shift else values


def token_quantities(step_in, cums, cols, decay_rate):
    step = jnp.maximum(step_in, 0.0) + jnp.log1p(jnp.exp(-jnp.abs(step_in)))
    final = cums[GROUP - 1 : GROUP, :]
    entering = jnp.exp(cums) * cols[:, 6:7]
    fading = jnp.exp(final - cums) * cols[:, 7:8]
    retain = jnp.exp(final) * cols[0:1, 8:9]
    return step, entering, fading, retain


def shifted_values(buf, cols):
    moved = [buf[HALO : HALO + GROUP, :]]
    for offset in range(1, CONV):
        before = buf[HALO - offset : HALO - offset + GROUP, :]
        moved.append(jnp.where(cols[:, offset - 1 : offset] > 0.0, before, 0.0))
    return moved


def conv_of(moved, taps, bias):
    total = bias + taps[0:1, :] * moved[0]
    for offset in range(1, CONV):
        total = total + taps[offset : offset + 1, :] * moved[offset]
    return total


def forward_kernel(
    in_ref, gate_w, value_w, state_w, step_w, taps_ref, bias_ref, staps_ref, sbias_ref,
    step_bias_ref, rate_ref, skip_ref, cols_ref, seg_ref,
    gate_out, value_out, mixed_out, bc_out, sraw_out, stepin_out, cums_out, held_out,
    vbuf, sbuf, gram_s, b_t, c_s, step_s, ent_s, fade_s, cums_s, cums_t, keep_s, hidden,
):
    g, j = pl.program_id(0), pl.program_id(1)
    blocks = pl.num_programs(1)
    nblocks = hidden.shape[0]
    rows = in_ref[...]
    cols = cols_ref[...]

    @pl.when(j == 0)
    def _():
        sbuf[0:HALO, :] = sbuf[GROUP : GROUP + HALO, :]
        raw = mm(rows, state_w[...])
        sbuf[HALO : HALO + GROUP, :] = raw
        sraw_out[...] = raw
        conv = conv_of(shifted_values(sbuf, cols), staps_ref[...], sbias_ref[...])
        bc = (conv * jax.nn.sigmoid(conv)).astype(BF16)
        bc_out[...] = bc
        b_low, c_low = bc[:, :STATE], bc[:, STATE:]
        b_t[...] = jnp.transpose(b_low.astype(F32)).astype(BF16)
        c_s[...] = c_low
        step_in = mm(rows, step_w[...]) + step_bias_ref[...]
        stepin_out[...] = step_in
        step = jnp.maximum(step_in, 0.0) + jnp.log1p(jnp.exp(-jnp.abs(step_in)))
        at_row, at_col = iota((GROUP, GROUP), 0), iota((GROUP, GROUP), 1)
        lower = (at_row >= at_col).astype(F32)
        cums = mm(lower, step * rate_ref[...], PRECISE)
        cums_out[...] = cums
        step, entering, fading, retain = token_quantities(step_in, cums, cols, rate_ref[...])
        spread(step_s, step, nblocks)
        spread(ent_s, entering, nblocks)
        spread(fade_s, fading, nblocks)
        spread(cums_s, cums, nblocks)
        spread(keep_s, jnp.broadcast_to(retain, (8, 128)), nblocks)
        cums_t[...] = jnp.transpose(cums)
        within = (at_row >= at_col) & (cols[:, 9:10] == seg_ref[...])
        gram_s[...] = jnp.where(within, mm_nt(c_low, b_low), 0.0)

    at = pl.multiple_of(j * BLOCK, BLOCK)
    gate_out[...] = mm(rows, gate_w[:, pl.ds(at, BLOCK)]).astype(BF16)
    value = mm(rows, value_w[:, pl.ds(at, BLOCK)])
    value_out[...] = value
    mine = vbuf.at[j]
    mine[0:HALO, :] = mine[GROUP : GROUP + HALO, :]
    mine[HALO : HALO + GROUP, :] = value
    conv = conv_of(shifted_values(mine, cols), taps_ref[...], bias_ref[...])
    x_low = (conv * jax.nn.sigmoid(conv)).astype(BF16)
    x_float = x_low.astype(F32)
    scaled_float = expand(step_s[j]) * x_float
    scaled = scaled_float.astype(BF16)

    @pl.when(g == 0)
    def _():
        hidden[j] = jnp.zeros((STATE, BLOCK), F32)

    state = hidden[j]
    held_out[0] = state
    total = expand(ent_s[j]) * mm(c_s[...], state.astype(BF16))
    weighted = (expand(fade_s[j]) * scaled.astype(F32)).astype(BF16)
    hidden[j] = expand(keep_s[j])[0:1, :] * state + mm(b_t[...], weighted)
    cums_here = cums_s[j]
    top = jnp.zeros((HALF, BLOCK), F32)
    bottom = jnp.zeros((HALF, BLOCK), F32)
    for i in range(PER_BLOCK):
        to = cums_here[:, i : i + 1]
        frm = cums_t[pl.ds(j * PER_BLOCK + i, 1), :]
        only = scaled * lane_mask(i)
        decay = jnp.exp(jnp.minimum(to[:HALF] - frm[:, :HALF], 0.0))
        top = top + mm((gram_s[:HALF, :HALF] * decay).astype(BF16), only[:HALF])
        decay = jnp.exp(jnp.minimum(to[HALF:] - frm, 0.0))
        bottom = bottom + mm((gram_s[HALF:, :] * decay).astype(BF16), only)
    mixed_out[...] = total + jnp.concatenate([top, bottom], axis=0) + skip_ref[...] * x_float


def branch_kernel(cot_ref, out_w, gate_ref, mixed_ref, gain_ref, grad_out, stats_out):
    grad = mm_nt(cot_ref[...], out_w[...])
    grad_out[...] = grad.astype(BF16)
    gate = gate_ref[...].astype(F32)
    gated = mixed_ref[...] * (gate * jax.nn.sigmoid(gate))
    squares = jnp.sum(gated * gated, axis=1, keepdims=True)
    inner = jnp.sum(grad * gain_ref[...] * gated, axis=1, keepdims=True)
    lane = iota((GROUP, 128), 1)
    stats_out[...] = jnp.where(lane == 0, squares, jnp.where(lane == 1, inner, 0.0))


def backward_kernel(
    gate_ref, value_ref, before_ref, mixed_ref, grad_ref, bc_ref, stepin_ref, cums_ref, held_ref,
    stats_ref, gate_w, value_w, out_w, step_w, taps_ref, bias_ref, rate_ref, skip_ref, gain_ref,
    cols_ref, seg_ref,
    branch_out, lowgate_out, lowvalue_out, lowstep_out, gbc_out, made_out, gin_out, small_out, sums_out,
    vbuf, gcbuf, gram_s, dgram, b_s, c_t, step_s, ent_s, fade_s, cums_s, cums_t, keep_s, grad_state,
    made, gin, gb_s, gc_s, u_s, v_s, fin_s, small_s, sums_s,
):
    g, j = pl.program_id(0), pl.program_id(1)
    groups, blocks = pl.num_programs(0), pl.num_programs(1)
    nblocks = grad_state.shape[0]
    cols = cols_ref[...]
    at_row, at_col = iota((GROUP, GROUP), 0), iota((GROUP, GROUP), 1)

    @pl.when((g == 0) & (j == 0))
    def _():
        grad_state[...] = jnp.zeros(grad_state.shape, F32)
        small_s[...] = jnp.zeros(small_s.shape, F32)
        sums_s[...] = jnp.zeros(sums_s.shape, F32)
        gcbuf[...] = jnp.zeros(gcbuf.shape, F32)

    @pl.when(j == 0)
    def _():
        bc = bc_ref[...]
        b_low, c_low = bc[:, :STATE], bc[:, STATE:]
        b_s[...] = b_low
        c_t[...] = jnp.transpose(c_low.astype(F32)).astype(BF16)
        cums = cums_ref[...]
        step, entering, fading, retain = token_quantities(stepin_ref[...], cums, cols, rate_ref[...])
        spread(step_s, step, nblocks)
        spread(ent_s, entering, nblocks)
        spread(fade_s, fading, nblocks)
        spread(cums_s, cums, nblocks)
        spread(keep_s, jnp.broadcast_to(retain, (8, 128)), nblocks)
        cums_t[...] = jnp.transpose(cums)
        within = (at_row <= at_col) & (cols[:, 9:10] == seg_ref[...])
        gram_s[...] = jnp.where(within, mm_nt(b_low, c_low), 0.0)
        dgram[...] = jnp.zeros(dgram.shape, F32)
        made[...] = jnp.zeros(made.shape, F32)
        gin[...] = jnp.zeros(gin.shape, F32)
        gb_s[...] = jnp.zeros(gb_s.shape, F32)
        gc_s[...] = jnp.zeros(gc_s.shape, F32)
        u_s[...] = jnp.zeros(u_s.shape, F32)
        v_s[...] = jnp.zeros(v_s.shape, F32)
        fin_s[...] = jnp.zeros(fin_s.shape, F32)

    at = pl.multiple_of(j * BLOCK, BLOCK)
    gate, mixed, grad = gate_ref[...].astype(F32), mixed_ref[...], grad_ref[...].astype(F32)
    gain, skip, taps = gain_ref[...], skip_ref[...], taps_ref[...]
    scale = stats_ref[:, 0:1]
    inner = stats_ref[:, 1:2]
    sig = jax.nn.sigmoid(gate)
    act = gate * sig
    gated = mixed * act
    scaled_gated = gated * scale
    branch = (scaled_gated * gain).astype(BF16)
    branch_out[...] = branch
    made[...] += mm(branch, out_w[pl.ds(at, BLOCK), :])
    grad_gain = jnp.sum(grad * scaled_gated, axis=0, keepdims=True)
    grad_gated = scale * (grad * gain) - gated * inner
    grad_mixed = grad_gated * act
    low_gate = (grad_gated * mixed * (sig * (1.0 + gate * (1.0 - sig)))).astype(BF16)
    lowgate_out[...] = low_gate

    vbuf[0:HALO, :] = before_ref[...]
    vbuf[HALO : HALO + GROUP, :] = value_ref[...]
    moved = shifted_values(vbuf, cols)
    conv = conv_of(moved, taps, bias_ref[...])
    sig = jax.nn.sigmoid(conv)
    x_float = (conv * sig).astype(BF16).astype(F32)
    slope = sig * (1.0 + conv * (1.0 - sig))
    step_wide = expand(step_s[j])
    fade_wide = expand(fade_s[j])
    scaled = (step_wide * x_float).astype(BF16)
    scaled_float = scaled.astype(F32)
    grad_skip = jnp.sum(grad_mixed * x_float, axis=0, keepdims=True)
    grad_scan = grad_mixed.astype(BF16)
    grad_scan_float = grad_scan.astype(F32)
    scanned = mixed - skip * x_float

    own = grad_state[j]
    state = held_ref[0]
    own_low, state_low = own.astype(BF16), state.astype(BF16)
    grad_weighted = mm(b_s[...], own_low)
    weighted = (fade_wide * scaled_float).astype(BF16)
    entered = (expand(ent_s[j]) * grad_scan_float).astype(BF16)
    gb_s[...] += mm_nt(weighted, own_low)
    gc_s[...] += mm_nt(entered, state_low)
    keep_wide = expand(keep_s[j])[0:1, :]
    kept = keep_wide * jnp.sum(state * own, axis=0, keepdims=True)
    grad_state[j] = keep_wide * own + mm(c_t[...], entered)

    cums_here = cums_s[j]
    top = jnp.zeros((HALF, BLOCK), F32)
    bottom = jnp.zeros((HALF, BLOCK), F32)
    dtop = dgram[:HALF, :]
    dbottom = dgram[HALF:, HALF:]
    for i in range(PER_BLOCK):
        frm = cums_here[:, i : i + 1]
        to = cums_t[pl.ds(j * PER_BLOCK + i, 1), :]
        mask = lane_mask(i)
        only_grad = grad_scan * mask
        only = scaled * mask
        decay = jnp.exp(jnp.minimum(to - frm[:HALF], 0.0))
        top = top + mm((gram_s[:HALF, :] * decay).astype(BF16), only_grad)
        dtop = dtop + mm_nt(only[:HALF], grad_scan) * decay
        decay = jnp.exp(jnp.minimum(to[:, HALF:] - frm[HALF:], 0.0))
        bottom = bottom + mm((gram_s[HALF:, HALF:] * decay).astype(BF16), only_grad[HALF:])
        dbottom = dbottom + mm_nt(only[HALF:], grad_scan[HALF:]) * decay
    dgram[:HALF, :] = dtop
    dgram[HALF:, HALF:] = dbottom
    faded = fade_wide * grad_weighted
    through = jnp.concatenate([top, bottom], axis=0) + faded
    column = scaled_float * through
    final = kept + jnp.sum(scaled_float * faded, axis=0, keepdims=True)
    place = (iota((BLOCK, 128), 1) == j * PER_BLOCK + iota((BLOCK, 128), 0) // HEAD_DIM).astype(F32)
    u_s[...] += mm(grad_scan_float * scanned - column, place, PRECISE)
    v_s[...] += mm(column, place, PRECISE)
    fin_s[...] += mm(jnp.broadcast_to(final, (8, BLOCK)), place, PRECISE)

    grad_conv = (step_wide * through + skip * grad_mixed) * slope
    after = gcbuf.at[j]
    after[GROUP : GROUP + HALO, :] = after[0:HALO, :]
    after[0:GROUP, :] = grad_conv
    grad_value = taps[0:1, :] * grad_conv
    for offset in range(1, CONV):
        up = jnp.where(cols[:, 2 + offset : 3 + offset] > 0.0, after[offset : offset + GROUP, :], 0.0)
        grad_value = grad_value + taps[offset : offset + 1, :] * up
    low_value = grad_value.astype(BF16)
    lowvalue_out[...] = low_value
    gin[...] += mm_nt(low_gate, gate_w[:, pl.ds(at, BLOCK)]) + mm_nt(low_value, value_w[:, pl.ds(at, BLOCK)])
    lines = [grad_gain, grad_skip]
    lines += [jnp.sum(grad_conv * moved[offset], axis=0, keepdims=True) for offset in range(CONV)]
    lines += [jnp.sum(grad_conv, axis=0, keepdims=True)]
    for at_line, line in enumerate(lines):
        small_s[j, at_line : at_line + 1, :] += line
    small_out[...] = small_s[j]

    @pl.when(j == blocks - 1)
    def _():
        bc = bc_ref[...]
        dg = jnp.where(gram_s[...] == gram_s[...], dgram[...], 0.0)
        within = (at_row <= at_col) & (cols[:, 9:10] == seg_ref[...])
        dg = jnp.where(within, dg, 0.0)
        grad_b = gb_s[...] + mm(dg.astype(BF16), bc[:, STATE:])
        grad_c = gc_s[...] + mm(jnp.transpose(dg).astype(BF16), bc[:, :STATE])
        gbc_out[:, :STATE] = grad_b.astype(BF16)
        gbc_out[:, STATE:] = grad_c.astype(BF16)
        last = iota((GROUP, 128), 0) == GROUP - 1
        grad_cums = u_s[...] + jnp.where(last, fin_s[0:1, :], 0.0)
        upper = (at_row <= at_col).astype(F32)
        grad_a = mm(upper, grad_cums, PRECISE)
        step_in = stepin_ref[...]
        step = jnp.maximum(step_in, 0.0) + jnp.log1p(jnp.exp(-jnp.abs(step_in)))
        sig_in = jax.nn.sigmoid(step_in)
        ratio = jnp.where(step_in < -15.0, 1.0, sig_in / step)
        grad_step = v_s[...] * ratio + grad_a * rate_ref[...] * sig_in
        low_step = grad_step.astype(BF16)
        lowstep_out[...] = low_step
        sums_s[0:1, :] += jnp.sum(grad_step, axis=0, keepdims=True)
        sums_s[1:2, :] += jnp.sum(grad_a * step, axis=0, keepdims=True)
        sums_out[...] = sums_s[...]
        gin_out[...] = (gin[...] + mm_nt(low_step, step_w[...])).astype(BF16)
        made_out[...] = made[...].astype(BF16)


def shape(dims, kind=F32):
    return jax.ShapeDtypeStruct(dims, kind)


def params(limit=60 << 20):
    return pltpu.CompilerParams(
        dimension_semantics=("arbitrary", "arbitrary"), vmem_limit_bytes=limit
    )


def whole(array):
    return pl.BlockSpec(
        array.shape, lambda g, j: (0,) * array.ndim, pipeline_mode=pl.Buffered(1)
    )


def forward_call(inputs, weights, vectors, cols, seg_line):
    gate_w, value_w, state_w, step_w = weights
    taps, bias, staps, sbias, step_bias, rate, skip = vectors
    length, model = inputs.shape
    inner = gate_w.shape[1]
    groups, blocks = length // GROUP, inner // BLOCK
    wide = pl.BlockSpec((GROUP, BLOCK), lambda g, j: (g, j))
    line = lambda rows: pl.BlockSpec((rows, BLOCK), lambda g, j: (0, j))
    rows_of = lambda width: pl.BlockSpec((GROUP, width), lambda g, j: (g, 0))
    return pl.pallas_call(
        forward_kernel,
        grid=(groups, blocks),
        in_specs=[
            rows_of(model), whole(gate_w), whole(value_w), whole(state_w), whole(step_w),
            line(CONV), line(1), whole(staps), whole(sbias), whole(step_bias), whole(rate), line(1),
            rows_of(cols.shape[1]), pl.BlockSpec((1, GROUP), lambda g, j: (0, g)),
        ],
        out_specs=[
            wide, wide, wide, rows_of(2 * STATE), rows_of(2 * STATE), rows_of(128), rows_of(128),
            pl.BlockSpec((1, STATE, BLOCK), lambda g, j: (g, 0, j)),
        ],
        out_shape=[
            shape((length, inner), BF16), shape((length, inner)), shape((length, inner)),
            shape((length, 2 * STATE), BF16), shape((length, 2 * STATE)), shape((length, 128)),
            shape((length, 128)), shape((groups, STATE, inner)),
        ],
        scratch_shapes=[
            pltpu.VMEM((blocks, GROUP + HALO, BLOCK), F32),
            pltpu.VMEM((GROUP + HALO, 2 * STATE), F32),
            pltpu.VMEM((GROUP, GROUP), F32),
            pltpu.VMEM((STATE, GROUP), BF16),
            pltpu.VMEM((GROUP, STATE), BF16),
            pltpu.VMEM((blocks, GROUP, 128), F32),
            pltpu.VMEM((blocks, GROUP, 128), F32),
            pltpu.VMEM((blocks, GROUP, 128), F32),
            pltpu.VMEM((blocks, GROUP, 128), F32),
            pltpu.VMEM((128, GROUP), F32),
            pltpu.VMEM((blocks, 8, 128), F32),
            pltpu.VMEM((blocks, STATE, BLOCK), F32),
        ],
        compiler_params=params(),
        cost_estimate=pl.CostEstimate(
            flops=2 * length * model * (2 * inner + 512), bytes_accessed=40 << 20, transcendentals=0
        ),
        name="ssd_forward",
    )(
        inputs, gate_w, value_w, state_w, step_w, taps, bias, staps, sbias, step_bias, rate, skip,
        cols, seg_line,
    )


def branch_call(cotan, out_w, gate_raw, mixed, gain):
    length, model = cotan.shape
    inner = out_w.shape[0]
    rows_of = lambda width: pl.BlockSpec((GROUP, width), lambda g: (g, 0))
    return pl.pallas_call(
        branch_kernel,
        grid=(length // GROUP,),
        in_specs=[
            rows_of(model),
            pl.BlockSpec(out_w.shape, lambda g: (0, 0), pipeline_mode=pl.Buffered(1)),
            rows_of(inner), rows_of(inner),
            pl.BlockSpec(gain.shape, lambda g: (0, 0)),
        ],
        out_specs=[rows_of(inner), rows_of(128)],
        out_shape=[shape((length, inner), BF16), shape((length, 128))],
        compiler_params=pltpu.CompilerParams(vmem_limit_bytes=60 << 20),
        cost_estimate=pl.CostEstimate(
            flops=2 * length * model * inner, bytes_accessed=24 << 20, transcendentals=0
        ),
        name="branch_gradient",
    )(cotan, out_w, gate_raw, mixed, gain)


def backward_call(saved, grad_branch, stats, weights, vectors, gain, cols, seg_line):
    gate_raw, value_raw, mixed, bc, _, step_in, cums, held = saved
    gate_w, value_w, out_w, step_w = weights
    taps, bias, rate, skip = vectors
    length, inner = gate_raw.shape
    model = out_w.shape[1]
    groups, blocks = length // GROUP, inner // BLOCK
    last = groups - 1
    wide = pl.BlockSpec((GROUP, BLOCK), lambda g, j: (last - g, j))
    line = lambda rows: pl.BlockSpec((rows, BLOCK), lambda g, j: (0, j))
    rows_of = lambda width: pl.BlockSpec((GROUP, width), lambda g, j: (last - g, 0))
    steps = GROUP // HALO
    before = pl.BlockSpec(
        (HALO, BLOCK), lambda g, j: (jnp.maximum((last - g) * steps - 1, 0), j)
    )
    return pl.pallas_call(
        backward_kernel,
        grid=(groups, blocks),
        in_specs=[
            wide, wide, before, wide, wide, rows_of(2 * STATE), rows_of(128), rows_of(128),
            pl.BlockSpec((1, STATE, BLOCK), lambda g, j: (last - g, 0, j)),
            rows_of(128), whole(gate_w), whole(value_w), whole(out_w), whole(step_w),
            line(CONV), line(1), whole(rate), line(1), line(1),
            rows_of(cols.shape[1]), pl.BlockSpec((1, GROUP), lambda g, j: (0, last - g)),
        ],
        out_specs=[
            wide, wide, wide, rows_of(128), rows_of(2 * STATE), rows_of(model), rows_of(model),
            line(8), pl.BlockSpec((8, 128), lambda g, j: (0, 0)),
        ],
        out_shape=[
            shape((length, inner), BF16), shape((length, inner), BF16), shape((length, inner), BF16),
            shape((length, 128), BF16), shape((length, 2 * STATE), BF16),
            shape((length, model), BF16), shape((length, model), BF16),
            shape((8, inner)), shape((8, 128)),
        ],
        scratch_shapes=[
            pltpu.VMEM((GROUP + HALO, BLOCK), F32),
            pltpu.VMEM((blocks, GROUP + HALO, BLOCK), F32),
            pltpu.VMEM((GROUP, GROUP), F32),
            pltpu.VMEM((GROUP, GROUP), F32),
            pltpu.VMEM((GROUP, STATE), BF16),
            pltpu.VMEM((STATE, GROUP), BF16),
            pltpu.VMEM((blocks, GROUP, 128), F32),
            pltpu.VMEM((blocks, GROUP, 128), F32),
            pltpu.VMEM((blocks, GROUP, 128), F32),
            pltpu.VMEM((blocks, GROUP, 128), F32),
            pltpu.VMEM((128, GROUP), F32),
            pltpu.VMEM((blocks, 8, 128), F32),
            pltpu.VMEM((blocks, STATE, BLOCK), F32),
            pltpu.VMEM((GROUP, model), F32),
            pltpu.VMEM((GROUP, model), F32),
            pltpu.VMEM((GROUP, STATE), F32),
            pltpu.VMEM((GROUP, STATE), F32),
            pltpu.VMEM((GROUP, 128), F32),
            pltpu.VMEM((GROUP, 128), F32),
            pltpu.VMEM((8, 128), F32),
            pltpu.VMEM((blocks, 8, BLOCK), F32),
            pltpu.VMEM((8, 128), F32),
        ],
        compiler_params=params(),
        cost_estimate=pl.CostEstimate(
            flops=6 * length * model * inner, bytes_accessed=60 << 20, transcendentals=0
        ),
        name="ssd_backward",
    )(
        gate_raw, value_raw, value_raw, mixed, grad_branch, bc, step_in, cums, held, stats,
        gate_w, value_w, out_w, step_w, taps, bias, rate, skip, gain, cols, seg_line,
    )

MESH = pl.DeviceIdType.MESH


def part_of(ref, at, size, axis):
    if axis == 0:
        return ref.at[pl.ds(pl.multiple_of(at * size, size), size), :]
    if axis == 1:
        return ref.at[:, pl.ds(pl.multiple_of(at * size, size), size)]
    return ref.at[at]


def greet(devices):
    barrier = pltpu.get_barrier_semaphore()
    for device in devices:
        pl.semaphore_signal(barrier, inc=1, device_id=device, device_id_type=MESH)
    pl.semaphore_wait(barrier, len(devices))


def gather_kernel(count, pieces, *refs):
    amount = len(pieces)
    sources, targets = refs[:amount], refs[amount : 2 * amount]
    own_sem, send_sem, recv_sem, pass_sem, took_sem = refs[2 * amount :]
    me, line = lax.axis_index("fsdp"), lax.axis_index("tp")
    chips = count // 2
    partner = me + 1 - 2 * lax.rem(me, 2)
    others = [lax.rem(me + 2 * hop, count) for hop in range(1, chips)]
    greet([(device, line) for device in others + [partner]])

    def remote(source, target, sends, receives, device):
        return pltpu.make_async_remote_copy(
            src_ref=source, dst_ref=target, send_sem=sends, recv_sem=receives,
            device_id=(device, line), device_id_type=MESH,
        )

    def place(which, at):
        size, axis = pieces[which]
        return part_of(targets[which], at, size, axis)

    started = []
    for which in range(amount):
        for hop in range(1, chips):
            copy = remote(
                sources[which], place(which, me), send_sem.at[hop, which],
                recv_sem.at[hop, which], lax.rem(me + 2 * hop, count),
            )
            copy.start()
            started.append(copy)
    for which in range(amount):
        copy = remote(
            sources[which], place(which, me), pass_sem.at[0, which], took_sem.at[0, which], partner
        )
        copy.start()
        started.append(copy)
    own = []
    for which in range(amount):
        copy = pltpu.make_async_copy(sources[which], place(which, me), own_sem.at[which])
        copy.start()
        own.append(copy)
    for which in range(amount):
        for hop in range(1, chips):
            origin = lax.rem(me - 2 * hop + count, count)
            block = place(which, origin)
            remote(
                block, block, send_sem.at[hop, which], recv_sem.at[hop, which], partner
            ).wait_recv()
            copy = remote(
                block, block, pass_sem.at[hop, which], took_sem.at[hop, which], partner
            )
            copy.start()
            started.append(copy)
    for which in range(amount):
        for hop in range(chips):
            block = place(which, lax.rem(partner - 2 * hop + count, count))
            remote(
                block, block, pass_sem.at[hop, which], took_sem.at[hop, which], partner
            ).wait_recv()
    for copy in started:
        copy.wait_send()
    for copy in own:
        copy.wait()


def gather_call(count, blocks, axes):
    pieces, shapes = [], []
    for block, axis in zip(blocks, axes):
        if axis == 2:
            pieces.append((0, 2))
            shapes.append(shape((count,) + block.shape, BF16))
        else:
            pieces.append((block.shape[axis], axis))
            dims = list(block.shape)
            dims[axis] *= count
            shapes.append(shape(tuple(dims), BF16))
    amount = len(blocks)
    sems = lambda: pltpu.SemaphoreType.DMA((count // 2, amount))
    return pl.pallas_call(
        partial(gather_kernel, count, pieces),
        in_specs=[pl.BlockSpec(memory_space=pl.ANY)] * amount,
        out_specs=[pl.BlockSpec(memory_space=pl.ANY)] * amount,
        out_shape=shapes,
        scratch_shapes=[pltpu.SemaphoreType.DMA((amount,)), sems(), sems(), sems(), sems()],
        compiler_params=pltpu.CompilerParams(collective_id=0, has_side_effects=True),
        cost_estimate=pl.CostEstimate(flops=0, bytes_accessed=250 << 20, transcendentals=0),
        name="gather_weights",
    )(*blocks)


def scatter_kernel(count, pieces, *refs):
    amount = len(pieces)
    sources, targets = refs[:amount], refs[amount : 2 * amount]
    scratch = refs[2 * amount :]
    mine, took, came = (scratch[at * amount : (at + 1) * amount] for at in range(3))
    own_sem, pass_sem, took_sem, send_sem, recv_sem = scratch[3 * amount :]
    me, line = lax.axis_index("fsdp"), lax.axis_index("tp")
    chips = count // 2
    partner = me + 1 - 2 * lax.rem(me, 2)
    others = [lax.rem(me + 2 * hop, count) for hop in range(1, chips)]
    greet([(device, line) for device in others + [partner]])

    def remote(source, target, sends, receives, device):
        return pltpu.make_async_remote_copy(
            src_ref=source, dst_ref=target, send_sem=sends, recv_sem=receives,
            device_id=(device, line), device_id_type=MESH,
        )

    def piece(which, at):
        size, axis = pieces[which]
        return part_of(sources[which], at, size, axis)

    order = list(range(1, chips)) + [0]
    handed, own = {}, {}
    for hop in order:
        for which in range(amount):
            copy = remote(
                piece(which, lax.rem(partner + 2 * hop, count)), took[which].at[hop],
                pass_sem.at[hop, which], took_sem.at[hop, which], partner,
            )
            copy.start()
            handed[hop, which] = copy
            copy = pltpu.make_async_copy(
                piece(which, lax.rem(me + 2 * hop, count)), mine[which].at[hop],
                own_sem.at[hop, which],
            )
            copy.start()
            own[hop, which] = copy
    sent = []
    for hop in order:
        for which in range(amount):
            own[hop, which].wait()
            handed[hop, which].wait_recv()
            total = mine[which][hop].astype(F32) + took[which][hop].astype(F32)
            if hop == 0:
                targets[which][...] = total
                continue
            mine[which][hop] = total.astype(BF16)
            copy = remote(
                mine[which].at[hop], came[which].at[hop - 1], send_sem.at[hop, which],
                recv_sem.at[hop, which], lax.rem(me + 2 * hop, count),
            )
            copy.start()
            sent.append(copy)
    for which in range(amount):
        for hop in range(1, chips):
            block = came[which].at[hop - 1]
            remote(
                block, block, send_sem.at[hop, which], recv_sem.at[hop, which], partner
            ).wait_recv()
            targets[which][...] += block[...].astype(F32)
    for copy in list(handed.values()) + sent:
        copy.wait_send()


def scatter_call(count, arrays, axes):
    pieces, shapes = [], []
    for array, axis in zip(arrays, axes):
        if axis == 2:
            pieces.append((0, 2))
            shapes.append(array.shape[1:])
        else:
            dims = list(array.shape)
            dims[axis] //= count
            pieces.append((dims[axis], axis))
            shapes.append(tuple(dims))
    amount, chips = len(arrays), count // 2
    sems = lambda: pltpu.SemaphoreType.DMA((chips, amount))
    return pl.pallas_call(
        partial(scatter_kernel, count, pieces),
        in_specs=[pl.BlockSpec(memory_space=pl.ANY)] * amount,
        out_specs=[pl.BlockSpec(memory_space=pltpu.VMEM)] * amount,
        out_shape=[shape(dims) for dims in shapes],
        scratch_shapes=[pltpu.VMEM((chips,) + dims, BF16) for dims in shapes]
        + [pltpu.VMEM((chips,) + dims, BF16) for dims in shapes]
        + [pltpu.VMEM((chips - 1,) + dims, BF16) for dims in shapes]
        + [sems(), sems(), sems(), sems(), sems()],
        compiler_params=pltpu.CompilerParams(
            collective_id=1, has_side_effects=True, vmem_limit_bytes=48 << 20
        ),
        cost_estimate=pl.CostEstimate(flops=0, bytes_accessed=250 << 20, transcendentals=0),
        name="scatter_gradients",
    )(*arrays)


def weight_kernel(micro, *refs):
    outs = refs[-4:]
    rows, lows = refs[:micro], refs[micro : 5 * micro]
    for which in range(4):
        total = mm_tn(rows[0][...], lows[which][...])
        for at in range(1, micro):
            total = total + mm_tn(rows[at][...], lows[4 * at + which][...])
        outs[which][...] = total.astype(BF16)


def weight_call(inputs, lows):
    micro, (length, model) = len(inputs), inputs[0].shape
    full = lambda array: pl.BlockSpec(array.shape, lambda g: (0, 0), pipeline_mode=pl.Buffered(1))
    flat = [array for low in lows for array in low]
    widths = [array.shape[1] for array in lows[0]]
    return pl.pallas_call(
        partial(weight_kernel, micro),
        grid=(model // BLOCK,),
        in_specs=[pl.BlockSpec((length, BLOCK), lambda g: (0, g))] * micro
        + [full(array) for array in flat],
        out_specs=[pl.BlockSpec((BLOCK, width), lambda g: (g, 0)) for width in widths],
        out_shape=[shape((model, width), BF16) for width in widths],
        compiler_params=pltpu.CompilerParams(vmem_limit_bytes=50 << 20),
        cost_estimate=pl.CostEstimate(
            flops=2 * micro * length * model * sum(widths), bytes_accessed=40 << 20, transcendentals=0
        ),
        name="weight_gradients",
    )(*inputs, *flat)


def outer_kernel(micro, *refs):
    total = mm_tn(refs[0][...], refs[micro][...])
    for at in range(1, micro):
        total = total + mm_tn(refs[at][...], refs[micro + at][...])
    refs[-1][...] = total.astype(BF16)


def outer_call(branches, cotans):
    micro, (length, inner) = len(branches), branches[0].shape
    model = cotans[0].shape[1]
    full = lambda array: pl.BlockSpec(array.shape, lambda g: (0, 0), pipeline_mode=pl.Buffered(1))
    return pl.pallas_call(
        partial(outer_kernel, micro),
        grid=(inner // BLOCK,),
        in_specs=[pl.BlockSpec((length, BLOCK), lambda g: (0, g))] * micro
        + [full(array) for array in cotans],
        out_specs=pl.BlockSpec((BLOCK, model), lambda g: (g, 0)),
        out_shape=shape((inner, model), BF16),
        compiler_params=pltpu.CompilerParams(vmem_limit_bytes=50 << 20),
        cost_estimate=pl.CostEstimate(
            flops=2 * micro * length * model * inner, bytes_accessed=30 << 20, transcendentals=0
        ),
        name="out_gradients",
    )(*branches, *cotans)


def shift_down(values, offset):
    return jnp.pad(values, ((offset, 0), (0, 0)))[: values.shape[0]]


def shift_up(values, offset):
    return jnp.pad(values, ((0, offset), (0, 0)))[offset:]


def document_columns(seg_row):
    length = seg_row.shape[0]
    previous = jnp.concatenate([jnp.full((1,), -1, seg_row.dtype), seg_row[GROUP - 1 : -1 : GROUP]])
    last = seg_row[GROUP - 1 :: GROUP]
    columns = []
    for offset in range(1, CONV):
        columns.append(jnp.pad(seg_row, (offset, 0), constant_values=-1)[:length] == seg_row)
    for offset in range(1, CONV):
        columns.append(jnp.pad(seg_row, (0, offset), constant_values=-1)[offset:] == seg_row)
    columns.append(seg_row == jnp.repeat(previous, GROUP))
    columns.append(seg_row == jnp.repeat(last, GROUP))
    columns.append(jnp.repeat(last == previous, GROUP))
    columns.append(seg_row)
    columns = [column.astype(F32) for column in columns]
    return jnp.stack(columns + [columns[0]] * (16 - len(columns)), axis=1)


def state_gradient(grad_bc, state_raw, taps, bias, cols):
    moved = [state_raw]
    for offset in range(1, CONV):
        moved.append(shift_down(state_raw, offset) * cols[:, offset - 1 : offset])
    conv = bias
    for offset in range(CONV):
        conv = conv + taps[offset][None, :] * moved[offset]
    sig = jax.nn.sigmoid(conv)
    grad_conv = grad_bc * (sig * (1.0 + conv * (1.0 - sig)))
    grad_raw = taps[0][None, :] * grad_conv
    for offset in range(1, CONV):
        grad_raw = grad_raw + taps[offset][None, :] * (
            shift_up(grad_conv, offset) * cols[:, 2 + offset : 3 + offset]
        )
    grad_taps = jnp.stack([jnp.sum(grad_conv * each, axis=0) for each in moved])
    return grad_raw.astype(BF16), grad_taps, jnp.sum(grad_conv, axis=0)


def local(
    hidden_in, segment_ids, cotangent, norm_gain, proj_gate, proj_value, proj_state, proj_step,
    conv_value, conv_value_bias, conv_state, conv_state_bias, step_bias, decay_log, skip_gain,
    gate_gain, proj_out,
):
    micro = hidden_in.shape[0]
    heads = step_bias.shape[0]
    rows_here = hidden_in.shape[2]
    tp_size = lax.axis_size("tp")
    me = lax.axis_index("tp")
    decay_rate = -jnp.exp(decay_log)
    pad_heads = lambda values: jnp.pad(values, (0, 128 - heads))[None, :]
    rate = pad_heads(decay_rate)
    step_bias_line = pad_heads(step_bias)
    skip = jnp.repeat(skip_gain, HEAD_DIM)[None, :]
    gain = gate_gain[None, :]
    taps, bias = conv_value, conv_value_bias[None, :]
    staps, sbias = conv_state, conv_state_bias[None, :]

    rows_float = hidden_in[:, 0].astype(F32)
    inv_root = lax.rsqrt(jnp.mean(rows_float * rows_float, axis=-1, keepdims=True) + EPSILON)
    input_rows = (rows_float * inv_root * norm_gain).astype(BF16)

    def gather_tp(values, *after):
        values = lax.optimization_barrier((values,) + after)[0]
        return lax.all_gather(values, "tp", axis=0, tiled=True)

    def scatter_tp(values, *after):
        values = lax.optimization_barrier((values,) + after)[0]
        return lax.psum_scatter(values, "tp", scatter_dimension=0, tiled=True)

    inputs = [gather_tp(input_rows[0])]
    fsdp_size = lax.axis_size("fsdp")
    model = hidden_in.shape[3]
    aligned = proj_out.shape[1] % 128 == 0
    axes = (0, 0, 0, 0, 1 if aligned else 2)
    step_block = jnp.pad(proj_step, ((0, 0), (0, 128 - heads)))
    gate_w, value_w, state_w, step_w, out_w = gather_call(
        fsdp_size, (proj_gate, proj_value, proj_state, step_block, proj_out), axes
    )
    if not aligned:
        out_w = jnp.transpose(out_w, (1, 0, 2)).reshape(-1, model)
    cotans = [gather_tp(cotangent[0, 0], inputs[0], step_w)]
    lows, block_rows, gin_rows, smalls = [], [], [], []
    token = cotans[0]
    for at in range(micro):
        seg_row = segment_ids[at, 0]
        cols = document_columns(seg_row)
        seg_line = seg_row.astype(F32)[None, :]
        saved = forward_call(
            inputs[at], (gate_w, value_w, state_w, step_w),
            (taps, bias, staps, sbias, step_bias_line, rate, skip), cols, seg_line,
        )
        grad_branch, partial_stats = branch_call(cotans[at], out_w, saved[0], saved[2], gain)
        sums = lax.psum(partial_stats[:, :2].T, "tp")
        scale = lax.rsqrt(sums[0] / INNER + EPSILON)
        pair = jnp.stack([scale, scale**3 * (sums[1] / INNER)], axis=1)
        stats = jnp.pad(pair, ((0, 0), (0, 126)))
        if at + 1 < micro:
            inputs.append(gather_tp(input_rows[at + 1], token))
            token = inputs[-1]
        branch, low_gate, low_value, low_step, grad_bc, made, gin, small, step_sums = backward_call(
            saved, grad_branch, stats, (gate_w, value_w, out_w, step_w), (taps, bias, rate, skip),
            gain, cols, seg_line,
        )
        if at + 1 < micro:
            inputs[-1] = lax.optimization_barrier((inputs[-1], gin))[0]
            cotans.append(gather_tp(cotangent[at + 1, 0], token))
            token = cotans[-1]
            produced = scatter_tp(made, token)
            summed = scatter_tp(gin, produced)
        else:
            summed = scatter_tp(gin, token)
            produced = scatter_tp(made, summed)
        token = produced
        block_rows.append((rows_float[at] + produced.astype(F32)).astype(BF16))
        grad_bc = lax.psum(grad_bc, "tp").astype(F32)
        low_state, grad_staps, grad_sbias = state_gradient(grad_bc, saved[4], staps, sbias, cols)
        mine = lax.dynamic_slice_in_dim(low_state, me * rows_here, rows_here, axis=0)
        gin_rows.append(summed.astype(F32) + mm_nt(mine, state_w))
        lows.append((low_gate, low_value, low_state, low_step, branch))
        smalls.append((small, step_sums, grad_staps, grad_sbias))

    grad_out = outer_call([low[4] for low in lows], cotans)
    grad_gate, grad_value, grad_state, grad_step = weight_call(inputs, [low[:4] for low in lows])
    if not aligned:
        grad_out = jnp.transpose(grad_out.reshape(-1, fsdp_size, proj_out.shape[1]), (1, 0, 2))
    grad_gate, grad_value, grad_state, grad_step, grad_out = scatter_call(
        fsdp_size, (grad_gate, grad_value, grad_state, grad_step, grad_out), axes
    )
    grad_step = grad_step[:, :heads]

    grad_inputs = jnp.stack(gin_rows)
    grad_norm_gain = jnp.sum(grad_inputs * rows_float * inv_root, axis=(0, 1))
    grad_normed = grad_inputs * norm_gain
    grad_rows = inv_root * grad_normed - rows_float * inv_root**3 * jnp.mean(
        grad_normed * rows_float, axis=-1, keepdims=True
    )
    grad_hidden = (cotangent[:, 0].astype(F32) + grad_rows).astype(BF16)

    small, step_sums, grad_staps, grad_sbias = (sum(parts) for parts in zip(*smalls))
    small, step_sums, grad_staps, grad_sbias = lax.psum(
        (small, step_sums, grad_staps, grad_sbias), "fsdp"
    )
    gain_total = lax.psum(grad_norm_gain, ("fsdp", "tp"))
    return (
        jnp.stack(block_rows)[:, None],
        grad_hidden[:, None],
        gain_total,
        grad_gate,
        grad_value,
        grad_state,
        grad_step,
        small[2 : 2 + CONV],
        small[2 + CONV],
        grad_staps,
        grad_sbias,
        step_sums[0, :heads],
        step_sums[1, :heads] * decay_rate,
        jnp.sum(small[1].reshape(heads, HEAD_DIM), axis=1),
        small[0],
        grad_out,
    )


def solution(mesh):
    in_specs = (
        P(None, "fsdp", "tp", None), P(None, "fsdp", None), P(None, "fsdp", "tp", None), P(),
        P("fsdp", "tp"), P("fsdp", "tp"), P("fsdp", None), P("fsdp", "tp"), P(None, "tp"), P("tp"),
        P(), P(), P("tp"), P("tp"), P("tp"), P("tp"), P("tp", "fsdp"),
    )
    out_specs = (
        P(None, "fsdp", "tp", None), P(None, "fsdp", "tp", None), P(), P("fsdp", "tp"),
        P("fsdp", "tp"), P("fsdp", None), P("fsdp", "tp"), P(None, "tp"), P("tp"), P(), P(),
        P("tp"), P("tp"), P("tp"), P("tp"), P("tp", "fsdp"),
    )
    return jax.shard_map(local, mesh=mesh, in_specs=in_specs, out_specs=out_specs, check_vma=False)
```

time: 2300 us -> 963 us (0.42)
  waiting for transfers between devices: 1020 us -> 276 us
  matrix products: 472 us -> 5.64 us
  Pallas kernels: 0 us -> 459 us
  local copies, waits for them, and re-layouts: 315 us -> 22.6 us
  other arithmetic: 303 us -> 31 us
  loops' own time: 29.4 us -> 0 us
    reduce_scatter x14 -> x4, waiting for transfers between devices: 737 us -> 75.9 us  [scatter_tp(): return lax.psum_scatter(values, 'tp', scatter_dimension=0, tiled=True)]
    pallas_call x0 -> x10, Pallas kernels: none -> 459 us  [the longest x2 142 us: backward_call(): pl.pallas_call(backward_kernel, grid=(groups, blocks), in_specs=[wide, wi...]
    dot_general x142 -> x2, matrix products: 453 us -> 5.64 us  [mm_nt(): lax.dot_general(former, latter, (((1,), (1,)), ((), ())), preferred_eleme...]
    all_gather x12 -> x4, waiting for transfers between devices: 279 us -> 163 us  [gather_tp(): return lax.all_gather(values, 'tp', axis=0, tiled=True)]
    reduce_sum x40 -> x5, other arithmetic: 89.6 us -> 9.13 us  [the longest x2 4.37 us: state_gradient(): grad_taps = jnp.stack([jnp.sum(grad_conv * each, axis=0) for each in moved])]
    reshape x16 -> x0, local copies, waits for them, and re-layouts: 75.2 us -> none  [the longest x4 32.6 us: micro_step(): scanned = scanned.reshape(LENGTH, heads_here, HEAD_DIM)]
    another operation x76 -> x3, other arithmetic: 62.4 us -> 3.53 us  [the longest x1 3.5 us: local(): jnp.stack(block_rows)[:, None]]
    another operation x84 -> x8, local copies, waits for them, and re-layouts: 58.9 us -> 4.04 us  [the longest x4 2.25 us: document_columns(): return jnp.stack(columns + [columns[0]] * (16 - len(columns)), axis=1)]
  transfers between devices with their start and end apart: 28 -> 9, of which waited for: 18 -> 4; matrix products, arithmetic and copies ran while one was open for 23% -> 5% of each run, Pallas kernels for 0% -> 48%
where the time goes in v1:
time: 963 us; the launch traced here: 956 us
  Pallas kernels  459 us (48%)
  waiting for transfers between devices  276 us (29%)
  blocking collectives  146 us (15%)
  other arithmetic  31 us (3%)
  local copies, waits for them, and re-layouts  22.6 us (2%)
  between operations  14.6 us (2%)
    all_gather x4, waiting for transfers between devices, gather_tp(): return lax.all_gather(values, 'tp', axis=0, tiled=True)  163 us
    pallas_call x2, Pallas kernels, backward_call(): pl.pallas_call(backward_kernel, grid=(groups, blocks), in_specs=[wide, wi...  142 us
    pallas_call x2, Pallas kernels, forward_call(): pl.pallas_call(forward_kernel, grid=(groups, blocks), in_specs=[rows_of(m...  84.8 us
    pallas_call x1, Pallas kernels, gather_call(): pl.pallas_call(partial(gather_kernel, count, pieces), in_specs=[pl.BlockS...  84.4 us
    pallas_call x1, Pallas kernels, scatter_call(): pl.pallas_call(partial(scatter_kernel, count, pieces), in_specs=[pl.Block...  83.8 us
    psum x2, blocking collectives, local(): sums = lax.psum(partial_stats[:, :2].T, 'tp')  79.6 us
    reduce_scatter x4, waiting for transfers between devices, scatter_tp(): return lax.psum_scatter(values, 'tp', scatter_dimension=0, tiled=True)  75.9 us
    psum x1, blocking collectives, local(): gain_total = lax.psum(grad_norm_gain, ('fsdp', 'tp'))  37.2 us
  transfers between devices with their start and end apart: 9, of which 4 were waited for; matrix products, arithmetic and copies ran while one was open for 5% of the time, Pallas kernels for 48%

profile of v1, /device:TPU:0, one launch (start us, length us, event | category | flops | bytes accessed | tf_op | source)
XLA Modules:
  0.0 955.5 jit_solution(12762548936191312020)
XLA Ops:
  7.2 2.2 fusion.5
  9.5 0.6 multiply_multiply_fusion.4
  10.0 0.5 fusion.7
  10.6 1.5 slice_bitcast_fusion.3
  12.3 0.6 pad.102.refs_3_
  12.9 84.4 %gather_weights.1 = (bf16[2048,1024]{1,0:T(8,128)(2,1)}, bf16[2048,1024]{1,0:T(8,128)(2,1)}, bf16[2048,256]{1,0:T(8,128)(2,1)}, bf16[2048,128]{1,0:T(8,128)(2,1)}, bf16[1024,2048]{1,0:T(8,128)(2,1)}) custom-call(bf16[256,1024]{1,0:T(8,128)(2,1)} %refs_0_.1, bf16[256,1024]{1,0:T(8,128)(2,1)} %refs_1_.1, bf16[256,256]{1,0:T(8,128)(2,1)} %refs_2_.1, ...), custom_call_target="tpu_custom_call" | custom-call | bytes 262144000 | tf_op jit(solution)/shard_map/gather_weights/pallas_call | solution.py:599
  97.4 1.5 slice_bitcast_fusion.4
  98.9 81.4 %all-gather.7.cloned.1.call-done.cot_ref.refs_2_ = bf16[1024,2048]{1,0:T(8,128)(2,1)} async-done(((bf16[256,2048]{1,0:T(8,128)(2,1)}), bf16[1024,2048]{1,0:T(8,128)(2,1)}) %all-gather.7.cloned.1.call-update) | async-done | bytes 4194320 | tf_op jit(solution)/shard_map/all_gather | solution.py:830
  180.4 81.4 %all-gather.9.cloned.1.call-done.in_ref.refs_1_ = bf16[1024,2048]{1,0:T(8,128)(2,1)} async-done(((bf16[256,2048]{1,0:T(8,128)(2,1)}), bf16[1024,2048]{1,0:T(8,128)(2,1)}) %all-gather.9.cloned.1.call-update) | async-done | bytes 4194320 | tf_op jit(solution)/shard_map/all_gather | solution.py:830
  261.9 0.6 convert_bitcast_fusion
  263.0 0.7 broadcast_in_dim_reshape.3.skip_ref
  264.4 1.0 copy.85.cols_ref
  265.4 0.5 pad_bitcast_fusion.1.step_bias_ref
  266.0 0.5 pad_bitcast_fusion.rate_ref
  266.5 42.7 %ssd_forward.2 = (bf16[1024,1024]{1,0:T(8,128)(2,1)}, f32[1024,1024]{1,0:T(8,128)}, f32[1024,1024]{1,0:T(8,128)}, bf16[1024,256]{1,0:T(8,128)(2,1)}, f32[1024,25...) custom-call(bf16[1024,2048]{1,0:T(8,128)(2,1)} %all-gather.5.cloned.1.call-done.in_ref.refs_0_, ...), custom_call_target="tpu_custom_call" | custom-call | flops 10737418240 | bytes 41943040 | tf_op jit(solution)/shard_map/ssd_forward/pallas_call | solution.py:370
  309.2 10.4 %branch_gradient.2 = (bf16[1024,1024]{1,0:T(8,128)(2,1)}, f32[1024,128]{1,0:T(8,128)}) custom-call(bf16[1024,2048]{1,0:T(8,128)(2,1)} %all-gather.7.cloned.1.call-done.cot_ref.refs_2_, bf16[1024,2048]{1,0:T(8,128)(2,1)} %get-tuple-element.84.out_w, bf16[1024,1024]{1,0:T(8,128)(2,1)} %get-tuple-element.80.gate_ref, f32[1024,1024]{1,0:T(8,128)} %get-tuple-element.82.mixed_ref, ...), custom_call_target="tpu_custom_call" | custom-call | flops 4294967296 | bytes 25165824 | tf_op jit(solution)/shard_map/branch_gradient/pallas_call | solution.py:416
  319.6 1.1 slice_bitcast_fusion.7
  320.7 39.4 %psum.63 = f32[2,1024]{0,1:T(8,128)S(1)} all-reduce(f32[2,1024]{0,1:T(8,128)S(1)} %slice_bitcast_fusion.7), channel_id=1, replica_groups=mesh['fsdp'=8,'tp'=4] {'tp'}, use_global_device_ids=true, to_apply=%region_1.2 | all-reduce | flops 2048 | bytes 16384 | tf_op jit(solution)/shard_map/psum | solution.py:859
  360.1 0.5 fusion.50
  360.9 0.9 pad.111.stats_ref
  361.8 71.0 %ssd_backward.2 = (bf16[1024,1024]{1,0:T(8,128)(2,1)}, bf16[1024,1024]{1,0:T(8,128)(2,1)}, bf16[1024,1024]{1,0:T(8,128)(2,1)}, bf16[1024,128]{1,0:T(8,128)(2,1)}...) custom-call(bf16[1024,1024]{1,0:T(8,128)(2,1)} %get-tuple-element.80, ...), custom_call_target="tpu_custom_call" | custom-call | flops 12884901888 | bytes 62914560 | tf_op jit(solution)/shard_map/ssd_backward/pallas_call | solution.py:450
  433.0 1.0 copy.88.cols_ref
  434.0 42.1 %ssd_forward.3 = (bf16[1024,1024]{1,0:T(8,128)(2,1)}, f32[1024,1024]{1,0:T(8,128)}, f32[1024,1024]{1,0:T(8,128)}, bf16[1024,256]{1,0:T(8,128)(2,1)}, f32[1024,25...) custom-call(bf16[1024,2048]{1,0:T(8,128)(2,1)} %all-gather.9.cloned.1.call-done.in_ref.refs_1_, ...), custom_call_target="tpu_custom_call" | custom-call | flops 10737418240 | bytes 41943040 | tf_op jit(solution)/shard_map/ssd_forward/pallas_call | solution.py:370
  476.1 10.3 %branch_gradient.3 = (bf16[1024,1024]{1,0:T(8,128)(2,1)}, f32[1024,128]{1,0:T(8,128)}) custom-call(bf16[1024,2048]{1,0:T(8,128)(2,1)} %all-gather.11.cloned.1.call-done.cot_ref.refs_3_, bf16[1024,2048]{1,0:T(8,128)(2,1)} %get-tuple-element.84.out_w, bf16[1024,1024]{1,0:T(8,128)(2,1)} %get-tuple-element.97.gate_ref, ...), custom_call_target="tpu_custom_call" | custom-call | flops 4294967296 | bytes 25165824 | tf_op jit(solution)/shard_map/branch_gradient/pallas_call | solution.py:416
  486.4 1.1 slice_bitcast_fusion.6
  487.5 40.2 %psum.64 = f32[2,1024]{0,1:T(8,128)S(1)} all-reduce(f32[2,1024]{0,1:T(8,128)S(1)} %slice_bitcast_fusion.6), channel_id=1, replica_groups=mesh['fsdp'=8,'tp'=4] {'tp'}, use_global_device_ids=true, to_apply=%region_3.4 | all-reduce | flops 2048 | bytes 16384 | tf_op jit(solution)/shard_map/psum | solution.py:859
  527.7 0.5 fusion.46
  528.5 0.8 pad.118.stats_ref
  529.3 70.9 %ssd_backward.3 = (bf16[1024,1024]{1,0:T(8,128)(2,1)}, bf16[1024,1024]{1,0:T(8,128)(2,1)}, bf16[1024,1024]{1,0:T(8,128)(2,1)}, bf16[1024,128]{1,0:T(8,128)(2,1)}...) custom-call(bf16[1024,1024]{1,0:T(8,128)(2,1)} %get-tuple-element.97, ...), custom_call_target="tpu_custom_call" | custom-call | flops 12884901888 | bytes 62914560 | tf_op jit(solution)/shard_map/ssd_backward/pallas_call | solution.py:450
  600.2 0.7 all-reduce.33.cloned.1.call-update
  601.0 0.7 reduce-scatter.11.cloned.1.call-update
  601.7 0.3 reduce-scatter.9.cloned.1.call-start
  602.0 75.8 %reduce-scatter.7.cloned.1.call-done = bf16[256,2048]{1,0:T(8,128)(2,1)} async-done(((bf16[1024,2048]{1,0:T(8,128)(2,1)}), bf16[256,2048]{1,0:T(8,128)(2,1)}) %reduce-scatter.7.cloned.1.call-update) | async-done | bytes 1048592 | tf_op jit(solution)/shard_map/reduce_scatter | solution.py:834
  677.9 4.2 convert_element_type.224
  682.2 0.6 add.251
  682.8 14.6 %out_gradients.1.refs_4_ = bf16[1024,2048]{1,0:T(8,128)(2,1)} custom-call(bf16[1024,1024]{1,0:T(8,128)(2,1)S(1)} %copy-done.2, bf16[1024,1024]{1,0:T(8,128)(2,1)} %get-tuple-element.126.refs_1_, bf16[1024,2048]{1,0:T(8,128)(2,1)} %all-gather.7.cloned.1.call-done.cot_ref.refs_2_, bf16[1024,2048]{1,0:T(8,128)(2,1)} %all-gather.11.cloned.1.call-done.cot_ref.refs_3_), custom_call_target="tpu_custom_call" | custom-call | flops 8589934592 | bytes 31457280 | tf_op jit(solution)/shard_map/out_gradients/pallas_call | solution.py:747
  697.4 35.5 %all-reduce.33.cloned.1.call-done = (bf16[1024,256]{1,0:T(8,128)(2,1)}, bf16[1024,256]{1,0:T(8,128)(2,1)}) async-done(((bf16[1024,256]{1,0:T(8,128)(2,1)}, bf16[1024,256]{1,0:T(8,128)(2,1)}), (bf16[1024,256]{1,0:T(8,128)(2,1)}, bf16[1024,256]{1,0:T(8,128)(2,1)})) %all-reduce.33.cloned.1.call-update) | async-done | bytes 1048592 | tf_op jit(solution)/shard_map/psum | solution.py:881
  732.9 2.6 multiply_reduce_fusion.7
  735.6 1.8 multiply_reduce_fusion.3
  737.4 1.5 fusion.23
  738.9 29.2 %weight_gradients.1 = (bf16[2048,1024]{1,0:T(8,128)(2,1)}, bf16[2048,1024]{1,0:T(8,128)(2,1)}, bf16[2048,256]{1,0:T(8,128)(2,1)S(1)}, bf16[2048,128]{1,0:T(8,128)(2,1)S(1)}) custom-call(bf16[1024,2048]{1,0:T(8,128)(2,1)} %all-gather.5.cloned.1.call-done.in_ref.refs_0_, bf16[1024,2048]{1,0:T(8,128)(2,1)} %all-gather.9.cloned.1.call-done.in_ref.refs_1_, ...), custom_call_target="tpu_custom_call" | custom-call | flops 20401094656 | bytes 41943040 | tf_op jit(solution)/shard_map/weight_gradients/pallas_call | solution.py:721
  768.1 83.8 %scatter_gradients.1 = (f32[256,1024]{1,0:T(8,128)S(1)}, f32[256,1024]{1,0:T(8,128)S(1)}, f32[256,256]{1,0:T(8,128)S(1)}, f32[256,128]{1,0:T(8,128)S(1)}, f32[1024,256]{1,0:T(8,128)S(1)}) custom-call(bf16[2048,1024]{1,0:T(8,128)(2,1)} %get-tuple-element.121.refs_0_, bf16[2048,1024]{1,0:T(8,128)(2,1)} %get-tuple-element.122.refs_1_, ...), custom_call_target="tpu_custom_call" | custom-call | bytes 262144000 | tf_op jit(solution)/shard_map/scatter_gradients/pallas_call | solution.py:689
  851.9 0.6 add.253
  852.4 0.6 maximum_add_fusion
  853.0 29.2 %all-reduce.29 = (f32[8,1024]{1,0:T(8,128)}, f32[4,256]{1,0:T(4,128)}, f32[256]{0:T(256)}, f32[8,128]{1,0:T(8,128)}) all-reduce(f32[8,1024]{1,0:T(8,128)} %add.251, f32[4,256]{1,0:T(4,128)} %maximum_add_fusion, f32[256]{0:T(256)} %add.253, f32[8,128]{1,0:T(8,128)S(1)} %add.254), channel_id=1, replica_groups=mesh['fsdp'=8,'tp'=4] {'fsdp'}, use_global_device_ids=true, to_apply=%region_12.13 | all-reduce | flops 10496 | bytes 83968 | tf_op jit(solution)/shard_map/psum | solution.py:906
  882.3 1.4 slice.234
  883.6 1.5 fusion.81
  885.1 0.7 reshape_squeeze.3
  885.8 1.3 reduce_sum.139
  887.1 0.7 copy.92
  887.8 1.2 slice_bitcast_fusion.8
  889.0 1.2 bitcast_multiply_fusion.4
  890.2 3.4 convolution_add_fusion
  893.6 2.2 convolution_add_fusion.1
  895.9 0.6 copy-done.7
  896.5 1.2 fusion.10
  897.8 37.2 %psum.67 = f32[2048]{0:T(1024)} all-reduce(f32[2048]{0:T(1024)S(1)} %get-tuple-element.200), channel_id=1, replica_groups=mesh['fsdp'=8,'tp'=4] {'fsdp','tp'}, use_global_device_ids=true, to_apply=%region_11.12 | all-reduce | flops 2048 | bytes 16384 | tf_op jit(solution)/shard_map/psum | solution.py:909
  935.0 5.1 fusion.3
  940.1 3.5 fusion.41
  943.6 1.5 maximum_bitcast_fusion
  945.1 1.0 copy.105
  946.1 1.0 copy.106
  947.0 0.7 copy.107
  947.7 1.0 copy.108
  (105 shorter events, 2.7 us)
Async XLA Ops:
  7.2 2.9 copy-start.5
  7.2 2.9 copy-start.13
  7.2 91.7 %all-gather.5.cloned.1.call-start = ((), (), s32[]{:S(2)}) async-start(), calls=%async_computation.4 | async-start | bytes 5242880 | tf_op jit(solution)/shard_map/all_gather | solution.py:830
  10.6 1.5 copy-start.18
  12.1 85.3 %copy-start.9 = (bf16[2,1,256,2048]{3,2,1,0:T(8,128)(2,1)S(1)}, bf16[2,1,256,2048]{3,2,1,0:T(8,128)(2,1)}, u32[]{:S(2)}) copy-start(bf16[2,1,256,2048]{3,2,1,0:T(8,128)(2,1)} %param.19) | copy-start | bytes 6291460
  12.1 168.3 %all-gather.7.cloned.1.call-start = ((), (), s32[]{:S(2)}) async-start(), calls=%async_computation.5 | async-start | bytes 5242880 | tf_op jit(solution)/shard_map/all_gather | solution.py:830
  98.8 163.1 %copy-start.16 = (s32[2,1,1024]{2,1,0:T(1,128)S(1)}, s32[2,1,1024]{2,1,0:T(1,128)}, u32[]{:S(2)}) copy-start(s32[2,1,1024]{2,1,0:T(1,128)} %param.18) | copy-start | bytes 24580
  98.8 164.0 %copy-start.23 = (f32[16]{0:T(128)S(1)}, f32[16]{0:T(128)}, u32[]{:S(2)}) copy-start(f32[16]{0:T(128)} %param.31) | copy-start | bytes 196
  98.8 166.6 %copy-start.24 = (f32[16]{0:T(128)S(1)}, f32[16]{0:T(128)}, u32[]{:S(2)}) copy-start(f32[16]{0:T(128)} %param.29) | copy-start | bytes 196
  98.8 167.1 %copy-start.25 = (f32[16]{0:T(128)S(1)}, f32[16]{0:T(128)}, u32[]{:S(2)}) copy-start(f32[16]{0:T(128)} %param.30) | copy-start | bytes 196
  98.9 162.9 %all-gather.9.cloned.1.call-start = ((), (), s32[]{:S(2)}) async-start(), calls=%async_computation.6 | async-start | bytes 5242880 | tf_op jit(solution)/shard_map/all_gather | solution.py:830
  180.4 252.4 %all-gather.11.cloned.1.call-start = ((), (), s32[]{:S(2)}) async-start(), calls=%async_computation.7 | async-start | bytes 5242880 | tf_op jit(solution)/shard_map/all_gather | solution.py:830
  261.9 338.3 %reduce-scatter.5.cloned.1.call-start = ((), (), s32[]{:S(2)}) async-start(), calls=%async_computation.8 | async-start | bytes 5242880 | tf_op jit(solution)/shard_map/reduce_scatter | solution.py:834
  432.8 245.0 %reduce-scatter.7.cloned.1.call-start = ((), (), s32[]{:S(2)}) async-start(), calls=%async_computation.9 | async-start | bytes 5242880 | tf_op jit(solution)/shard_map/reduce_scatter | solution.py:834
  600.2 132.7 %all-reduce.33.cloned.1.call-start = ((), (), s32[]{:S(2)}) async-start(), calls=%async_computation.12 | async-start | bytes 2097152 | tf_op jit(solution)/shard_map/psum | solution.py:881
  601.0 292.7 %reduce-scatter.11.cloned.1.call-start = ((), (), s32[]{:S(2)}) async-start(), calls=%async_computation.11 | async-start | bytes 5242880 | tf_op jit(solution)/shard_map/reduce_scatter | solution.py:834
  601.7 338.4 %reduce-scatter.9.cloned.1.call-start = ((), (), s32[]{:S(2)}) async-start(), calls=%async_computation.10 | async-start | bytes 5242880 | tf_op jit(solution)/shard_map/reduce_scatter | solution.py:834
  677.8 4.3 copy-start.22
  677.8 4.3 copy-start.20
  677.8 4.3 copy-start.21
  677.9 4.3 copy-start.14
  677.9 4.3 copy-start.15
  677.9 4.9 copy-start.2
  682.8 50.1 %copy-start.10 = (f32[1024,256]{1,0:T(8,128)S(1)}, f32[1024,256]{1,0:T(8,128)}, u32[]{:S(2)}) copy-start(f32[1024,256]{1,0:T(8,128)} %get-tuple-element.112) | copy-start | bytes 3145732
  682.8 50.1 %copy-start.19 = (f32[256]{0:T(256)S(1)}, f32[256]{0:T(256)}, u32[]{:S(2)}) copy-start(f32[256]{0:T(256)} %param.28) | copy-start | bytes 3076
  697.4 38.1 %copy-start.11 = (f32[1024,256]{1,0:T(8,128)S(1)}, f32[1024,256]{1,0:T(8,128)}, u32[]{:S(2)}) copy-start(f32[1024,256]{1,0:T(8,128)} %get-tuple-element.114) | copy-start | bytes 3145732
  732.9 2.6 copy-start.12
  737.3 1.5 copy-start.3
  737.4 1.5 copy-start.4
  738.8 29.2 %copy-start = (bf16[1024,256]{1,0:T(8,128)(2,1)}, bf16[1024,256]{1,0:T(8,128)(2,1)S(1)}, u32[]{:S(2)}) copy-start(bf16[1024,256]{1,0:T(8,128)(2,1)S(1)} %get-tuple-element.243.refs_4_) | copy-start | bytes 1572868
  738.8 29.2 %copy-start.1 = (bf16[1024,256]{1,0:T(8,128)(2,1)}, bf16[1024,256]{1,0:T(8,128)(2,1)S(1)}, u32[]{:S(2)}) copy-start(bf16[1024,256]{1,0:T(8,128)(2,1)S(1)} %get-tuple-element.244.refs_8_) | copy-start | bytes 1572868
  893.6 2.3 copy-start.6
  893.6 2.9 copy-start.7
  895.8 1.9 copy-start.8
  896.5 38.5 %copy-start.17 = (f32[2,256]{1,0:T(2,128)S(1)}, f32[2,256]{1,0:T(2,128)}, u32[]{:S(2)}) copy-start(f32[2,256]{1,0:T(2,128)} %get-tuple-element.261) | copy-start | bytes 6148
Sparse Core Ops, SparseCore 0:
  12.2 83.4 all-gather.4
  99.0 81.2 all-gather.6
  182.5 79.2 all-gather.8
  263.8 92.8 all-gather.10
  432.9 89.4 reduce-scatter.4
  600.3 77.4 reduce-scatter.6
  680.2 52.6 all-reduce.32
  735.3 76.1 reduce-scatter.10
  813.8 77.2 reduce-scatter.8

commit v2 on v1

--- a/solution.py
+++ b/solution.py
@@ -18,6 +18,8 @@
 INNER = 4096
 EPSILON = 1e-05
 PRECISE = lax.Precision.HIGHEST
+FORWARD_INS, FORWARD_OUTS = 16, 9
+BACKWARD_INS, BACKWARD_OUTS = 20, 8
 F32 = jnp.float32
 BF16 = jnp.bfloat16
 
@@ -88,11 +90,280 @@
     return total
 
 
+MESH = pl.DeviceIdType.MESH
+
+
+def part_of(ref, at, size, axis):
+    if axis == 0:
+        return ref.at[pl.ds(pl.multiple_of(at * size, size), size), :]
+    if axis == 1:
+        return ref.at[:, pl.ds(pl.multiple_of(at * size, size), size)]
+    return ref.at[at]
+
+
+def greet(devices):
+    barrier = pltpu.get_barrier_semaphore()
+    for device in devices:
+        pl.semaphore_signal(barrier, inc=1, device_id=device, device_id_type=MESH)
+    pl.semaphore_wait(barrier, len(devices))
+
+
+def remote_copy(source, target, sends, receives, device):
+    return pltpu.make_async_remote_copy(
+        src_ref=source, dst_ref=target, send_sem=sends, recv_sem=receives,
+        device_id=device, device_id_type=MESH,
+    )
+
+
+class LineScatter:
+    def __init__(self, size, source, own, slots, last, own_sem, send_sem, recv_sem, last_sem):
+        self.size, self.source, self.own, self.slots, self.last = size, source, own, slots, last
+        self.own_sem, self.send_sem, self.recv_sem, self.last_sem = own_sem, send_sem, recv_sem, last_sem
+        self.me, self.column = lax.axis_index("tp"), lax.axis_index("fsdp")
+        self.rows = last.shape[0]
+
+    @staticmethod
+    def scratch(size, rows, width):
+        hops = size - 1
+        return [
+            pltpu.VMEM((2, hops, rows, width), BF16), pltpu.VMEM((2, hops, rows, width), BF16),
+            pltpu.VMEM((rows, width), BF16), pltpu.SemaphoreType.DMA((2, hops)),
+            pltpu.SemaphoreType.DMA((2, hops)), pltpu.SemaphoreType.DMA((2, hops)),
+            pltpu.SemaphoreType.DMA((1,)),
+        ]
+
+    def place(self, flow):
+        return self.me if flow == 0 else self.size - 1 - self.me
+
+    def local(self, flow, hop):
+        block = self.size - 1 - hop + self.place(flow)
+        if flow:
+            block = self.size - 1 - block
+        at = pl.multiple_of(block * self.rows, self.rows)
+        return pltpu.make_async_copy(
+            self.source.at[pl.ds(at, self.rows), :], self.own.at[flow, hop], self.own_sem.at[flow, hop]
+        )
+
+    def final(self):
+        at = pl.multiple_of(self.me * self.rows, self.rows)
+        return pltpu.make_async_copy(
+            self.source.at[pl.ds(at, self.rows), :], self.last, self.last_sem.at[0]
+        )
+
+    def sending(self, flow, hop):
+        neighbour = self.me + 1 if flow == 0 else self.me - 1
+        neighbour = jnp.clip(neighbour, 0, self.size - 1)
+        return remote_copy(
+            self.own.at[flow, hop], self.slots.at[flow, hop], self.send_sem.at[flow, hop],
+            self.recv_sem.at[flow, hop], (self.column, neighbour),
+        )
+
+    def greet(self):
+        barrier = pltpu.get_barrier_semaphore()
+        for flow in range(2):
+            neighbour = self.me + 1 if flow == 0 else self.me - 1
+
+            @pl.when((neighbour >= 0) & (neighbour < self.size))
+            def _():
+                pl.semaphore_signal(
+                    barrier, inc=1, device_id=(self.column, neighbour), device_id_type=MESH
+                )
+
+        inside = (self.me > 0) & (self.me < self.size - 1)
+        pl.semaphore_wait(barrier, 1 + inside.astype(jnp.int32))
+
+    def begin(self):
+        self.final().start()
+        for hop in range(self.size - 1):
+            for flow in range(2):
+
+                @pl.when(self.place(flow) <= hop)
+                def _():
+                    self.local(flow, hop).start()
+
+    def hop(self, hop):
+        for flow in range(2):
+            place = self.place(flow)
+
+            @pl.when(place <= hop)
+            def _():
+                self.local(flow, hop).wait()
+                if hop > 0:
+
+                    @pl.when(place >= 1)
+                    def _():
+                        self.sending(flow, hop - 1).wait_recv()
+                        total = self.own[flow, hop].astype(F32) + self.slots[flow, hop - 1].astype(F32)
+                        self.own[flow, hop] = total.astype(BF16)
+
+                self.sending(flow, hop).start()
+
+    def end(self, out):
+        hops = self.size - 1
+        self.final().wait()
+        out[...] = self.last[...].astype(F32)
+        for flow in range(2):
+
+            @pl.when(self.place(flow) >= 1)
+            def _():
+                self.sending(flow, hops - 1).wait_recv()
+                out[...] += self.slots[flow, hops - 1].astype(F32)
+
+        for hop in range(hops):
+            for flow in range(2):
+
+                @pl.when(self.place(flow) <= hop)
+                def _():
+                    self.sending(flow, hop).wait_send()
+
+
+class LineGather:
+    def __init__(self, size, source, target, own_sem, send_sem, recv_sem):
+        self.size, self.source, self.target = size, source, target
+        self.own_sem, self.send_sem, self.recv_sem = own_sem, send_sem, recv_sem
+        self.me, self.column = lax.axis_index("tp"), lax.axis_index("fsdp")
+        self.rows = source.shape[0]
+
+    @staticmethod
+    def scratch(size):
+        return [
+            pltpu.SemaphoreType.DMA((1,)), pltpu.SemaphoreType.DMA((2, size - 1)),
+            pltpu.SemaphoreType.DMA((2, size - 1)),
+        ]
+
+    def place(self, flow):
+        return self.me if flow == 0 else self.size - 1 - self.me
+
+    def block(self, at):
+        at = pl.multiple_of(jnp.clip(at, 0, self.size - 1) * self.rows, self.rows)
+        return self.target.at[pl.ds(at, self.rows), :]
+
+    def sending(self, flow, hop):
+        neighbour = self.me + 1 if flow == 0 else self.me - 1
+        neighbour = jnp.clip(neighbour, 0, self.size - 1)
+        block = self.block(self.me - hop if flow == 0 else self.me + hop)
+        return remote_copy(
+            self.source if hop == 0 else block, block, self.send_sem.at[flow, hop],
+            self.recv_sem.at[flow, hop], (self.column, neighbour),
+        )
+
+    def local(self):
+        return pltpu.make_async_copy(self.source, self.block(self.me), self.own_sem.at[0])
+
+    def begin(self):
+        self.local().start()
+        self.hop(0)
+
+    def hop(self, hop):
+        for flow in range(2):
+            place = self.place(flow)
+            if hop > 0:
+
+                @pl.when(place >= hop)
+                def _():
+                    self.sending(flow, hop - 1).wait_recv()
+
+            if hop < self.size - 1:
+
+                @pl.when((place >= hop) & (place < self.size - 1))
+                def _():
+                    self.sending(flow, hop).start()
+
+    def end(self):
+        self.hop(self.size - 1)
+        self.local().wait()
+        for hop in range(self.size - 1):
+            for flow in range(2):
+                place = self.place(flow)
+
+                @pl.when((place >= hop) & (place < self.size - 1))
+                def _():
+                    self.sending(flow, hop).wait_send()
+
+
+def run_line(step, steps, scatter, gather, out):
+    size = (scatter or gather).size
+    actions = [[] for _ in range(size + 1)]
+    if scatter:
+        first = 1 if gather else 0
+        actions[0] += [scatter.greet, scatter.begin]
+        for hop in range(size - 1):
+            actions[first + hop].append(partial(scatter.hop, hop))
+        actions[first + size - 1].append(partial(scatter.end, out))
+    if gather:
+        if not scatter:
+            actions[0].append(partial(LineScatter.greet, gather))
+        actions[0].append(gather.begin)
+        for hop in range(1, size - 1):
+            actions[hop].insert(0, partial(gather.hop, hop))
+        actions[size - 1].insert(0, gather.end)
+    for at, todo in zip(steps, actions):
+        if todo:
+
+            @pl.when(step == at)
+            def _():
+                for action in todo:
+                    action()
+
+
+class Hosted:
+    def __init__(self, size, scatter=None, gather=None):
+        self.size, self.scatter, self.gather = size, scatter, gather
+
+    def operands(self):
+        return [each for each in (self.scatter, self.gather) if each is not None]
+
+    def in_specs(self):
+        return [pl.BlockSpec(memory_space=pl.ANY)] * len(self.operands())
+
+    def outs(self):
+        shapes, specs = [], []
+        if self.scatter is not None:
+            rows, width = self.scatter.shape[0] // self.size, self.scatter.shape[1]
+            shapes.append(shape((rows, width)))
+            specs.append(pl.BlockSpec((rows, width), lambda g, j: (0, 0)))
+        if self.gather is not None:
+            rows, width = self.gather.shape
+            shapes.append(shape((rows * self.size, width), BF16))
+            specs.append(pl.BlockSpec(memory_space=pl.ANY))
+        return specs, shapes
+
+    def scratch(self):
+        needed = []
+        if self.scatter is not None:
+            rows, width = self.scatter.shape[0] // self.size, self.scatter.shape[1]
+            needed += LineScatter.scratch(self.size, rows, width)
+        if self.gather is not None:
+            needed += LineGather.scratch(self.size)
+        return needed
+
+    def wrap(self, body, ins, outs, pace):
+        has_scatter, has_gather = self.scatter is not None, self.gather is not None
+        hosts = has_scatter + has_gather
+        size, spare = self.size, len(self.scratch())
+        if not hosts:
+            return body
+
+        def kernel(*refs):
+            sources, targets = refs[ins : ins + hosts], refs[ins + hosts + outs : ins + outs + 2 * hosts]
+            tail = refs[len(refs) - spare :]
+            body(
+                *refs[:ins], *refs[ins + hosts : ins + hosts + outs],
+                *refs[ins + outs + 2 * hosts : len(refs) - spare],
+            )
+            scatter = LineScatter(size, sources[0], *tail[:7]) if has_scatter else None
+            gather = LineGather(size, sources[-1], targets[-1], *tail[-3:]) if has_gather else None
+            step = pl.program_id(0) * pl.num_programs(1) + pl.program_id(1)
+            run_line(step, pace, scatter, gather, targets[0])
+
+        return kernel
+
+
 def forward_kernel(
     in_ref, gate_w, value_w, state_w, step_w, taps_ref, bias_ref, staps_ref, sbias_ref,
-    step_bias_ref, rate_ref, skip_ref, cols_ref, seg_ref,
-    gate_out, value_out, mixed_out, bc_out, sraw_out, stepin_out, cums_out, held_out,
-    vbuf, sbuf, gram_s, b_t, c_s, step_s, ent_s, fade_s, cums_s, cums_t, keep_s, hidden,
+    step_bias_ref, rate_ref, skip_ref, cols_ref, seg_ref, out_w, gain_ref,
+    gate_out, value_out, mixed_out, bc_out, sraw_out, stepin_out, cums_out, held_out, made_out,
+    vbuf, sbuf, gram_s, b_t, c_s, step_s, ent_s, fade_s, cums_s, cums_t, keep_s, hidden, made,
 ):
     g, j = pl.program_id(0), pl.program_id(1)
     blocks = pl.num_programs(1)
@@ -130,7 +401,8 @@
         gram_s[...] = jnp.where(within, mm_nt(c_low, b_low), 0.0)
 
     at = pl.multiple_of(j * BLOCK, BLOCK)
-    gate_out[...] = mm(rows, gate_w[:, pl.ds(at, BLOCK)]).astype(BF16)
+    gate = mm(rows, gate_w[:, pl.ds(at, BLOCK)])
+    gate_out[...] = gate.astype(BF16)
     value = mm(rows, value_w[:, pl.ds(at, BLOCK)])
     value_out[...] = value
     mine = vbuf.at[j]
@@ -147,8 +419,9 @@
         hidden[j] = jnp.zeros((STATE, BLOCK), F32)
 
     state = hidden[j]
-    held_out[0] = state
-    total = expand(ent_s[j]) * mm(c_s[...], state.astype(BF16))
+    state_low = state.astype(BF16)
+    held_out[0] = state_low
+    total = expand(ent_s[j]) * mm(c_s[...], state_low)
     weighted = (expand(fade_s[j]) * scaled.astype(F32)).astype(BF16)
     hidden[j] = expand(keep_s[j])[0:1, :] * state + mm(b_t[...], weighted)
     cums_here = cums_s[j]
@@ -162,10 +435,29 @@
         top = top + mm((gram_s[:HALF, :HALF] * decay).astype(BF16), only[:HALF])
         decay = jnp.exp(jnp.minimum(to[HALF:] - frm, 0.0))
         bottom = bottom + mm((gram_s[HALF:, :] * decay).astype(BF16), only)
-    mixed_out[...] = total + jnp.concatenate([top, bottom], axis=0) + skip_ref[...] * x_float
-
-
-def branch_kernel(cot_ref, out_w, gate_ref, mixed_ref, gain_ref, grad_out, stats_out):
+    mixed = total + jnp.concatenate([top, bottom], axis=0) + skip_ref[...] * x_float
+    mixed_out[...] = mixed
+    scaled_gate = (mixed * (gate * jax.nn.sigmoid(gate)) * gain_ref[...]).astype(BF16)
+
+    @pl.when(j == 0)
+    def _():
+        made[...] = mm(scaled_gate, out_w[pl.ds(at, BLOCK), :])
+
+    @pl.when(j > 0)
+    def _():
+        made[...] += mm(scaled_gate, out_w[pl.ds(at, BLOCK), :])
+
+    @pl.when(j == blocks - 1)
+    def _():
+        made_out[...] = made[...].astype(BF16)
+
+
+def branch_kernel(
+    tp_size, total_inner, cot_ref, out_w, gate_ref, mixed_ref, gain_ref,
+    grad_out, stats_out, sums_s, slots, turn_s, send_sem, recv_sem,
+):
+    step, groups = pl.program_id(0), pl.num_programs(0)
+    me, column = lax.axis_index("tp"), lax.axis_index("fsdp")
     grad = mm_nt(cot_ref[...], out_w[...])
     grad_out[...] = grad.astype(BF16)
     gate = gate_ref[...].astype(F32)
@@ -173,16 +465,42 @@
     squares = jnp.sum(gated * gated, axis=1, keepdims=True)
     inner = jnp.sum(grad * gain_ref[...] * gated, axis=1, keepdims=True)
     lane = iota((GROUP, 128), 1)
-    stats_out[...] = jnp.where(lane == 0, squares, jnp.where(lane == 1, inner, 0.0))
+    both = jnp.where(lane == 0, squares, jnp.where(lane == 1, inner, 0.0))
+    sums_s[step] = jnp.transpose(both)[:8]
+
+    @pl.when(step == groups - 1)
+    def _():
+        greet([(column, lax.rem(me + hop, tp_size)) for hop in range(1, tp_size)])
+        slots[me] = sums_s[...]
+        copies = [
+            remote_copy(
+                sums_s, slots.at[me], send_sem.at[hop - 1], recv_sem.at[hop - 1],
+                (column, lax.rem(me + hop, tp_size)),
+            )
+            for hop in range(1, tp_size)
+        ]
+        for copy in copies:
+            copy.start()
+        for copy in copies:
+            copy.wait()
+        total = slots[0]
+        for at in range(1, tp_size):
+            total = total + slots[at]
+        turn_s[...] = jnp.zeros(turn_s.shape, F32)
+        scale = lax.rsqrt(total[:, 0:1, :] / total_inner + EPSILON)
+        turn_s[:, 0:1, :] = scale
+        turn_s[:, 1:2, :] = scale * scale * scale * (total[:, 1:2, :] / total_inner)
+        for group in range(turn_s.shape[0]):
+            stats_out[group * GROUP : (group + 1) * GROUP, :] = jnp.transpose(turn_s[group])
 
 
 def backward_kernel(
     gate_ref, value_ref, before_ref, mixed_ref, grad_ref, bc_ref, stepin_ref, cums_ref, held_ref,
-    stats_ref, gate_w, value_w, out_w, step_w, taps_ref, bias_ref, rate_ref, skip_ref, gain_ref,
+    stats_ref, gate_w, value_w, step_w, taps_ref, bias_ref, rate_ref, skip_ref, gain_ref,
     cols_ref, seg_ref,
-    branch_out, lowgate_out, lowvalue_out, lowstep_out, gbc_out, made_out, gin_out, small_out, sums_out,
+    branch_out, lowgate_out, lowvalue_out, lowstep_out, gbc_out, gin_out, small_out, sums_out,
     vbuf, gcbuf, gram_s, dgram, b_s, c_t, step_s, ent_s, fade_s, cums_s, cums_t, keep_s, grad_state,
-    made, gin, gb_s, gc_s, u_s, v_s, fin_s, small_s, sums_s,
+    gin, gb_s, gc_s, u_s, v_s, fin_s, small_s, sums_s,
 ):
     g, j = pl.program_id(0), pl.program_id(1)
     groups, blocks = pl.num_programs(0), pl.num_programs(1)
@@ -214,7 +532,6 @@
         within = (at_row <= at_col) & (cols[:, 9:10] == seg_ref[...])
         gram_s[...] = jnp.where(within, mm_nt(b_low, c_low), 0.0)
         dgram[...] = jnp.zeros(dgram.shape, F32)
-        made[...] = jnp.zeros(made.shape, F32)
         gin[...] = jnp.zeros(gin.shape, F32)
         gb_s[...] = jnp.zeros(gb_s.shape, F32)
         gc_s[...] = jnp.zeros(gc_s.shape, F32)
@@ -231,9 +548,7 @@
     act = gate * sig
     gated = mixed * act
     scaled_gated = gated * scale
-    branch = (scaled_gated * gain).astype(BF16)
-    branch_out[...] = branch
-    made[...] += mm(branch, out_w[pl.ds(at, BLOCK), :])
+    branch_out[...] = (scaled_gated * gain).astype(BF16)
     grad_gain = jnp.sum(grad * scaled_gated, axis=0, keepdims=True)
     grad_gated = scale * (grad * gain) - gated * inner
     grad_mixed = grad_gated * act
@@ -257,15 +572,15 @@
     scanned = mixed - skip * x_float
 
     own = grad_state[j]
-    state = held_ref[0]
-    own_low, state_low = own.astype(BF16), state.astype(BF16)
+    state_low = held_ref[0]
+    own_low = own.astype(BF16)
     grad_weighted = mm(b_s[...], own_low)
     weighted = (fade_wide * scaled_float).astype(BF16)
     entered = (expand(ent_s[j]) * grad_scan_float).astype(BF16)
     gb_s[...] += mm_nt(weighted, own_low)
     gc_s[...] += mm_nt(entered, state_low)
     keep_wide = expand(keep_s[j])[0:1, :]
-    kept = keep_wide * jnp.sum(state * own, axis=0, keepdims=True)
+    kept = keep_wide * jnp.sum(state_low.astype(F32) * own, axis=0, keepdims=True)
     grad_state[j] = keep_wide * own + mm(c_t[...], entered)
 
     cums_here = cums_s[j]
@@ -312,14 +627,16 @@
     lines += [jnp.sum(grad_conv, axis=0, keepdims=True)]
     for at_line, line in enumerate(lines):
         small_s[j, at_line : at_line + 1, :] += line
-    small_out[...] = small_s[j]
+
+    @pl.when(g == groups - 1)
+    def _():
+        small_out[:, pl.ds(at, BLOCK)] = small_s[j]
 
     @pl.when(j == blocks - 1)
     def _():
         bc = bc_ref[...]
-        dg = jnp.where(gram_s[...] == gram_s[...], dgram[...], 0.0)
         within = (at_row <= at_col) & (cols[:, 9:10] == seg_ref[...])
-        dg = jnp.where(within, dg, 0.0)
+        dg = jnp.where(within, dgram[...], 0.0)
         grad_b = gb_s[...] + mm(dg.astype(BF16), bc[:, STATE:])
         grad_c = gc_s[...] + mm(jnp.transpose(dg).astype(BF16), bc[:, :STATE])
         gbc_out[:, :STATE] = grad_b.astype(BF16)
@@ -339,16 +656,16 @@
         sums_s[1:2, :] += jnp.sum(grad_a * step, axis=0, keepdims=True)
         sums_out[...] = sums_s[...]
         gin_out[...] = (gin[...] + mm_nt(low_step, step_w[...])).astype(BF16)
-        made_out[...] = made[...].astype(BF16)
 
 
 def shape(dims, kind=F32):
     return jax.ShapeDtypeStruct(dims, kind)
 
 
-def params(limit=60 << 20):
+def params(collective=None):
+    extra = {} if collective is None else dict(collective_id=collective, has_side_effects=True)
     return pltpu.CompilerParams(
-        dimension_semantics=("arbitrary", "arbitrary"), vmem_limit_bytes=limit
+        dimension_semantics=("arbitrary", "arbitrary"), vmem_limit_bytes=60 << 20, **extra
     )
 
 
@@ -358,8 +675,8 @@
     )
 
 
-def forward_call(inputs, weights, vectors, cols, seg_line):
-    gate_w, value_w, state_w, step_w = weights
+def forward_call(inputs, weights, vectors, gain, cols, seg_line, hosted, pace):
+    gate_w, value_w, state_w, step_w, out_w = weights
     taps, bias, staps, sbias, step_bias, rate, skip = vectors
     length, model = inputs.shape
     inner = gate_w.shape[1]
@@ -367,23 +684,25 @@
     wide = pl.BlockSpec((GROUP, BLOCK), lambda g, j: (g, j))
     line = lambda rows: pl.BlockSpec((rows, BLOCK), lambda g, j: (0, j))
     rows_of = lambda width: pl.BlockSpec((GROUP, width), lambda g, j: (g, 0))
+    specs, shapes = hosted.outs()
     return pl.pallas_call(
-        forward_kernel,
+        hosted.wrap(forward_kernel, FORWARD_INS, FORWARD_OUTS, pace),
         grid=(groups, blocks),
         in_specs=[
             rows_of(model), whole(gate_w), whole(value_w), whole(state_w), whole(step_w),
             line(CONV), line(1), whole(staps), whole(sbias), whole(step_bias), whole(rate), line(1),
             rows_of(cols.shape[1]), pl.BlockSpec((1, GROUP), lambda g, j: (0, g)),
-        ],
+            whole(out_w), line(1),
+        ] + hosted.in_specs(),
         out_specs=[
             wide, wide, wide, rows_of(2 * STATE), rows_of(2 * STATE), rows_of(128), rows_of(128),
-            pl.BlockSpec((1, STATE, BLOCK), lambda g, j: (g, 0, j)),
-        ],
+            pl.BlockSpec((1, STATE, BLOCK), lambda g, j: (g, 0, j)), rows_of(model),
+        ] + specs,
         out_shape=[
             shape((length, inner), BF16), shape((length, inner)), shape((length, inner)),
             shape((length, 2 * STATE), BF16), shape((length, 2 * STATE)), shape((length, 128)),
-            shape((length, 128)), shape((groups, STATE, inner)),
-        ],
+            shape((length, 128)), shape((groups, STATE, inner), BF16), shape((length, model), BF16),
+        ] + shapes,
         scratch_shapes=[
             pltpu.VMEM((blocks, GROUP + HALO, BLOCK), F32),
             pltpu.VMEM((GROUP + HALO, 2 * STATE), F32),
@@ -397,47 +716,58 @@
             pltpu.VMEM((128, GROUP), F32),
             pltpu.VMEM((blocks, 8, 128), F32),
             pltpu.VMEM((blocks, STATE, BLOCK), F32),
-        ],
-        compiler_params=params(),
+            pltpu.VMEM((GROUP, model), F32),
+        ] + hosted.scratch(),
+        compiler_params=params(2 if hosted.operands() else None),
         cost_estimate=pl.CostEstimate(
-            flops=2 * length * model * (2 * inner + 512), bytes_accessed=40 << 20, transcendentals=0
+            flops=2 * length * model * (3 * inner + 512), bytes_accessed=40 << 20, transcendentals=0
         ),
         name="ssd_forward",
     )(
         inputs, gate_w, value_w, state_w, step_w, taps, bias, staps, sbias, step_bias, rate, skip,
-        cols, seg_line,
-    )
-
-
-def branch_call(cotan, out_w, gate_raw, mixed, gain):
+        cols, seg_line, out_w, gain, *hosted.operands(),
+    )
+
+
+def branch_call(cotan, out_w, gate_raw, mixed, gain, tp_size):
     length, model = cotan.shape
     inner = out_w.shape[0]
-    rows_of = lambda width: pl.BlockSpec((GROUP, width), lambda g: (g, 0))
+    groups = length // GROUP
+    rows_of = lambda width: pl.BlockSpec((GROUP, width), lambda i: (i, 0))
+    full = lambda dims, **extra: pl.BlockSpec(dims, lambda i: (0, 0), **extra)
     return pl.pallas_call(
-        branch_kernel,
-        grid=(length // GROUP,),
+        partial(branch_kernel, tp_size, inner * tp_size),
+        grid=(groups,),
         in_specs=[
-            rows_of(model),
-            pl.BlockSpec(out_w.shape, lambda g: (0, 0), pipeline_mode=pl.Buffered(1)),
-            rows_of(inner), rows_of(inner),
-            pl.BlockSpec(gain.shape, lambda g: (0, 0)),
+            rows_of(model), full(out_w.shape, pipeline_mode=pl.Buffered(1)),
+            rows_of(inner), rows_of(inner), full(gain.shape),
         ],
-        out_specs=[rows_of(inner), rows_of(128)],
+        out_specs=[rows_of(inner), full((length, 128))],
         out_shape=[shape((length, inner), BF16), shape((length, 128))],
-        compiler_params=pltpu.CompilerParams(vmem_limit_bytes=60 << 20),
+        scratch_shapes=[
+            pltpu.VMEM((groups, 8, GROUP), F32),
+            pltpu.VMEM((tp_size, groups, 8, GROUP), F32),
+            pltpu.VMEM((groups, 128, GROUP), F32),
+            pltpu.SemaphoreType.DMA((tp_size - 1,)),
+            pltpu.SemaphoreType.DMA((tp_size - 1,)),
+        ],
+        compiler_params=pltpu.CompilerParams(
+            collective_id=3, has_side_effects=True, vmem_limit_bytes=50 << 20
+        ),
         cost_estimate=pl.CostEstimate(
-            flops=2 * length * model * inner, bytes_accessed=24 << 20, transcendentals=0
+            flops=2 * length * model * inner, bytes_accessed=20 << 20, transcendentals=0
         ),
         name="branch_gradient",
     )(cotan, out_w, gate_raw, mixed, gain)
 
 
-def backward_call(saved, grad_branch, stats, weights, vectors, gain, cols, seg_line):
-    gate_raw, value_raw, mixed, bc, _, step_in, cums, held = saved
-    gate_w, value_w, out_w, step_w = weights
+def backward_call(saved, grad_branch, stats, weights, vectors, gain, cols, seg_line, hosted, pace, collective):
+    gate_raw, value_raw, mixed, bc, _, step_in, cums, held, _ = saved
+    gate_w, value_w, step_w = weights
     taps, bias, rate, skip = vectors
     length, inner = gate_raw.shape
-    model = out_w.shape[1]
+    model = gate_w.shape[0]
+    specs, shapes = hosted.outs()
     groups, blocks = length // GROUP, inner // BLOCK
     last = groups - 1
     wide = pl.BlockSpec((GROUP, BLOCK), lambda g, j: (last - g, j))
@@ -448,25 +778,24 @@
         (HALO, BLOCK), lambda g, j: (jnp.maximum((last - g) * steps - 1, 0), j)
     )
     return pl.pallas_call(
-        backward_kernel,
+        hosted.wrap(backward_kernel, BACKWARD_INS, BACKWARD_OUTS, pace),
         grid=(groups, blocks),
         in_specs=[
             wide, wide, before, wide, wide, rows_of(2 * STATE), rows_of(128), rows_of(128),
             pl.BlockSpec((1, STATE, BLOCK), lambda g, j: (last - g, 0, j)),
-            rows_of(128), whole(gate_w), whole(value_w), whole(out_w), whole(step_w),
+            rows_of(128), whole(gate_w), whole(value_w), whole(step_w),
             line(CONV), line(1), whole(rate), line(1), line(1),
             rows_of(cols.shape[1]), pl.BlockSpec((1, GROUP), lambda g, j: (0, last - g)),
-        ],
+        ] + hosted.in_specs(),
         out_specs=[
-            wide, wide, wide, rows_of(128), rows_of(2 * STATE), rows_of(model), rows_of(model),
-            line(8), pl.BlockSpec((8, 128), lambda g, j: (0, 0)),
-        ],
+            wide, wide, wide, rows_of(128), rows_of(2 * STATE), rows_of(model),
+            pl.BlockSpec((8, inner), lambda g, j: (0, 0)), pl.BlockSpec((8, 128), lambda g, j: (0, 0)),
+        ] + specs,
         out_shape=[
             shape((length, inner), BF16), shape((length, inner), BF16), shape((length, inner), BF16),
             shape((length, 128), BF16), shape((length, 2 * STATE), BF16),
-            shape((length, model), BF16), shape((length, model), BF16),
-            shape((8, inner)), shape((8, 128)),
-        ],
+            shape((length, model), BF16), shape((8, inner)), shape((8, 128)),
+        ] + shapes,
         scratch_shapes=[
             pltpu.VMEM((GROUP + HALO, BLOCK), F32),
             pltpu.VMEM((blocks, GROUP + HALO, BLOCK), F32),
@@ -482,7 +811,6 @@
             pltpu.VMEM((blocks, 8, 128), F32),
             pltpu.VMEM((blocks, STATE, BLOCK), F32),
             pltpu.VMEM((GROUP, model), F32),
-            pltpu.VMEM((GROUP, model), F32),
             pltpu.VMEM((GROUP, STATE), F32),
             pltpu.VMEM((GROUP, STATE), F32),
             pltpu.VMEM((GROUP, 128), F32),
@@ -490,34 +818,16 @@
             pltpu.VMEM((8, 128), F32),
             pltpu.VMEM((blocks, 8, BLOCK), F32),
             pltpu.VMEM((8, 128), F32),
-        ],
-        compiler_params=params(),
+        ] + hosted.scratch(),
+        compiler_params=params(collective),
         cost_estimate=pl.CostEstimate(
             flops=6 * length * model * inner, bytes_accessed=60 << 20, transcendentals=0
         ),
         name="ssd_backward",
     )(
         gate_raw, value_raw, value_raw, mixed, grad_branch, bc, step_in, cums, held, stats,
-        gate_w, value_w, out_w, step_w, taps, bias, rate, skip, gain, cols, seg_line,
-    )
-
-MESH = pl.DeviceIdType.MESH
-
-
-def part_of(ref, at, size, axis):
-    if axis == 0:
-        return ref.at[pl.ds(pl.multiple_of(at * size, size), size), :]
-    if axis == 1:
-        return ref.at[:, pl.ds(pl.multiple_of(at * size, size), size)]
-    return ref.at[at]
-
-
-def greet(devices):
-    barrier = pltpu.get_barrier_semaphore()
-    for device in devices:
-        pl.semaphore_signal(barrier, inc=1, device_id=device, device_id_type=MESH)
-    pl.semaphore_wait(barrier, len(devices))
-
+        gate_w, value_w, step_w, taps, bias, rate, skip, gain, cols, seg_line, *hosted.operands(),
+    )
 
 def gather_kernel(count, pieces, *refs):
     amount = len(pieces)
@@ -844,46 +1154,58 @@
     )
     if not aligned:
         out_w = jnp.transpose(out_w, (1, 0, 2)).reshape(-1, model)
-    cotans = [gather_tp(cotangent[0, 0], inputs[0], step_w)]
-    lows, block_rows, gin_rows, smalls = [], [], [], []
-    token = cotans[0]
+    inputs.append(gather_tp(input_rows[1], inputs[0], step_w))
+    forward_weights = (gate_w, value_w, state_w, step_w, out_w)
+    vectors = (taps, bias, staps, sbias, step_bias_line, rate, skip)
+    columns = [document_columns(segment_ids[at, 0]) for at in range(micro)]
+    seg_lines = [segment_ids[at, 0].astype(F32)[None, :] for at in range(micro)]
+    quick, slow = [0, 7, 15, 15, 15], [0, 5, 10, 15, 15]
+
+    def forward(at, hosted):
+        return forward_call(
+            inputs[at], forward_weights, vectors, gain, columns[at], seg_lines[at], hosted, quick
+        )
+
+    def backward(at, hosted, collective):
+        grad_branch, stats = branch_call(cotans[at], out_w, saved[at][0], saved[at][2], gain, tp_size)
+        scales.append(stats)
+        return backward_call(
+            saved[at], grad_branch, stats, (gate_w, value_w, step_w), (taps, bias, rate, skip),
+            gain, columns[at], seg_lines[at], hosted, slow, collective,
+        )
+
+    scales, produced, summed = [], [], []
+    saved = [forward(0, Hosted(tp_size))]
+    *kept, made_sum, cotan = forward(1, Hosted(tp_size, saved[0][8], cotangent[0, 0]))
+    saved.append(kept)
+    produced.append(made_sum)
+    cotans = [cotan]
+    *former, made_sum, cotan = backward(0, Hosted(tp_size, saved[1][8], cotangent[1, 0]), 4)
+    produced.append(made_sum)
+    cotans.append(cotan)
+    grad_bcs = [lax.psum(former[4], "tp")]
+    *latter, gin_sum = backward(1, Hosted(tp_size, former[5]), 5)
+    summed.append(gin_sum)
+    grad_bcs.append(lax.psum(lax.optimization_barrier((latter[4], grad_bcs[0]))[0], "tp"))
+    summed.append(scatter_tp(latter[5], grad_bcs[1]).astype(F32))
+    lows = [[each[1], each[2], each[3], each[0]] for each in (former, latter)]
+    smalls = [(each[6], each[7]) for each in (former, latter)]
+    raws = [each[4] for each in saved]
+
+    gin_rows = []
     for at in range(micro):
-        seg_row = segment_ids[at, 0]
-        cols = document_columns(seg_row)
-        seg_line = seg_row.astype(F32)[None, :]
-        saved = forward_call(
-            inputs[at], (gate_w, value_w, state_w, step_w),
-            (taps, bias, staps, sbias, step_bias_line, rate, skip), cols, seg_line,
+        low_state, grad_staps, grad_sbias = state_gradient(
+            grad_bcs[at].astype(F32), raws[at], staps, sbias, columns[at]
         )
-        grad_branch, partial_stats = branch_call(cotans[at], out_w, saved[0], saved[2], gain)
-        sums = lax.psum(partial_stats[:, :2].T, "tp")
-        scale = lax.rsqrt(sums[0] / INNER + EPSILON)
-        pair = jnp.stack([scale, scale**3 * (sums[1] / INNER)], axis=1)
-        stats = jnp.pad(pair, ((0, 0), (0, 126)))
-        if at + 1 < micro:
-            inputs.append(gather_tp(input_rows[at + 1], token))
-            token = inputs[-1]
-        branch, low_gate, low_value, low_step, grad_bc, made, gin, small, step_sums = backward_call(
-            saved, grad_branch, stats, (gate_w, value_w, out_w, step_w), (taps, bias, rate, skip),
-            gain, cols, seg_line,
-        )
-        if at + 1 < micro:
-            inputs[-1] = lax.optimization_barrier((inputs[-1], gin))[0]
-            cotans.append(gather_tp(cotangent[at + 1, 0], token))
-            token = cotans[-1]
-            produced = scatter_tp(made, token)
-            summed = scatter_tp(gin, produced)
-        else:
-            summed = scatter_tp(gin, token)
-            produced = scatter_tp(made, summed)
-        token = produced
-        block_rows.append((rows_float[at] + produced.astype(F32)).astype(BF16))
-        grad_bc = lax.psum(grad_bc, "tp").astype(F32)
-        low_state, grad_staps, grad_sbias = state_gradient(grad_bc, saved[4], staps, sbias, cols)
         mine = lax.dynamic_slice_in_dim(low_state, me * rows_here, rows_here, axis=0)
-        gin_rows.append(summed.astype(F32) + mm_nt(mine, state_w))
-        lows.append((low_gate, low_value, low_state, low_step, branch))
-        smalls.append((small, step_sums, grad_staps, grad_sbias))
+        gin_rows.append(summed[at] + mm_nt(mine, state_w))
+        low_gate, low_value, low_step, branch = lows[at]
+        lows[at] = (low_gate, low_value, low_state, low_step, branch)
+        smalls[at] = smalls[at] + (grad_staps, grad_sbias)
+    block_rows = []
+    for at in range(micro):
+        scale = lax.dynamic_slice_in_dim(scales[at], me * rows_here, rows_here, axis=0)[:, 0:1]
+        block_rows.append((rows_float[at] + produced[at] * scale).astype(BF16))
 
     grad_out = outer_call([low[4] for low in lows], cotans)
     grad_gate, grad_value, grad_state, grad_step = weight_call(inputs, [low[:4] for low in lows])

time: 963 us -> 786 us (0.82)
  waiting for transfers between devices: 276 us -> 62.3 us
  Pallas kernels: 459 us -> 585 us
  blocking collectives: 146 us -> 63.8 us
    all_gather x4 -> x2, waiting for transfers between devices: 163 us -> 20.2 us  [gather_tp(): return lax.all_gather(values, 'tp', axis=0, tiled=True)]
    pallas_call x6, Pallas kernels: 247 us -> 375 us  [the longest x2 183 us: backward_call(): pl.pallas_call(hosted.wrap(backward_kernel, BACKWARD_INS, BACKWARD_OUTS,...]
    psum x2 -> x0, blocking collectives: 79.6 us -> none  [local(): sums = lax.psum(partial_stats[:, :2].T, 'tp')]
    reduce_scatter x4 -> x1, waiting for transfers between devices: 75.9 us -> 0.01 us  [scatter_tp(): return lax.psum_scatter(values, 'tp', scatter_dimension=0, tiled=True)]
    psum x1 -> x2, waiting for transfers between devices: 35.5 us -> 42 us  [the longest x1 42 us: local(): lax.psum(lax.optimization_barrier((latter[4], grad_bcs[0]))[0], 'tp')]
  transfers between devices with their start and end apart: 9 -> 5, of which waited for: 4 -> 2; matrix products, arithmetic and copies ran while one was open for 5% -> 4% of each run, Pallas kernels for 48% -> 46%
where the time goes in v2:
time: 786 us; the launch traced here: 782 us
  Pallas kernels  585 us (74%)
  blocking collectives  63.8 us (8%)
  waiting for transfers between devices  62.3 us (8%)
  other arithmetic  25.4 us (3%)
  local copies, waits for them, and re-layouts  24.9 us (3%)
  between operations  14.5 us (2%)
    pallas_call x2, Pallas kernels, backward_call(): pl.pallas_call(hosted.wrap(backward_kernel, BACKWARD_INS, BACKWARD_OUTS,...  183 us
    pallas_call x2, Pallas kernels, forward_call(): pl.pallas_call(hosted.wrap(forward_kernel, FORWARD_INS, FORWARD_OUTS, pac...  160 us
    pallas_call x1, Pallas kernels, gather_call(): pl.pallas_call(partial(gather_kernel, count, pieces), in_specs=[pl.BlockS...  84.4 us
    pallas_call x1, Pallas kernels, scatter_call(): pl.pallas_call(partial(scatter_kernel, count, pieces), in_specs=[pl.Block...  82.7 us
    psum x1, waiting for transfers between devices, local(): lax.psum(lax.optimization_barrier((latter[4], grad_bcs[0]))[0], 'tp')  42 us
    psum x1, blocking collectives, local(): gain_total = lax.psum(grad_norm_gain, ('fsdp', 'tp'))  39.2 us
    pallas_call x2, Pallas kernels, branch_call(): pl.pallas_call(partial(branch_kernel, tp_size, inner * tp_size), grid=(gr...  33 us
    pallas_call x1, Pallas kernels, weight_call(): pl.pallas_call(partial(weight_kernel, micro), grid=(model // BLOCK,), in_...  28.4 us
  transfers between devices with their start and end apart: 5, of which 2 were waited for; matrix products, arithmetic and copies ran while one was open for 4% of the time, Pallas kernels for 46%

profile of v2, /device:TPU:0, one launch (start us, length us, event | category | flops | bytes accessed | tf_op | source)
XLA Modules:
  0.0 782.3 jit_solution(1098569093328423805)
XLA Ops:
  7.2 2.2 fusion.5
  9.5 0.5 fusion.7
  10.1 1.5 slice_bitcast_fusion.3
  11.6 0.1 copy.75
  11.7 0.7 pad.95.refs_3_
  12.4 84.4 %gather_weights.1 = (bf16[2048,1024]{1,0:T(8,128)(2,1)}, bf16[2048,1024]{1,0:T(8,128)(2,1)}, bf16[2048,256]{1,0:T(8,128)(2,1)}, bf16[2048,128]{1,0:T(8,128)(2,1)}, bf16[1024,2048]{1,0:T(8,128)(2,1)}) custom-call(bf16[256,1024]{1,0:T(8,128)(2,1)} %refs_0_.1, bf16[256,1024]{1,0:T(8,128)(2,1)} %refs_1_.1, bf16[256,256]{1,0:T(8,128)(2,1)} %refs_2_.1, ...), custom_call_target="tpu_custom_call" | custom-call | bytes 262144000 | tf_op jit(solution)/shard_map/gather_weights/pallas_call | solution.py:909
  97.0 0.6 convert_bitcast_fusion.1
  97.6 0.1 slice.173
  97.7 0.1 slice.174
  97.7 0.1 slice.182
  97.8 0.1 slice.183
  97.9 0.1 pad_add_fusion
  98.0 0.1 broadcast_bitcast_fusion.5
  98.3 0.1 compare_convert_fusion.4
  98.5 0.1 fusion.57
  98.6 0.1 stack.129
  98.7 1.0 copy.76.cols_ref.refs_18_
  99.8 0.7 broadcast_in_dim_reshape.3.skip_ref.refs_11_.refs_16_
  100.5 0.1 stack.122
  100.7 1.0 copy.77.refs_12_.refs_18_
  101.7 0.5 pad_bitcast_fusion
  102.2 3.1 slice_bitcast_fusion.4
  105.3 52.8 %ssd_forward.2 = (bf16[1024,1024]{1,0:T(8,128)(2,1)}, f32[1024,1024]{1,0:T(8,128)}, f32[1024,1024]{1,0:T(8,128)}, bf16[1024,256]{1,0:T(8,128)(2,1)}, f32[1024,25...) custom-call(bf16[1024,2048]{1,0:T(8,128)(2,1)} %all-gather.3.cloned., ...), custom_call_target="tpu_custom_call" | custom-call | flops 15032385536 | bytes 41943040 | tf_op jit(solution)/shard_map/ssd_forward/pallas_call | solution.py:688
  158.2 20.2 %all-gather.5.cloned.1.call-done.refs_0_.refs_1_ = bf16[1024,2048]{1,0:T(8,128)(2,1)} async-done(((bf16[256,2048]{1,0:T(8,128)(2,1)}), bf16[1024,2048]{1,0:T(8,128)(2,1)}) %all-gather.5.cloned.1.call-update) | async-done | bytes 4194320 | tf_op jit(solution)/shard_map/all_gather | solution.py:1140
  178.4 106.7 %ssd_forward.3 = (bf16[1024,1024]{1,0:T(8,128)(2,1)}, f32[1024,1024]{1,0:T(8,128)}, f32[1024,1024]{1,0:T(8,128)}, bf16[1024,256]{1,0:T(8,128)(2,1)}, f32[1024,25...) custom-call(bf16[1024,2048]{1,0:T(8,128)(2,1)} %all-gather.5.cloned., ...), custom_call_target="tpu_custom_call" | custom-call | flops 15032385536 | bytes 41943040 | tf_op jit(solution)/shard_map/ssd_forward/pallas_call | solution.py:688
  285.1 15.5 %branch_gradient.2 = (bf16[1024,1024]{1,0:T(8,128)(2,1)S(1)}, f32[1024,128]{1,0:T(8,128)S(1)}) custom-call(bf16[1024,2048]{1,0:T(8,128)(2,1)} %get-tuple-element.84.cot_ref.refs_2_, bf16[1024,2048]{1,0:T(8,128)(2,1)} %get-tuple-element.81.out_w.refs_14_, bf16[1024,1024]{1,0:T(8,128)(2,1)} %get-tuple-element.85.gate_ref.refs_0_, ...), custom_call_target="tpu_custom_call" | custom-call | flops 4294967296 | bytes 20971520 | tf_op jit(solution)/shard_map/branch_gradient/pallas_call | solution.py:738
  300.6 0.8 copy-done.2
  301.4 1.3 copy-done.7
  302.7 99.6 %ssd_backward.2 = (bf16[1024,1024]{1,0:T(8,128)(2,1)}, bf16[1024,1024]{1,0:T(8,128)(2,1)}, bf16[1024,1024]{1,0:T(8,128)(2,1)}, bf16[1024,128]{1,0:T(8,128)(2,1)}...) custom-call(bf16[1024,1024]{1,0:T(8,128)(2,1)} %get-tuple-element.85, ...), custom_call_target="tpu_custom_call" | custom-call | flops 12884901888 | bytes 62914560 | tf_op jit(solution)/shard_map/ssd_backward/pallas_call | solution.py:780
  402.4 17.5 %branch_gradient.3 = (bf16[1024,1024]{1,0:T(8,128)(2,1)S(1)}, f32[1024,128]{1,0:T(8,128)S(1)}) custom-call(bf16[1024,2048]{1,0:T(8,128)(2,1)} %get-tuple-element.96.cot_ref.refs_3_, bf16[1024,2048]{1,0:T(8,128)(2,1)} %get-tuple-element.81.out_w.refs_14_, bf16[1024,1024]{1,0:T(8,128)(2,1)} %get-tuple-element.97.gate_ref.refs_0_, ...), custom_call_target="tpu_custom_call" | custom-call | flops 4294967296 | bytes 20971520 | tf_op jit(solution)/shard_map/branch_gradient/pallas_call | solution.py:738
  419.9 0.8 copy-done.3
  420.7 1.3 copy-done.6
  422.0 83.0 %ssd_backward.3 = (bf16[1024,1024]{1,0:T(8,128)(2,1)}, bf16[1024,1024]{1,0:T(8,128)(2,1)}, bf16[1024,1024]{1,0:T(8,128)(2,1)}, bf16[1024,128]{1,0:T(8,128)(2,1)}...) custom-call(bf16[1024,1024]{1,0:T(8,128)(2,1)} %get-tuple-element.97, ...), custom_call_target="tpu_custom_call" | custom-call | flops 12884901888 | bytes 62914560 | tf_op jit(solution)/shard_map/ssd_backward/pallas_call | solution.py:780
  505.1 42.0 %all-reduce.33.cloned.1.call-done = bf16[1024,256]{1,0:T(8,128)(2,1)} async-done(((bf16[1024,256]{1,0:T(8,128)(2,1)}), bf16[1024,256]{1,0:T(8,128)(2,1)}) %all-reduce.33.cloned.1.call-update) | async-done | bytes 524304 | tf_op jit(solution)/shard_map/psum | solution.py:1189
  547.1 2.5 convert_element_type.212
  549.7 1.0 dynamic-slice_reduce_fusion
  550.7 1.0 dynamic-slice_reduce_fusion.1
  551.7 3.9 fusion.41
  555.7 1.5 maximum_bitcast_fusion
  557.2 0.9 copy-done.8
  558.1 14.6 %out_gradients.1.refs_4_ = bf16[1024,2048]{1,0:T(8,128)(2,1)} custom-call(bf16[1024,1024]{1,0:T(8,128)(2,1)S(1)} %copy-done.8, bf16[1024,1024]{1,0:T(8,128)(2,1)} %get-tuple-element.126.refs_1_, bf16[1024,2048]{1,0:T(8,128)(2,1)} %get-tuple-element.84.cot_ref.refs_2_, bf16[1024,2048]{1,0:T(8,128)(2,1)} %get-tuple-element.96.cot_ref.refs_3_), custom_call_target="tpu_custom_call" | custom-call | flops 8589934592 | bytes 31457280 | tf_op jit(solution)/shard_map/out_gradients/pallas_call | solution.py:1057
  572.7 1.8 multiply_reduce_fusion.7
  574.5 1.8 multiply_reduce_fusion.3
  576.3 24.6 %all-reduce.27 = (f32[8,1024]{1,0:T(8,128)S(1)}, f32[4,256]{1,0:T(4,128)}, f32[256]{0:T(256)}, f32[8,128]{1,0:T(8,128)}) all-reduce(f32[8,1024]{1,0:T(8,128)S(1)} %add.207, f32[4,256]{1,0:T(4,128)S(1)} %maximum_add_fusion, f32[256]{0:T(256)S(1)} %add.209, f32[8,128]{1,0:T(8,128)S(1)} %add.210), channel_id=1, replica_groups=mesh['fsdp'=8,'tp'=4] {'fsdp'}, use_global_device_ids=true, to_apply=%region_7.8 | all-reduce | flops 10496 | bytes 83968 | tf_op jit(solution)/shard_map/psum | solution.py:1228
  600.9 0.6 slice.216
  601.5 0.6 fusion.71
  602.1 0.7 reshape_squeeze.3
  602.8 1.4 fusion.23
  604.3 28.4 %weight_gradients.1 = (bf16[2048,1024]{1,0:T(8,128)(2,1)}, bf16[2048,1024]{1,0:T(8,128)(2,1)}, bf16[2048,256]{1,0:T(8,128)(2,1)S(1)}, bf16[2048,128]{1,0:T(8,128)(2,1)S(1)}) custom-call(bf16[1024,2048]{1,0:T(8,128)(2,1)} %all-gather.3.cloned.1.call-done.in_ref.refs_0_, bf16[1024,2048]{1,0:T(8,128)(2,1)} %all-gather.5.cloned.1.call-done.refs_0_.refs_1_, ...), custom_call_target="tpu_custom_call" | custom-call | flops 20401094656 | bytes 41943040 | tf_op jit(solution)/shard_map/weight_gradients/pallas_call | solution.py:1031
  632.7 82.7 %scatter_gradients.1 = (f32[256,1024]{1,0:T(8,128)S(1)}, f32[256,1024]{1,0:T(8,128)S(1)}, f32[256,256]{1,0:T(8,128)S(1)}, f32[256,128]{1,0:T(8,128)S(1)}, f32[1024,256]{1,0:T(8,128)S(1)}) custom-call(bf16[2048,1024]{1,0:T(8,128)(2,1)} %get-tuple-element.121.refs_0_, bf16[2048,1024]{1,0:T(8,128)(2,1)} %get-tuple-element.122.refs_1_, ...), custom_call_target="tpu_custom_call" | custom-call | bytes 262144000 | tf_op jit(solution)/shard_map/scatter_gradients/pallas_call | solution.py:999
  715.4 0.7 copy.81
  716.0 1.3 reduce_sum.139
  717.4 1.2 slice_bitcast_fusion.6
  718.6 1.2 bitcast_multiply_fusion.4
  719.8 3.8 convolution_add_fusion.1
  723.5 2.2 convolution_add_fusion
  725.8 0.6 copy-done.13
  726.4 1.2 fusion.10
  727.7 39.2 %psum.51 = f32[2048]{0:T(1024)} all-reduce(f32[2048]{0:T(1024)S(1)} %get-tuple-element.184), channel_id=1, replica_groups=mesh['fsdp'=8,'tp'=4] {'fsdp','tp'}, use_global_device_ids=true, to_apply=%region_6.7 | all-reduce | flops 2048 | bytes 16384 | tf_op jit(solution)/shard_map/psum | solution.py:1231
  766.9 5.1 fusion.3
  772.0 1.0 copy.94
  772.9 1.0 copy.95
  773.9 0.7 copy.96
  774.6 1.0 copy.97
  (90 shorter events, 1.0 us)
Async XLA Ops:
  7.2 2.3 copy-start.11
  7.2 2.3 copy-start.19
  7.2 89.7 %all-gather.3.cloned.1.call-start = ((), (), s32[]{:S(2)}) async-start(), calls=%async_computation.1 | async-start | bytes 5242880 | tf_op jit(solution)/shard_map/all_gather | solution.py:1140
  10.0 1.6 copy-start.23
  11.5 85.4 %copy-start.22 = (s32[2,1,1024]{2,1,0:T(1,128)S(1)}, s32[2,1,1024]{2,1,0:T(1,128)}, u32[]{:S(2)}) copy-start(s32[2,1,1024]{2,1,0:T(1,128)} %param.18) | copy-start | bytes 24580
  11.5 88.2 %copy-start.28 = (f32[16]{0:T(128)S(1)}, f32[16]{0:T(128)}, u32[]{:S(2)}) copy-start(f32[16]{0:T(128)} %param.31) | copy-start | bytes 196
  11.5 166.8 %all-gather.5.cloned.1.call-start = ((), (), s32[]{:S(2)}) async-start(), calls=%async_computation.2 | async-start | bytes 5242880 | tf_op jit(solution)/shard_map/all_gather | solution.py:1140
  12.4 89.3 %copy-start.30 = (f32[16]{0:T(128)S(1)}, f32[16]{0:T(128)}, u32[]{:S(2)}) copy-start(f32[16]{0:T(128)} %param.30) | copy-start | bytes 196
  12.4 89.3 %copy-start.29 = (f32[16]{0:T(128)S(1)}, f32[16]{0:T(128)}, u32[]{:S(2)}) copy-start(f32[16]{0:T(128)} %param.29) | copy-start | bytes 196
  96.9 408.1 %all-reduce.31.cloned.1.call-start = ((), (), s32[]{:S(2)}) async-start(), calls=%async_computation.3 | async-start | bytes 1048576 | tf_op jit(solution)/shard_map/psum | solution.py:1186
  178.4 106.7 %copy-start.4 = (f32[1024]{0:T(1024)S(1)}, f32[1024]{0:T(1024)}, u32[]{:S(2)}) copy-start(f32[1024]{0:T(1024)} %param.32) | copy-start | bytes 12292
  300.6 0.8 copy-start.2
  301.4 1.3 copy-start.7
  302.7 99.6 %copy-start.5 = (f32[1024]{0:T(1024)S(1)}, f32[1024]{0:T(1024)}, u32[]{:S(2)}) copy-start(f32[1024]{0:T(1024)} %param.32) | copy-start | bytes 12292
  402.3 144.7 %all-reduce.33.cloned.1.call-start = ((), (), s32[]{:S(2)}) async-start(), calls=%async_computation.4 | async-start | bytes 1048576 | tf_op jit(solution)/shard_map/psum | solution.py:1189
  419.9 0.8 copy-start.3
  420.7 1.3 copy-start.6
  505.0 218.5 %reduce-scatter.2.cloned.1.call-start = ((), (), s32[]{:S(2)}) async-start(), calls=%async_computation.5 | async-start | bytes 5242880 | tf_op jit(solution)/shard_map/reduce_scatter | solution.py:1144
  547.1 2.5 copy-start.27
  547.1 2.5 copy-start.25
  547.1 2.5 copy-start.26
  547.1 2.5 copy-start.20
  547.1 2.5 copy-start.21
  555.7 2.4 copy-start.8
  558.1 14.6 %copy-start.15 = (f32[1024,256]{1,0:T(8,128)S(1)}, f32[1024,256]{1,0:T(8,128)}, u32[]{:S(2)}) copy-start(f32[1024,256]{1,0:T(8,128)} %get-tuple-element.109) | copy-start | bytes 3145732
  558.1 14.6 %copy-start.17 = (bf16[1024,256]{1,0:T(8,128)(2,1)S(1)}, bf16[1024,256]{1,0:T(8,128)(2,1)}, u32[]{:S(2)}) copy-start(bf16[1024,256]{1,0:T(8,128)(2,1)} %all-reduce.31.cloned.1.call-done) | copy-start | bytes 1572868
  558.1 14.6 %copy-start.24 = (f32[256]{0:T(256)S(1)}, f32[256]{0:T(256)}, u32[]{:S(2)}) copy-start(f32[256]{0:T(256)} %param.28) | copy-start | bytes 3076
  572.7 1.8 copy-start.16
  572.7 1.8 copy-start.18
  576.3 28.0 %copy-start.9 = (bf16[1024,128]{1,0:T(8,128)(2,1)S(1)}, bf16[1024,128]{1,0:T(8,128)(2,1)}, u32[]{:S(2)}) copy-start(bf16[1024,128]{1,0:T(8,128)(2,1)} %get-tuple-element.117.refs_5_) | copy-start | bytes 786436
  576.3 28.0 %copy-start.10 = (bf16[1024,128]{1,0:T(8,128)(2,1)S(1)}, bf16[1024,128]{1,0:T(8,128)(2,1)}, u32[]{:S(2)}) copy-start(bf16[1024,128]{1,0:T(8,128)(2,1)} %get-tuple-element.120.refs_9_) | copy-start | bytes 786436
  604.2 28.4 %copy-start = (bf16[1024,256]{1,0:T(8,128)(2,1)}, bf16[1024,256]{1,0:T(8,128)(2,1)S(1)}, u32[]{:S(2)}) copy-start(bf16[1024,256]{1,0:T(8,128)(2,1)S(1)} %get-tuple-element.222.refs_8_) | copy-start | bytes 1572868
  604.2 28.4 %copy-start.1 = (bf16[1024,256]{1,0:T(8,128)(2,1)}, bf16[1024,256]{1,0:T(8,128)(2,1)S(1)}, u32[]{:S(2)}) copy-start(bf16[1024,256]{1,0:T(8,128)(2,1)S(1)} %get-tuple-element.221.refs_4_) | copy-start | bytes 1572868
  723.5 2.3 copy-start.12
  723.5 2.9 copy-start.13
  725.7 1.9 copy-start.14
Sparse Core Ops, SparseCore 0:
  11.7 83.4 all-gather.2
  97.3 81.0 all-gather.4
  402.4 44.2 all-reduce.30
  505.1 41.8 all-reduce.32
  549.2 76.7 reduce-scatter.1

commit v3 on v2

--- a/solution.py
+++ b/solution.py
@@ -158,20 +158,6 @@
             self.recv_sem.at[flow, hop], (self.column, neighbour),
         )
 
-    def greet(self):
-        barrier = pltpu.get_barrier_semaphore()
-        for flow in range(2):
-            neighbour = self.me + 1 if flow == 0 else self.me - 1
-
-            @pl.when((neighbour >= 0) & (neighbour < self.size))
-            def _():
-                pl.semaphore_signal(
-                    barrier, inc=1, device_id=(self.column, neighbour), device_id_type=MESH
-                )
-
-        inside = (self.me > 0) & (self.me < self.size - 1)
-        pl.semaphore_wait(barrier, 1 + inside.astype(jnp.int32))
-
     def begin(self):
         self.final().start()
         for hop in range(self.size - 1):
@@ -286,17 +272,16 @@
     actions = [[] for _ in range(size + 1)]
     if scatter:
         first = 1 if gather else 0
-        actions[0] += [scatter.greet, scatter.begin]
+        actions[0].append(scatter.begin)
         for hop in range(size - 1):
             actions[first + hop].append(partial(scatter.hop, hop))
         actions[first + size - 1].append(partial(scatter.end, out))
     if gather:
-        if not scatter:
-            actions[0].append(partial(LineScatter.greet, gather))
         actions[0].append(gather.begin)
         for hop in range(1, size - 1):
             actions[hop].insert(0, partial(gather.hop, hop))
         actions[size - 1].insert(0, gather.end)
+    actions = [todo for todo in actions if todo]
     for at, todo in zip(steps, actions):
         if todo:
 
@@ -347,13 +332,19 @@
         def kernel(*refs):
             sources, targets = refs[ins : ins + hosts], refs[ins + hosts + outs : ins + outs + 2 * hosts]
             tail = refs[len(refs) - spare :]
+            step = pl.program_id(0) * pl.num_programs(1) + pl.program_id(1)
+            me, column = lax.axis_index("tp"), lax.axis_index("fsdp")
+
+            @pl.when(step == 0)
+            def _():
+                greet([(column, lax.rem(me + hop, size)) for hop in range(1, size)])
+
             body(
                 *refs[:ins], *refs[ins + hosts : ins + hosts + outs],
                 *refs[ins + outs + 2 * hosts : len(refs) - spare],
             )
             scatter = LineScatter(size, sources[0], *tail[:7]) if has_scatter else None
             gather = LineGather(size, sources[-1], targets[-1], *tail[-3:]) if has_gather else None
-            step = pl.program_id(0) * pl.num_programs(1) + pl.program_id(1)
             run_line(step, pace, scatter, gather, targets[0])
 
         return kernel
@@ -788,8 +779,8 @@
             rows_of(cols.shape[1]), pl.BlockSpec((1, GROUP), lambda g, j: (0, last - g)),
         ] + hosted.in_specs(),
         out_specs=[
-            wide, wide, wide, rows_of(128), rows_of(2 * STATE), rows_of(model),
-            pl.BlockSpec((8, inner), lambda g, j: (0, 0)), pl.BlockSpec((8, 128), lambda g, j: (0, 0)),
+            wide, wide, wide, rows_of(128), rows_of(2 * STATE),
+            rows_of(model), pl.BlockSpec((8, inner), lambda g, j: (0, 0)), pl.BlockSpec((8, 128), lambda g, j: (0, 0)),
         ] + specs,
         out_shape=[
             shape((length, inner), BF16), shape((length, inner), BF16), shape((length, inner), BF16),
@@ -1069,6 +1060,554 @@
     )(*branches, *cotans)
 
 
+def tail_kernel(chips, tp_size, micro, widths, *refs):
+    columns, lows, parts, raws = refs[:4], refs[4:12], refs[12:14], refs[14:16]
+    cols_ref, staps_ref, sbias_ref, pack = refs[16:20]
+    outs, state_out, pack_out, ssum_out, low_out = refs[20:24], refs[24], refs[25], refs[26], refs[27]
+    (
+        cols_s, give, took, mine, came, passed, total_s, kept_s,
+        sgive, stook, smine, scame, stotal, skept_s,
+        pack_took, pack_sum, pack_slots, ssum, ssum_took, ssum_sum, ssum_slots,
+        raw_s, own_s, slots_s, whole_s, sum_s, low_s, vbuf, gcbuf,
+        cols_sem, give_sem, took_sem, send_sem, recv_sem, sgive_sem, stook_sem, ssend_sem, srecv_sem,
+        pass_sem, pack_sem, ssum_sem, raw_sem, own_sem, part_send, part_recv, whole_send, whole_recv,
+    ) = refs[28:]
+    step, steps = pl.program_id(0), pl.num_programs(0)
+    me, line = lax.axis_index("fsdp"), lax.axis_index("tp")
+    count = 2 * chips
+    core, chip = lax.rem(me, 2), me // 2
+    partner = me + 1 - 2 * core
+    split = total_s.shape[1] // 256 * 128
+
+    def flipped(hop, which_core):
+        x, y = lax.rem(chip, 2), chip // 2
+        hop_x, hop_y = hop % 2, hop // 2
+        x, y = x + hop_x - 2 * x * hop_x, y + hop_y - 2 * y * hop_y
+        return (2 * y + x) * 2 + which_core
+
+    def tile_of(at):
+        pair = lax.rem(at, count) // 2
+        hop = jnp.where(pair == 0, 3, pair - 1)
+        return hop, flipped(hop, jnp.where(lax.rem(at, 2) == 0, 1 - core, core))
+
+    def fetch(at, which):
+        _, shard = tile_of(at)
+        slot = lax.rem(at, 2)
+        return pltpu.make_async_copy(
+            columns[which].at[:, pl.ds(pl.multiple_of(shard * BLOCK, BLOCK), BLOCK)],
+            cols_s.at[slot, which], cols_sem.at[slot, which],
+        )
+
+    def far(hop):
+        return (flipped(hop, core), line)
+
+    def giving(hop):
+        return remote_copy(
+            give.at[hop], took.at[hop], give_sem.at[hop], took_sem.at[hop], (partner, line)
+        )
+
+    def sending(hop):
+        return remote_copy(
+            mine.at[hop - 1], came.at[hop - 1], send_sem.at[hop - 1], recv_sem.at[hop - 1], far(hop)
+        )
+
+    def passing(hop):
+        columns = pl.ds(0, split) if hop == 1 else pl.ds(split, total_s.shape[1] - split)
+        return remote_copy(
+            mine.at[2, :, columns], passed.at[:, columns], pass_sem.at[0, hop - 1],
+            pass_sem.at[1, hop - 1], far(hop),
+        )
+
+    def sgiving(hop):
+        return remote_copy(
+            sgive.at[hop], stook.at[hop], sgive_sem.at[hop], stook_sem.at[hop], (partner, line)
+        )
+
+    def ssending(hop):
+        return remote_copy(
+            smine.at[hop - 1], scame.at[hop - 1], ssend_sem.at[hop - 1], srecv_sem.at[hop - 1], far(hop)
+        )
+
+    pack_pass = remote_copy(pack, pack_took, pack_sem.at[0, 0], pack_sem.at[1, 0], (partner, line))
+    ssum_pass = remote_copy(ssum, ssum_took, ssum_sem.at[0, 0], ssum_sem.at[1, 0], (partner, line))
+
+    def pack_send(hop):
+        return remote_copy(
+            pack_sum, pack_slots.at[chip], pack_sem.at[0, hop], pack_sem.at[1, hop], far(hop)
+        )
+
+    def ssum_send(hop):
+        return remote_copy(
+            ssum_sum, ssum_slots.at[chip], ssum_sem.at[0, hop], ssum_sem.at[1, hop], far(hop)
+        )
+
+    def rows_at(ref, at):
+        return ref.at[pl.ds(pl.multiple_of(at * GROUP, GROUP), GROUP), :]
+
+    def handing(hop):
+        owner = lax.rem(line + hop, tp_size)
+        return remote_copy(
+            rows_at(parts[late], owner), slots_s.at[line], part_send.at[hop - 1],
+            part_recv.at[hop - 1], (me, owner),
+        )
+
+    late = micro - 1
+
+    def own_part():
+        return pltpu.make_async_copy(rows_at(parts[late], line), own_s, own_sem.at[late])
+
+    def ready(at):
+        length = raws[at].shape[0]
+        return pltpu.make_async_copy(
+            parts[at], whole_s.at[pl.ds(at * length, length), :], own_sem.at[at]
+        )
+
+    def raw_copy(at):
+        length = raws[at].shape[0]
+        return pltpu.make_async_copy(
+            raws[at], raw_s.at[pl.ds(at * length, length), :], raw_sem.at[at]
+        )
+
+    groups = raws[0].shape[0] // GROUP
+
+    def spreading(hop):
+        block = rows_at(whole_s, late * groups + line)
+        return remote_copy(
+            sum_s, block, whole_send.at[hop - 1], whole_recv.at[hop - 1],
+            (me, lax.rem(line + hop, tp_size)),
+        )
+
+    @pl.when(step == 0)
+    def _():
+        for which in range(4):
+            fetch(step, which).start()
+        own_part().start()
+        for at in range(micro):
+            raw_copy(at).start()
+            if at != late:
+                ready(at).start()
+        greet(
+            [far(hop) for hop in range(1, chips)] + [(partner, line)]
+            + [(me, lax.rem(line + hop, tp_size)) for hop in range(1, tp_size)]
+        )
+        for hop in range(1, tp_size):
+            handing(hop).start()
+        pack_pass.start()
+
+    @pl.when(step + 1 < count)
+    def _():
+        for which in range(4):
+            fetch(step + 1, which).start()
+
+    @pl.when((step + 1 >= count) & (step + 1 < steps))
+    def _():
+        for which in range(2):
+            fetch(step + 1, which).start()
+
+    for which in range(2):
+        fetch(step, which).wait()
+
+    @pl.when(step < count)
+    def _():
+        for which in range(2, 4):
+            fetch(step, which).wait()
+
+    slot = lax.rem(step, 2)
+    hop, _ = tile_of(step)
+    even = lax.rem(step, 2) == 0
+
+    def tile(which):
+        sides = (0, 1) if which < 3 else (2, 3)
+        return mm_tn(cols_s[slot, sides[0]], lows[2 * which][...]) + mm_tn(
+            cols_s[slot, sides[1]], lows[2 * which + 1][...]
+        )
+
+    @pl.when((step < count) & even)
+    def _():
+        at = 0
+        for which, width in enumerate(widths):
+            give[hop, :, at : at + width] = tile(which).astype(BF16)
+            at += width
+        giving(hop).start()
+
+    @pl.when((step < count) & jnp.logical_not(even))
+    def _():
+        at = 0
+        for which, width in enumerate(widths):
+            total_s[:, at : at + width] = tile(which)
+            at += width
+        giving(hop).wait_recv()
+        total_s[...] += took[hop].astype(F32)
+
+        @pl.when(hop == 3)
+        def _():
+            mine[2] = total_s[...].astype(BF16)
+            passing(1).start()
+            passing(2).start()
+
+        @pl.when(hop == 0)
+        def _():
+            kept_s[...] = total_s[...]
+
+        @pl.when(hop == 1)
+        def _():
+            passing(2).wait_recv()
+            total_s[:, split:] += passed[:, split:].astype(F32)
+            mine[0] = total_s[...].astype(BF16)
+            sending(1).start()
+
+        @pl.when(hop == 2)
+        def _():
+            passing(1).wait_recv()
+            total_s[:, :split] += passed[:, :split].astype(F32)
+            mine[1] = total_s[...].astype(BF16)
+            sending(2).start()
+
+    @pl.when(step == 1)
+    def _():
+        pack_pass.wait()
+        pack_sum[...] = pack[...] + pack_took[...]
+        pack_slots[chip] = pack_sum[...]
+        for other in range(1, chips):
+            pack_send(other).start()
+
+    @pl.when(step == 5)
+    def _():
+        own_part().wait()
+        slots_s[line] = own_s[...]
+        for hop in range(1, tp_size):
+            handing(hop).wait()
+        total = slots_s[0].astype(F32)
+        for other in range(1, tp_size):
+            total = total + slots_s[other].astype(F32)
+        sum_s[...] = total.astype(BF16)
+        mine_rows = rows_at(whole_s, late * groups + line)
+        mine_rows[...] = sum_s[...]
+        for hop in range(1, tp_size):
+            spreading(hop).start()
+
+    @pl.when(step == count - 1)
+    def _():
+        for at in range(micro):
+            raw_copy(at).wait()
+            if at != late:
+                ready(at).wait()
+        for hop in range(1, tp_size):
+            spreading(hop).wait()
+        ssum[...] = jnp.zeros(ssum.shape, F32)
+        taps, bias = staps_ref[...], sbias_ref[...]
+
+        def state_group(turn, carry):
+            group = micro * groups - 1 - turn
+            at = pl.multiple_of(group * GROUP, GROUP)
+            cols = cols_ref[pl.ds(at, GROUP), :]
+            vbuf[HALO : HALO + GROUP, :] = raw_s[pl.ds(at, GROUP), :]
+            ahead = pl.multiple_of(jnp.maximum(group * (GROUP // HALO) - 1, 0) * HALO, HALO)
+            vbuf[0:HALO, :] = raw_s[pl.ds(ahead, HALO), :]
+            moved = shifted_values(vbuf, cols)
+            conv = conv_of(moved, taps, bias)
+            sig = jax.nn.sigmoid(conv)
+            grad = whole_s[pl.ds(at, GROUP), :].astype(F32) * (sig * (1.0 + conv * (1.0 - sig)))
+            gcbuf[GROUP : GROUP + HALO, :] = gcbuf[0:HALO, :]
+            gcbuf[0:GROUP, :] = grad
+            back = taps[0:1, :] * grad
+            for offset in range(1, CONV):
+                up = jnp.where(
+                    cols[:, 2 + offset : 3 + offset] > 0.0, gcbuf[offset : offset + GROUP, :], 0.0
+                )
+                back = back + taps[offset : offset + 1, :] * up
+            low_s[pl.ds(at, GROUP), :] = back.astype(BF16)
+            for offset in range(CONV):
+                ssum[offset : offset + 1, :] += jnp.sum(grad * moved[offset], axis=0, keepdims=True)
+            ssum[CONV : CONV + 1, :] += jnp.sum(grad, axis=0, keepdims=True)
+            return carry
+
+        lax.fori_loop(0, micro * groups, state_group, 0)
+        ssum_pass.start()
+        for at in range(micro):
+            low_out[at] = low_s[pl.ds(pl.multiple_of((at * groups + line) * GROUP, GROUP), GROUP), :]
+
+    def state_tile():
+        length = groups * GROUP
+        return mm_tn(cols_s[slot, 0], low_s[0:length, :]) + mm_tn(
+            cols_s[slot, 1], low_s[length : 2 * length, :]
+        )
+
+    @pl.when((step >= count) & even)
+    def _():
+        sgive[hop] = state_tile().astype(BF16)
+        sgiving(hop).start()
+
+    @pl.when((step >= count) & jnp.logical_not(even))
+    def _():
+        stotal[...] = state_tile()
+        sgiving(hop).wait_recv()
+        stotal[...] += stook[hop].astype(F32)
+
+        @pl.when(hop == 0)
+        def _():
+            skept_s[...] = stotal[...]
+
+        @pl.when(hop > 0)
+        def _():
+            smine[hop - 1] = stotal[...].astype(BF16)
+            ssending(hop).start()
+
+    @pl.when(step == count + 1)
+    def _():
+        ssum_pass.wait()
+        ssum_sum[...] = ssum[...] + ssum_took[...]
+        ssum_slots[chip] = ssum_sum[...]
+        for other in range(1, chips):
+            ssum_send(other).start()
+
+    @pl.when(step == steps - 1)
+    def _():
+        for sends, slots, out in ((pack_send, pack_slots, pack_out), (ssum_send, ssum_slots, ssum_out)):
+            for other in range(1, chips):
+                sends(other).wait()
+            total = slots[0]
+            for other in range(1, chips):
+                total = total + slots[other]
+            out[...] = total
+        for other in (1, 2):
+            sending(other).wait_recv()
+            kept_s[...] += came[other - 1].astype(F32)
+        for other in range(1, chips):
+            ssending(other).wait_recv()
+            skept_s[...] += scame[other - 1].astype(F32)
+        state_out[...] = skept_s[...]
+        at = 0
+        for which, width in enumerate(widths):
+            part = kept_s[:, at : at + width]
+            outs[which][...] = part if which < 3 else jnp.transpose(part)
+            at += width
+        for other in (1, 2):
+            passing(other).wait_send()
+            sending(other).wait_send()
+        for other in range(1, chips):
+            ssending(other).wait_send()
+        for other in range(chips):
+            giving(other).wait_send()
+            sgiving(other).wait_send()
+
+
+def tail_call(count, tp_size, inputs, cotans, lows, parts, raws, cols, staps, sbias, pack):
+    micro, length = len(inputs), inputs[0].shape[0]
+    chips = count // 2
+    order = [low[which] for which in range(4) for low in lows]
+    widths = [low.shape[1] for low in order[::2]]
+    total, narrow = sum(widths), 2 * STATE
+    hbm = pl.BlockSpec(memory_space=pl.ANY)
+    full = lambda array: pl.BlockSpec(array.shape, lambda i: (0,) * array.ndim, pipeline_mode=pl.Buffered(1))
+    out_dims = [(BLOCK, width) for width in widths[:3]] + [(widths[3], BLOCK), (BLOCK, narrow)]
+    out_shapes = [shape(dims) for dims in out_dims] + [
+        shape(pack.shape), shape((8, narrow)), shape((micro, GROUP, narrow), BF16)
+    ]
+    dma = lambda *dims: pltpu.SemaphoreType.DMA(dims)
+    return pl.pallas_call(
+        partial(tail_kernel, chips, tp_size, micro, widths),
+        grid=(2 * count,),
+        in_specs=[hbm] * 4 + [full(low) for low in order] + [hbm] * 4
+        + [full(cols), full(staps), full(sbias), full(pack)],
+        out_specs=[full(each) for each in out_shapes],
+        out_shape=out_shapes,
+        scratch_shapes=[
+            pltpu.VMEM((2, 4, length, BLOCK), BF16),
+            pltpu.VMEM((chips, BLOCK, total), BF16),
+            pltpu.VMEM((chips, BLOCK, total), BF16),
+            pltpu.VMEM((3, BLOCK, total), BF16),
+            pltpu.VMEM((2, BLOCK, total), BF16),
+            pltpu.VMEM((BLOCK, total), BF16),
+            pltpu.VMEM((BLOCK, total), F32),
+            pltpu.VMEM((BLOCK, total), F32),
+            pltpu.VMEM((chips, BLOCK, narrow), BF16),
+            pltpu.VMEM((chips, BLOCK, narrow), BF16),
+            pltpu.VMEM((chips - 1, BLOCK, narrow), BF16),
+            pltpu.VMEM((chips - 1, BLOCK, narrow), BF16),
+            pltpu.VMEM((BLOCK, narrow), F32),
+            pltpu.VMEM((BLOCK, narrow), F32),
+            pltpu.VMEM(pack.shape, F32),
+            pltpu.VMEM(pack.shape, F32),
+            pltpu.VMEM((chips,) + pack.shape, F32),
+            pltpu.VMEM((8, narrow), F32),
+            pltpu.VMEM((8, narrow), F32),
+            pltpu.VMEM((8, narrow), F32),
+            pltpu.VMEM((chips, 8, narrow), F32),
+            pltpu.VMEM((micro * length, narrow), F32),
+            pltpu.VMEM((GROUP, narrow), BF16),
+            pltpu.VMEM((tp_size, GROUP, narrow), BF16),
+            pltpu.VMEM((micro * length, narrow), BF16),
+            pltpu.VMEM((GROUP, narrow), BF16),
+            pltpu.VMEM((micro * length, narrow), BF16),
+            pltpu.VMEM((GROUP + HALO, narrow), F32),
+            pltpu.VMEM((GROUP + HALO, narrow), F32),
+            dma(2, 4), dma(chips), dma(chips), dma(2), dma(2),
+            dma(chips), dma(chips), dma(chips - 1), dma(chips - 1),
+            dma(2, 2), dma(2, chips), dma(2, chips), dma(micro), dma(micro),
+            dma(tp_size - 1), dma(tp_size - 1), dma(tp_size - 1), dma(tp_size - 1),
+        ],
+        compiler_params=pltpu.CompilerParams(
+            collective_id=6, has_side_effects=True, vmem_limit_bytes=62 << 20
+        ),
+        cost_estimate=pl.CostEstimate(
+            flops=4 * length * BLOCK * count * total, bytes_accessed=250 << 20, transcendentals=0
+        ),
+        name="weight_gradients",
+    )(*inputs, *cotans, *order, *parts, *raws, cols, staps, sbias, pack)
+
+
+def rows_kernel(
+    sum0, sum1, low_ref, state_w, rows_ref, cot_ref, gain_ref, made0, made1, scale_ref,
+    hidden_out, block_out, gain_out,
+):
+    step = pl.program_id(0)
+    half = pl.num_programs(0) // 2
+    gain = gain_ref[...]
+
+    def work(summed, made):
+        grad = summed[...].astype(F32) + mm_nt(low_ref[0], state_w[...])
+        rows = rows_ref[0].astype(F32)
+        inv_root = lax.rsqrt(jnp.mean(rows * rows, axis=1, keepdims=True) + EPSILON)
+        part = jnp.sum(grad * (rows * inv_root), axis=0, keepdims=True)
+        normed = grad * gain
+        inner = jnp.mean(normed * rows, axis=1, keepdims=True)
+        back = inv_root * normed - rows * (inv_root * inv_root * inv_root * inner)
+        hidden_out[0] = (cot_ref[0].astype(F32) + back).astype(BF16)
+        block_out[0] = (rows + made[...] * scale_ref[0][:, 0:1]).astype(BF16)
+        width = gain_out.shape[1]
+        for at in range(gain_out.shape[0]):
+            piece = part[:, at * width : (at + 1) * width]
+
+            @pl.when(step == 0)
+            def _():
+                gain_out[at : at + 1, :] = piece
+
+            @pl.when(step > 0)
+            def _():
+                gain_out[at : at + 1, :] += piece
+
+    @pl.when(step < half)
+    def _():
+        work(sum0, made0)
+
+    @pl.when(step >= half)
+    def _():
+        work(sum1, made1)
+
+
+def rows_call(sums, lows, state_w, rows, cotan, gain, made, scales):
+    micro, length, model = rows.shape
+    tiles = 2
+    tile = length // tiles
+    both = lambda width: pl.BlockSpec((1, tile, width), lambda i: (i // tiles, i % tiles, 0))
+    former = pl.BlockSpec((tile, model), lambda i: (jnp.minimum(i, tiles - 1), 0))
+    latter = pl.BlockSpec((tile, model), lambda i: (jnp.maximum(i - tiles, 0), 0))
+    full = lambda dims: pl.BlockSpec(dims, lambda i: (0, 0))
+    return pl.pallas_call(
+        rows_kernel,
+        grid=(micro * tiles,),
+        in_specs=[
+            former, latter, both(2 * STATE), full(state_w.shape), both(model), both(model),
+            full(gain.shape), former, latter, both(128),
+        ],
+        out_specs=[both(model), both(model), full((8, model // 8))],
+        out_shape=[shape(rows.shape, BF16), shape(rows.shape, BF16), shape((8, model // 8))],
+        compiler_params=pltpu.CompilerParams(vmem_limit_bytes=50 << 20),
+        cost_estimate=pl.CostEstimate(flops=1 << 30, bytes_accessed=18 << 20, transcendentals=0),
+        name="finish_rows",
+    )(*sums, lows, state_w, rows, cotan, gain, *made, scales)
+
+
+def gain_kernel(
+    tp_size, count, part, gain_out, line_slots, line_sum, slots, send_sem, recv_sem, far_send, far_recv,
+):
+    me, column = lax.axis_index("tp"), lax.axis_index("fsdp")
+    greet(
+        [(column, lax.rem(me + hop, tp_size)) for hop in range(1, tp_size)]
+        + [(lax.rem(column + hop, count), me) for hop in range(1, count)]
+    )
+    line_slots[me] = part[...]
+    copies = [
+        remote_copy(
+            part, line_slots.at[me], send_sem.at[hop - 1], recv_sem.at[hop - 1],
+            (column, lax.rem(me + hop, tp_size)),
+        )
+        for hop in range(1, tp_size)
+    ]
+    for copy in copies:
+        copy.start()
+    for copy in copies:
+        copy.wait()
+    total = line_slots[0]
+    for at in range(1, tp_size):
+        total = total + line_slots[at]
+    line_sum[...] = total
+    slots[column] = total
+    copies = [
+        remote_copy(
+            line_sum, slots.at[column], far_send.at[hop - 1], far_recv.at[hop - 1],
+            (lax.rem(column + hop, count), me),
+        )
+        for hop in range(1, count)
+    ]
+    for copy in copies:
+        copy.start()
+    for copy in copies:
+        copy.wait()
+    total = slots[0]
+    for at in range(1, count):
+        total = total + slots[at]
+    gain_out[...] = total
+
+
+def gain_call(tp_size, count, part):
+    vmem = pl.BlockSpec(memory_space=pltpu.VMEM)
+    return pl.pallas_call(
+        partial(gain_kernel, tp_size, count),
+        in_specs=[vmem],
+        out_specs=vmem,
+        out_shape=shape(part.shape),
+        scratch_shapes=[
+            pltpu.VMEM((tp_size,) + part.shape, F32), pltpu.VMEM(part.shape, F32),
+            pltpu.VMEM((count,) + part.shape, F32),
+            pltpu.SemaphoreType.DMA((tp_size - 1,)), pltpu.SemaphoreType.DMA((tp_size - 1,)),
+            pltpu.SemaphoreType.DMA((count - 1,)), pltpu.SemaphoreType.DMA((count - 1,)),
+        ],
+        compiler_params=pltpu.CompilerParams(
+            collective_id=7, has_side_effects=True, vmem_limit_bytes=32 << 20
+        ),
+        cost_estimate=pl.CostEstimate(flops=0, bytes_accessed=1 << 20, transcendentals=0),
+        name="gain_sum",
+    )(part)
+
+
+def unpack_kernel(heads, pack_ref, ssum_ref, rate_ref, gain, skip, conv, bias, sconv, sbias, step, decay):
+    gain[...] = pack_ref[0:1, :]
+    lanes = pack_ref.shape[1]
+    place = (iota((lanes, 128), 0) // HEAD_DIM == iota((lanes, 128), 1)).astype(F32)
+    sums = mm(pack_ref[0:8, :], place, PRECISE)
+    skip[...] = sums[1:2, :heads]
+    conv[...] = pack_ref[2 : 2 + CONV, :]
+    bias[...] = pack_ref[2 + CONV : 3 + CONV, :]
+    sconv[...] = ssum_ref[0:CONV, :]
+    sbias[...] = ssum_ref[CONV : CONV + 1, :]
+    step[...] = pack_ref[8:9, :heads]
+    decay[...] = pack_ref[9:10, :heads] * rate_ref[:, :heads]
+
+
+def unpack_call(pack, ssum, rate, heads):
+    inner = pack.shape[1]
+    vmem = pl.BlockSpec(memory_space=pltpu.VMEM)
+    dims = [(1, inner), (1, heads), (CONV, inner), (1, inner), (CONV, 2 * STATE), (1, 2 * STATE),
+            (1, heads), (1, heads)]
+    return pl.pallas_call(
+        partial(unpack_kernel, heads), in_specs=[vmem] * 3, out_specs=[vmem] * 8,
+        out_shape=[shape(each) for each in dims], name="small_gradients",
+        cost_estimate=pl.CostEstimate(flops=0, bytes_accessed=1 << 18, transcendentals=0),
+    )(pack, ssum, rate)
+
+
 def shift_down(values, offset):
     return jnp.pad(values, ((offset, 0), (0, 0)))[: values.shape[0]]
 
@@ -1183,68 +1722,69 @@
     *former, made_sum, cotan = backward(0, Hosted(tp_size, saved[1][8], cotangent[1, 0]), 4)
     produced.append(made_sum)
     cotans.append(cotan)
-    grad_bcs = [lax.psum(former[4], "tp")]
+    early = lax.psum(former[4], "tp")
     *latter, gin_sum = backward(1, Hosted(tp_size, former[5]), 5)
-    summed.append(gin_sum)
-    grad_bcs.append(lax.psum(lax.optimization_barrier((latter[4], grad_bcs[0]))[0], "tp"))
-    summed.append(scatter_tp(latter[5], grad_bcs[1]).astype(F32))
+    summed = [gin_sum, scatter_tp(latter[5])]
     lows = [[each[1], each[2], each[3], each[0]] for each in (former, latter)]
-    smalls = [(each[6], each[7]) for each in (former, latter)]
-    raws = [each[4] for each in saved]
-
-    gin_rows = []
-    for at in range(micro):
-        low_state, grad_staps, grad_sbias = state_gradient(
-            grad_bcs[at].astype(F32), raws[at], staps, sbias, columns[at]
-        )
-        mine = lax.dynamic_slice_in_dim(low_state, me * rows_here, rows_here, axis=0)
-        gin_rows.append(summed[at] + mm_nt(mine, state_w))
-        low_gate, low_value, low_step, branch = lows[at]
-        lows[at] = (low_gate, low_value, low_state, low_step, branch)
-        smalls[at] = smalls[at] + (grad_staps, grad_sbias)
-    block_rows = []
-    for at in range(micro):
-        scale = lax.dynamic_slice_in_dim(scales[at], me * rows_here, rows_here, axis=0)[:, 0:1]
-        block_rows.append((rows_float[at] + produced[at] * scale).astype(BF16))
-
-    grad_out = outer_call([low[4] for low in lows], cotans)
-    grad_gate, grad_value, grad_state, grad_step = weight_call(inputs, [low[:4] for low in lows])
-    if not aligned:
-        grad_out = jnp.transpose(grad_out.reshape(-1, fsdp_size, proj_out.shape[1]), (1, 0, 2))
-    grad_gate, grad_value, grad_state, grad_step, grad_out = scatter_call(
-        fsdp_size, (grad_gate, grad_value, grad_state, grad_step, grad_out), axes
+    parts, raws = (early, latter[4]), [each[4] for each in saved]
+    inner_here = proj_gate.shape[1]
+    pack = jnp.concatenate(
+        [former[6] + latter[6], jnp.pad(former[7] + latter[7], ((0, 0), (0, inner_here - 128)))], axis=0
     )
+    if aligned and fsdp_size == 8 and model // fsdp_size == BLOCK:
+        grad_gate, grad_value, grad_step, grad_out, grad_state, pack, state_sum, mine = tail_call(
+            fsdp_size, tp_size, inputs, cotans, lows, parts, raws, jnp.concatenate(columns, axis=0),
+            staps, sbias, pack,
+        )
+    else:
+        mine, state_sum = [], 0.0
+        for at in range(micro):
+            grad_bc = (parts[at] if at == 0 else lax.psum(parts[at], "tp")).astype(F32)
+            low_state, grad_staps, grad_sbias = state_gradient(
+                grad_bc, raws[at], staps, sbias, columns[at]
+            )
+            mine.append(lax.dynamic_slice_in_dim(low_state, me * rows_here, rows_here, axis=0))
+            lows[at].insert(2, low_state)
+            state_sum = state_sum + jnp.concatenate(
+                [grad_staps, grad_sbias[None, :], jnp.zeros((3, 2 * STATE), F32)], axis=0
+            )
+        mine = jnp.stack(mine)
+        grad_out = outer_call([low[4] for low in lows], cotans)
+        grad_gate, grad_value, grad_state, grad_step = weight_call(inputs, [low[:4] for low in lows])
+        if not aligned:
+            grad_out = jnp.transpose(grad_out.reshape(-1, fsdp_size, proj_out.shape[1]), (1, 0, 2))
+        grad_gate, grad_value, grad_state, grad_step, grad_out = scatter_call(
+            fsdp_size, (grad_gate, grad_value, grad_state, grad_step, grad_out), axes
+        )
+        pack, state_sum = lax.psum((pack, state_sum), "fsdp")
     grad_step = grad_step[:, :heads]
-
-    grad_inputs = jnp.stack(gin_rows)
-    grad_norm_gain = jnp.sum(grad_inputs * rows_float * inv_root, axis=(0, 1))
-    grad_normed = grad_inputs * norm_gain
-    grad_rows = inv_root * grad_normed - rows_float * inv_root**3 * jnp.mean(
-        grad_normed * rows_float, axis=-1, keepdims=True
+    my_scales = jnp.stack(
+        [lax.dynamic_slice_in_dim(each, me * rows_here, rows_here, axis=0) for each in scales]
     )
-    grad_hidden = (cotangent[:, 0].astype(F32) + grad_rows).astype(BF16)
-
-    small, step_sums, grad_staps, grad_sbias = (sum(parts) for parts in zip(*smalls))
-    small, step_sums, grad_staps, grad_sbias = lax.psum(
-        (small, step_sums, grad_staps, grad_sbias), "fsdp"
+    grad_hidden, block_rows, gain_part = rows_call(
+        summed, mine, state_w, hidden_in[:, 0], cotangent[:, 0], norm_gain[None, :],
+        produced, my_scales,
     )
-    gain_total = lax.psum(grad_norm_gain, ("fsdp", "tp"))
+    gain_total = gain_call(tp_size, fsdp_size, gain_part)
+    grad_gain, grad_skip, grad_conv, grad_bias, grad_sconv, grad_sbias, grad_in, grad_decay = (
+        unpack_call(pack, state_sum, rate, heads)
+    )
     return (
-        jnp.stack(block_rows)[:, None],
+        block_rows[:, None],
         grad_hidden[:, None],
-        gain_total,
+        gain_total.reshape(-1),
         grad_gate,
         grad_value,
         grad_state,
         grad_step,
-        small[2 : 2 + CONV],
-        small[2 + CONV],
-        grad_staps,
-        grad_sbias,
-        step_sums[0, :heads],
-        step_sums[1, :heads] * decay_rate,
-        jnp.sum(small[1].reshape(heads, HEAD_DIM), axis=1),
-        small[0],
+        grad_conv,
+        grad_bias.reshape(-1),
+        grad_sconv,
+        grad_sbias.reshape(-1),
+        grad_in.reshape(-1),
+        grad_decay.reshape(-1),
+        grad_skip.reshape(-1),
+        grad_gain.reshape(-1),
         grad_out,
     )
 

time: 786 us -> 647 us (0.82)
  blocking collectives: 63.8 us -> 0 us
  waiting for transfers between devices: 62.3 us -> 21.4 us
  other arithmetic: 25.4 us -> 5.84 us
    psum x2 -> x0, blocking collectives: 63.8 us -> none  [the longest x1 39.2 us: local(): gain_total = lax.psum(grad_norm_gain, ('fsdp', 'tp'))]
    psum x2 -> x1, waiting for transfers between devices: 42 us -> 0.02 us  [local(): early = lax.psum(former[4], 'tp')]
    pallas_call x3 -> x4, Pallas kernels: 126 us -> 114 us  [the longest x1 93.9 us: tail_call(): pl.pallas_call(partial(tail_kernel, chips, tp_size, micro, widths), grid=...]
    convert_element_type x3 -> x0, other arithmetic: 8.99 us -> none  [the longest x1 5.09 us: local(): grad_hidden = (cotangent[:, 0].astype(F32) + grad_rows).astype(BF16)]
  transfers between devices with their start and end apart: 5 -> 4, of which waited for: 2 -> 1; matrix products, arithmetic and copies ran while one was open for 4% -> 2% of each run, Pallas kernels for 46% -> 52%
where the time goes in v3:
time: 647 us; the launch traced here: 644 us
  Pallas kernels  578 us (89%)
  local copies, waits for them, and re-layouts  23.5 us (4%)
  waiting for transfers between devices  21.4 us (3%)
  between operations  14.3 us (2%)
    pallas_call x2, Pallas kernels, backward_call(): pl.pallas_call(hosted.wrap(backward_kernel, BACKWARD_INS, BACKWARD_OUTS,...  186 us
    pallas_call x2, Pallas kernels, forward_call(): pl.pallas_call(hosted.wrap(forward_kernel, FORWARD_INS, FORWARD_OUTS, pac...  161 us
    pallas_call x1, Pallas kernels, tail_call(): pl.pallas_call(partial(tail_kernel, chips, tp_size, micro, widths), grid=...  93.9 us
    pallas_call x1, Pallas kernels, gather_call(): pl.pallas_call(partial(gather_kernel, count, pieces), in_specs=[pl.BlockS...  84.4 us
    pallas_call x2, Pallas kernels, branch_call(): pl.pallas_call(partial(branch_kernel, tp_size, inner * tp_size), grid=(gr...  32.8 us
    all_gather x2, waiting for transfers between devices, gather_tp(): return lax.all_gather(values, 'tp', axis=0, tiled=True)  21.3 us
  transfers between devices with their start and end apart: 4, of which 1 were waited for; matrix products, arithmetic and copies ran while one was open for 2% of the time, Pallas kernels for 52%

profile of v3, /device:TPU:0, one launch (start us, length us, event | category | flops | bytes accessed | tf_op | source)
XLA Modules:
  0.0 643.5 jit_solution(14967072757642412809)
XLA Ops:
  7.2 0.0 all-gather.3.cloned.1.call-start
  7.2 2.1 fusion
  9.3 2.1 fusion.2
  11.5 1.5 slice_bitcast_fusion
  13.0 0.0 all-gather.5.cloned.1.call-start
  13.0 0.1 copy.77
  13.2 0.6 pad.57.refs_3_
  13.8 84.4 %gather_weights.1 = (bf16[2048,1024]{1,0:T(8,128)(2,1)}, bf16[2048,1024]{1,0:T(8,128)(2,1)}, bf16[2048,256]{1,0:T(8,128)(2,1)}, bf16[2048,128]{1,0:T(8,128)(2,1)}, bf16[1024,2048]{1,0:T(8,128)(2,1)}) custom-call(bf16[256,1024]{1,0:T(8,128)(2,1)} %refs_0_.1, bf16[256,1024]{1,0:T(8,128)(2,1)} %refs_1_.1, bf16[256,256]{1,0:T(8,128)(2,1)} %refs_2_.1, ...), custom_call_target="tpu_custom_call" | custom-call | bytes 262144000 | tf_op jit(solution)/shard_map/gather_weights/pallas_call | solution.py:900
  98.3 0.0 all-gather.3.cloned.1.call-done.in_ref.refs_0_
  98.3 0.0 all-gather.5.cloned.1.call-update
  98.3 0.0 all-reduce.18.cloned.1.call-start
  98.4 0.6 convert_bitcast_fusion
  99.0 0.1 slice.89
  99.1 0.1 slice.90
  99.2 0.1 slice.80
  99.3 0.1 slice.81
  99.3 0.1 pad_add_fusion
  99.4 0.1 broadcast_bitcast_fusion.2
  99.5 0.1 broadcast_bitcast_fusion.5
  99.6 0.1 broadcast_bitcast_fusion.1
  99.7 0.1 broadcast_bitcast_fusion.4
  99.7 0.1 compare_convert_fusion.4
  99.8 0.1 broadcast_bitcast_fusion
  99.9 0.1 fusion.15
  100.0 0.1 stack.132
  100.1 1.0 copy.78.cols_ref.refs_18_
  101.2 0.1 broadcast_in_dim.53
  101.2 0.7 broadcast_in_dim_reshape.3.skip_ref.refs_11_.refs_16_
  101.9 0.1 broadcast_bitcast_fusion.3
  102.0 0.1 fusion.21
  102.1 0.1 stack.119
  102.2 1.0 copy.79.refs_12_.refs_18_
  103.2 0.5 pad_bitcast_fusion
  103.8 1.5 slice_bitcast_fusion.2
  105.2 53.3 %ssd_forward.2 = (bf16[1024,1024]{1,0:T(8,128)(2,1)}, f32[1024,1024]{1,0:T(8,128)}, f32[1024,1024]{1,0:T(8,128)}, bf16[1024,256]{1,0:T(8,128)(2,1)}, f32[1024,25...) custom-call(bf16[1024,2048]{1,0:T(8,128)(2,1)} %all-gather.3.cloned., ...), custom_call_target="tpu_custom_call" | custom-call | flops 15032385536 | bytes 41943040 | tf_op jit(solution)/shard_map/ssd_forward/pallas_call | solution.py:679
  158.5 21.3 %all-gather.5.cloned.1.call-done.refs_0_.refs_1_ = bf16[1024,2048]{1,0:T(8,128)(2,1)} async-done(((bf16[256,2048]{1,0:T(8,128)(2,1)}), bf16[1024,2048]{1,0:T(8,128)(2,1)}) %all-gather.5.cloned.1.call-update) | async-done | bytes 4194320 | tf_op jit(solution)/shard_map/all_gather | solution.py:1679
  179.8 108.0 %ssd_forward.3 = (bf16[1024,1024]{1,0:T(8,128)(2,1)}, f32[1024,1024]{1,0:T(8,128)}, f32[1024,1024]{1,0:T(8,128)}, bf16[1024,256]{1,0:T(8,128)(2,1)}, f32[1024,25...) custom-call(bf16[1024,2048]{1,0:T(8,128)(2,1)} %all-gather.5.cloned., ...), custom_call_target="tpu_custom_call" | custom-call | flops 15032385536 | bytes 41943040 | tf_op jit(solution)/shard_map/ssd_forward/pallas_call | solution.py:679
  287.8 15.5 %branch_gradient.2 = (bf16[1024,1024]{1,0:T(8,128)(2,1)S(1)}, f32[1024,128]{1,0:T(8,128)S(1)}) custom-call(bf16[1024,2048]{1,0:T(8,128)(2,1)} %get-tuple-element.97.cot_ref.refs_2_, bf16[1024,2048]{1,0:T(8,128)(2,1)} %get-tuple-element.89.out_w.refs_14_, bf16[1024,1024]{1,0:T(8,128)(2,1)} %get-tuple-element.94.gate_ref.refs_0_, ...), custom_call_target="tpu_custom_call" | custom-call | flops 4294967296 | bytes 20971520 | tf_op jit(solution)/shard_map/branch_gradient/pallas_call | solution.py:729
  303.3 0.8 copy-done.3
  304.1 1.3 copy-done.9
  305.4 100.6 %ssd_backward.2 = (bf16[1024,1024]{1,0:T(8,128)(2,1)}, bf16[1024,1024]{1,0:T(8,128)(2,1)}, bf16[1024,1024]{1,0:T(8,128)(2,1)}, bf16[1024,128]{1,0:T(8,128)(2,1)}...) custom-call(bf16[1024,1024]{1,0:T(8,128)(2,1)} %get-tuple-element.94, ...), custom_call_target="tpu_custom_call" | custom-call | flops 12884901888 | bytes 62914560 | tf_op jit(solution)/shard_map/ssd_backward/pallas_call | solution.py:771
  406.1 0.0 all-reduce.18.cloned.1.call-update
  406.1 0.0 reduce-scatter.2.cloned.1.call-start
  406.1 17.3 %branch_gradient.3 = (bf16[1024,1024]{1,0:T(8,128)(2,1)S(1)}, f32[1024,128]{1,0:T(8,128)S(1)}) custom-call(bf16[1024,2048]{1,0:T(8,128)(2,1)} %get-tuple-element.105.cot_ref.refs_3_, bf16[1024,2048]{1,0:T(8,128)(2,1)} %get-tuple-element.89.out_w.refs_14_, bf16[1024,1024]{1,0:T(8,128)(2,1)} %get-tuple-element.91.gate_ref.refs_0_, ...), custom_call_target="tpu_custom_call" | custom-call | flops 4294967296 | bytes 20971520 | tf_op jit(solution)/shard_map/branch_gradient/pallas_call | solution.py:729
  423.5 0.8 copy-done.4
  424.2 1.3 copy-done.8
  425.6 85.1 %ssd_backward.3 = (bf16[1024,1024]{1,0:T(8,128)(2,1)}, bf16[1024,1024]{1,0:T(8,128)(2,1)}, bf16[1024,1024]{1,0:T(8,128)(2,1)}, bf16[1024,128]{1,0:T(8,128)(2,1)}...) custom-call(bf16[1024,1024]{1,0:T(8,128)(2,1)} %get-tuple-element.91, ...), custom_call_target="tpu_custom_call" | custom-call | flops 12884901888 | bytes 62914560 | tf_op jit(solution)/shard_map/ssd_backward/pallas_call | solution.py:771
  510.8 1.3 copy.82.refs_16_
  512.1 0.6 select_maximum_fusion.refs_19_
  512.8 0.9 dynamic-slice_bitcast_fusion
  513.7 0.9 dynamic-slice_bitcast_fusion.1
  514.6 0.0 all-reduce.18.cloned.1.call-done.refs_12_
  514.7 93.9 %weight_gradients.1 = (f32[256,1024]{1,0:T(8,128)}, f32[256,1024]{1,0:T(8,128)}, f32[256,128]{1,0:T(8,128)}, f32[1024,256]{1,0:T(8,128)}, f32[256,256]{1,0:T(8,1...) custom-call(bf16[1024,2048]{1,0:T(8,128)(2,1)} %all-gather.3.cloned.1.call-done.in_ref.refs_0_, ...), custom_call_target="tpu_custom_call" | custom-call | flops 26843545600 | bytes 262144000 | tf_op jit(solution)/shard_map/weight_gradients/pallas_call | solution.py:1408
  608.6 1.6 copy.85
  610.2 1.8 small_gradients.1
  612.0 1.2 copy-done.1
  613.3 0.9 copy-done.2
  614.2 8.1 %finish_rows.1 = (bf16[2,256,2048]{2,1,0:T(8,128)(2,1)}, bf16[2,256,2048]{2,1,0:T(8,128)(2,1)}, f32[8,256]{1,0:T(8,128)S(1)}) custom-call(f32[256,2048]{1,0:T(8,128)} %get-tuple-element.113.sum0, bf16[256,2048]{1,0:T(8,128)(2,1)S(1)} %copy-done.1, bf16[2,256,256]{2,1,0:T(8,128)(2,1)S(1)} %copy-done.2, bf16[2048,256]{1,0:T(8,128)(2,1)S(1)} %copy-done, ...), custom_call_target="tpu_custom_call" | custom-call | flops 1073741824 | bytes 18874368 | tf_op jit(solution)/shard_map/finish_rows/pallas_call | solution.py:1507
  622.3 10.3 %gain_sum.1 = f32[8,256]{1,0:T(8,128)S(1)} custom-call(f32[8,256]{1,0:T(8,128)S(1)} %get-tuple-element.136.part), custom_call_target="tpu_custom_call" | custom-call | bytes 1048576 | tf_op jit(solution)/shard_map/gain_sum/pallas_call | solution.py:1566
  632.6 0.6 copy.92
  633.2 1.0 copy.98
  634.2 1.0 copy.99
  635.1 0.7 copy.100
  635.8 1.0 copy.101
  (58 shorter events, 0.2 us)
Async XLA Ops:
  7.2 2.1 copy-start.5
  7.2 91.1 %all-gather.3.cloned.1.call-start = ((), (), s32[]{:S(2)}) async-start(), calls=%async_computation.1 | async-start | bytes 5242880 | tf_op jit(solution)/shard_map/all_gather | solution.py:1679
  11.5 1.6 copy-start.18
  12.9 85.4 %copy-start.17 = (s32[2,1,1024]{2,1,0:T(1,128)S(1)}, s32[2,1,1024]{2,1,0:T(1,128)}, u32[]{:S(2)}) copy-start(s32[2,1,1024]{2,1,0:T(1,128)} %param.18) | copy-start | bytes 24580
  13.0 88.2 %copy-start.21 = (f32[16]{0:T(128)S(1)}, f32[16]{0:T(128)}, u32[]{:S(2)}) copy-start(f32[16]{0:T(128)} %param.31) | copy-start | bytes 196
  13.0 166.8 %all-gather.5.cloned.1.call-start = ((), (), s32[]{:S(2)}) async-start(), calls=%async_computation.2 | async-start | bytes 5242880 | tf_op jit(solution)/shard_map/all_gather | solution.py:1679
  13.8 89.4 %copy-start.23 = (f32[16]{0:T(128)S(1)}, f32[16]{0:T(128)}, u32[]{:S(2)}) copy-start(f32[16]{0:T(128)} %param.30) | copy-start | bytes 196
  13.8 89.4 %copy-start.22 = (f32[16]{0:T(128)S(1)}, f32[16]{0:T(128)}, u32[]{:S(2)}) copy-start(f32[16]{0:T(128)} %param.29) | copy-start | bytes 196
  13.8 90.0 %copy-start.10 = (bf16[2,1,256,2048]{3,2,1,0:T(8,128)(2,1)S(1)}, bf16[2,1,256,2048]{3,2,1,0:T(8,128)(2,1)}, u32[]{:S(2)}) copy-start(bf16[2,1,256,2048]{3,2,1,0:T(8,128)(2,1)} %param.19) | copy-start | bytes 6291460
  98.3 416.4 %all-reduce.18.cloned.1.call-start = ((), (), s32[]{:S(2)}) async-start(), calls=%async_computation.4 | async-start | bytes 1048576 | tf_op jit(solution)/shard_map/psum | solution.py:1725
  179.8 108.0 %copy-start.6 = (f32[1024]{0:T(1024)S(1)}, f32[1024]{0:T(1024)}, u32[]{:S(2)}) copy-start(f32[1024]{0:T(1024)} %param.32) | copy-start | bytes 12292
  303.3 0.8 copy-start.3
  304.1 1.3 copy-start.9
  305.4 100.7 %copy-start.7 = (f32[1024]{0:T(1024)S(1)}, f32[1024]{0:T(1024)}, u32[]{:S(2)}) copy-start(f32[1024]{0:T(1024)} %param.32) | copy-start | bytes 12292
  406.1 205.9 %reduce-scatter.2.cloned.1.call-start = ((), (), s32[]{:S(2)}) async-start(), calls=%async_computation.3 | async-start | bytes 5242880 | tf_op jit(solution)/shard_map/reduce_scatter | solution.py:1683
  423.4 0.8 copy-start.4
  424.2 1.3 copy-start.8
  510.7 1.4 copy-start.15
  510.7 1.4 copy-start.16
  510.7 1.4 copy-start.19
  510.7 1.4 copy-start.20
  514.7 97.3 %copy-start = (bf16[2048,256]{1,0:T(8,128)(2,1)S(1)}, bf16[2048,256]{1,0:T(8,128)(2,1)}, u32[]{:S(2)}) copy-start(bf16[2048,256]{1,0:T(8,128)(2,1)} %get-tuple-element.88.state_w.refs_3_) | copy-start | bytes 3145732
  612.0 1.2 copy-start.1
  613.3 0.9 copy-start.2
  614.2 19.0 %copy-start.13 = (f32[256,1024]{1,0:T(8,128)S(1)}, f32[256,1024]{1,0:T(8,128)}, u32[]{:S(2)}) copy-start(f32[256,1024]{1,0:T(8,128)} %get-tuple-element.251) | copy-start | bytes 3145732
  622.3 11.8 %copy-start.12 = (f32[256,1024]{1,0:T(8,128)S(1)}, f32[256,1024]{1,0:T(8,128)}, u32[]{:S(2)}) copy-start(f32[256,1024]{1,0:T(8,128)} %get-tuple-element.252) | copy-start | bytes 3145732
  633.2 1.9 copy-start.14
  633.2 2.7 copy-start.11
Sparse Core Ops, SparseCore 0:
  13.1 83.4 all-gather.2
  98.7 81.0 all-gather.4
  406.2 42.5 all-reduce.17
  510.9 94.9 reduce-scatter.1

commit v4 on v3

--- a/solution.py
+++ b/solution.py
@@ -18,8 +18,9 @@
 INNER = 4096
 EPSILON = 1e-05
 PRECISE = lax.Precision.HIGHEST
+PARTS = 2
 FORWARD_INS, FORWARD_OUTS = 16, 9
-BACKWARD_INS, BACKWARD_OUTS = 20, 8
+BACKWARD_INS, BACKWARD_OUTS = 23, 9
 F32 = jnp.float32
 BF16 = jnp.bfloat16
 
@@ -128,12 +129,16 @@
         return [
             pltpu.VMEM((2, hops, rows, width), BF16), pltpu.VMEM((2, hops, rows, width), BF16),
             pltpu.VMEM((rows, width), BF16), pltpu.SemaphoreType.DMA((2, hops)),
-            pltpu.SemaphoreType.DMA((2, hops)), pltpu.SemaphoreType.DMA((2, hops)),
+            pltpu.SemaphoreType.DMA((2, hops, PARTS)), pltpu.SemaphoreType.DMA((2, hops, PARTS)),
             pltpu.SemaphoreType.DMA((1,)),
         ]
 
     def place(self, flow):
         return self.me if flow == 0 else self.size - 1 - self.me
+
+    def part(self, part):
+        rows = self.rows // PARTS
+        return pl.ds(part * rows, rows)
 
     def local(self, flow, hop):
         block = self.size - 1 - hop + self.place(flow)
@@ -150,12 +155,13 @@
             self.source.at[pl.ds(at, self.rows), :], self.last, self.last_sem.at[0]
         )
 
-    def sending(self, flow, hop):
+    def sending(self, flow, hop, part):
         neighbour = self.me + 1 if flow == 0 else self.me - 1
         neighbour = jnp.clip(neighbour, 0, self.size - 1)
         return remote_copy(
-            self.own.at[flow, hop], self.slots.at[flow, hop], self.send_sem.at[flow, hop],
-            self.recv_sem.at[flow, hop], (self.column, neighbour),
+            self.own.at[flow, hop, self.part(part), :], self.slots.at[flow, hop, self.part(part), :],
+            self.send_sem.at[flow, hop, part], self.recv_sem.at[flow, hop, part],
+            (self.column, neighbour),
         )
 
     def begin(self):
@@ -167,40 +173,45 @@
                 def _():
                     self.local(flow, hop).start()
 
-    def hop(self, hop):
+    def hop(self, hop, part):
+        rows = self.part(part)
         for flow in range(2):
             place = self.place(flow)
 
             @pl.when(place <= hop)
             def _():
-                self.local(flow, hop).wait()
+                if part == 0:
+                    self.local(flow, hop).wait()
                 if hop > 0:
 
                     @pl.when(place >= 1)
                     def _():
-                        self.sending(flow, hop - 1).wait_recv()
-                        total = self.own[flow, hop].astype(F32) + self.slots[flow, hop - 1].astype(F32)
-                        self.own[flow, hop] = total.astype(BF16)
-
-                self.sending(flow, hop).start()
-
-    def end(self, out):
+                        self.sending(flow, hop - 1, part).wait_recv()
+                        total = self.own[flow, hop, rows, :].astype(F32)
+                        total = total + self.slots[flow, hop - 1, rows, :].astype(F32)
+                        self.own[flow, hop, rows, :] = total.astype(BF16)
+
+                self.sending(flow, hop, part).start()
+
+    def end(self, out, part):
         hops = self.size - 1
-        self.final().wait()
-        out[...] = self.last[...].astype(F32)
+        rows = self.part(part)
+        if part == 0:
+            self.final().wait()
+        out[rows, :] = self.last[rows, :].astype(F32)
         for flow in range(2):
 
             @pl.when(self.place(flow) >= 1)
             def _():
-                self.sending(flow, hops - 1).wait_recv()
-                out[...] += self.slots[flow, hops - 1].astype(F32)
+                self.sending(flow, hops - 1, part).wait_recv()
+                out[rows, :] += self.slots[flow, hops - 1, rows, :].astype(F32)
 
         for hop in range(hops):
             for flow in range(2):
 
                 @pl.when(self.place(flow) <= hop)
                 def _():
-                    self.sending(flow, hop).wait_send()
+                    self.sending(flow, hop, part).wait_send()
 
 
 class LineGather:
@@ -213,8 +224,8 @@
     @staticmethod
     def scratch(size):
         return [
-            pltpu.SemaphoreType.DMA((1,)), pltpu.SemaphoreType.DMA((2, size - 1)),
-            pltpu.SemaphoreType.DMA((2, size - 1)),
+            pltpu.SemaphoreType.DMA((1,)), pltpu.SemaphoreType.DMA((2, size - 1, PARTS)),
+            pltpu.SemaphoreType.DMA((2, size - 1, PARTS)),
         ]
 
     def place(self, flow):
@@ -224,71 +235,71 @@
         at = pl.multiple_of(jnp.clip(at, 0, self.size - 1) * self.rows, self.rows)
         return self.target.at[pl.ds(at, self.rows), :]
 
-    def sending(self, flow, hop):
+    def sending(self, flow, hop, part):
         neighbour = self.me + 1 if flow == 0 else self.me - 1
         neighbour = jnp.clip(neighbour, 0, self.size - 1)
-        block = self.block(self.me - hop if flow == 0 else self.me + hop)
+        rows = pl.ds(part * (self.rows // PARTS), self.rows // PARTS)
+        block = self.block(self.me - hop if flow == 0 else self.me + hop).at[rows, :]
         return remote_copy(
-            self.source if hop == 0 else block, block, self.send_sem.at[flow, hop],
-            self.recv_sem.at[flow, hop], (self.column, neighbour),
+            self.source.at[rows, :] if hop == 0 else block, block, self.send_sem.at[flow, hop, part],
+            self.recv_sem.at[flow, hop, part], (self.column, neighbour),
         )
 
     def local(self):
         return pltpu.make_async_copy(self.source, self.block(self.me), self.own_sem.at[0])
 
-    def begin(self):
-        self.local().start()
-        self.hop(0)
-
-    def hop(self, hop):
+    def hop(self, hop, part):
+        if hop == 0 and part == 0:
+            self.local().start()
         for flow in range(2):
             place = self.place(flow)
             if hop > 0:
 
                 @pl.when(place >= hop)
                 def _():
-                    self.sending(flow, hop - 1).wait_recv()
+                    self.sending(flow, hop - 1, part).wait_recv()
 
             if hop < self.size - 1:
 
                 @pl.when((place >= hop) & (place < self.size - 1))
                 def _():
-                    self.sending(flow, hop).start()
-
-    def end(self):
-        self.hop(self.size - 1)
-        self.local().wait()
+                    self.sending(flow, hop, part).start()
+
+    def end(self, part):
+        self.hop(self.size - 1, part)
+        if part == 0:
+            self.local().wait()
         for hop in range(self.size - 1):
             for flow in range(2):
                 place = self.place(flow)
 
                 @pl.when((place >= hop) & (place < self.size - 1))
                 def _():
-                    self.sending(flow, hop).wait_send()
+                    self.sending(flow, hop, part).wait_send()
 
 
 def run_line(step, steps, scatter, gather, out):
     size = (scatter or gather).size
-    actions = [[] for _ in range(size + 1)]
+    first = 1 if scatter and gather else 0
+    actions = [[] for _ in range(PARTS * (size + first))]
+    for part in range(PARTS):
+        if gather:
+            for hop in range(size - 1):
+                actions[PARTS * hop + part].append(partial(gather.hop, hop, part))
+            actions[PARTS * (size - 1) + part].append(partial(gather.end, part))
+        if scatter:
+            for hop in range(size - 1):
+                actions[PARTS * (first + hop) + part].append(partial(scatter.hop, hop, part))
+            actions[PARTS * (first + size - 1) + part].append(partial(scatter.end, out, part))
     if scatter:
-        first = 1 if gather else 0
-        actions[0].append(scatter.begin)
-        for hop in range(size - 1):
-            actions[first + hop].append(partial(scatter.hop, hop))
-        actions[first + size - 1].append(partial(scatter.end, out))
-    if gather:
-        actions[0].append(gather.begin)
-        for hop in range(1, size - 1):
-            actions[hop].insert(0, partial(gather.hop, hop))
-        actions[size - 1].insert(0, gather.end)
-    actions = [todo for todo in actions if todo]
-    for at, todo in zip(steps, actions):
-        if todo:
-
-            @pl.when(step == at)
-            def _():
-                for action in todo:
-                    action()
+        actions[0].insert(0, scatter.begin)
+    for at in sorted(set(steps)):
+        todo = [action for when, each in zip(steps, actions) if when == at for action in each]
+
+        @pl.when(step == at)
+        def _():
+            for action in todo:
+                action()
 
 
 class Hosted:
@@ -443,29 +454,60 @@
         made_out[...] = made[...].astype(BF16)
 
 
-def branch_kernel(
-    tp_size, total_inner, cot_ref, out_w, gate_ref, mixed_ref, gain_ref,
-    grad_out, stats_out, sums_s, slots, turn_s, send_sem, recv_sem,
+def backward_kernel(
+    tp_size, cot_ref, out_w, gate_rows, mixed_rows, gain_row,
+    gate_ref, value_ref, before_ref, mixed_ref, bc_ref, stepin_ref, cums_ref, held_ref,
+    gate_w, value_w, step_w, taps_ref, bias_ref, rate_ref, skip_ref, gain_ref, cols_ref, seg_ref,
+    branch_out, lowgate_out, lowvalue_out, lowstep_out, gbc_out, gin_out, small_out, sums_out, stats_out,
+    vbuf, gcbuf, gram_s, dgram, b_s, c_t, step_s, ent_s, fade_s, cums_s, cums_t, keep_s, grad_state,
+    gin, gb_s, gc_s, u_s, v_s, fin_s, small_s, sums_s,
+    branch_s, rowsum_s, slots_s, turn_s, swap_send, swap_recv,
 ):
-    step, groups = pl.program_id(0), pl.num_programs(0)
+    g, j = pl.program_id(0) - 1, pl.program_id(1)
+    groups, blocks = pl.num_programs(0) - 1, pl.num_programs(1)
+
+    @pl.when(g < 0)
+    def _():
+        row_sums(
+            tp_size, cot_ref, out_w, gate_rows, mixed_rows, gain_row,
+            branch_s, rowsum_s, slots_s, turn_s, swap_send, swap_recv, stats_out,
+        )
+
+    @pl.when(g >= 0)
+    def _():
+        backward_step(
+            g, j, groups, blocks, gate_ref, value_ref, before_ref, mixed_ref,
+            bc_ref, stepin_ref, cums_ref, held_ref,
+            gate_w, value_w, step_w, taps_ref, bias_ref, rate_ref, skip_ref, gain_ref, cols_ref, seg_ref,
+            branch_out, lowgate_out, lowvalue_out, lowstep_out, gbc_out, gin_out, small_out, sums_out,
+            vbuf, gcbuf, gram_s, dgram, b_s, c_t, step_s, ent_s, fade_s, cums_s, cums_t, keep_s,
+            grad_state, gin, gb_s, gc_s, u_s, v_s, fin_s, small_s, sums_s, branch_s, stats_out,
+        )
+
+
+def row_sums(
+    tp_size, cot_ref, out_w, gate_rows, mixed_rows, gain_row,
+    branch_s, rowsum_s, slots_s, turn_s, swap_send, swap_recv, stats_out,
+):
+    step, groups = pl.program_id(1), pl.num_programs(1)
     me, column = lax.axis_index("tp"), lax.axis_index("fsdp")
+    total_inner = gain_row.shape[1] * tp_size
     grad = mm_nt(cot_ref[...], out_w[...])
-    grad_out[...] = grad.astype(BF16)
-    gate = gate_ref[...].astype(F32)
-    gated = mixed_ref[...] * (gate * jax.nn.sigmoid(gate))
+    branch_s[step] = grad.astype(BF16)
+    gate = gate_rows[...].astype(F32)
+    gated = mixed_rows[...] * (gate * jax.nn.sigmoid(gate))
     squares = jnp.sum(gated * gated, axis=1, keepdims=True)
-    inner = jnp.sum(grad * gain_ref[...] * gated, axis=1, keepdims=True)
+    inner = jnp.sum(grad * gain_row[...] * gated, axis=1, keepdims=True)
     lane = iota((GROUP, 128), 1)
     both = jnp.where(lane == 0, squares, jnp.where(lane == 1, inner, 0.0))
-    sums_s[step] = jnp.transpose(both)[:8]
+    rowsum_s[step] = jnp.transpose(both)[:8]
 
     @pl.when(step == groups - 1)
     def _():
-        greet([(column, lax.rem(me + hop, tp_size)) for hop in range(1, tp_size)])
-        slots[me] = sums_s[...]
+        slots_s[me] = rowsum_s[...]
         copies = [
             remote_copy(
-                sums_s, slots.at[me], send_sem.at[hop - 1], recv_sem.at[hop - 1],
+                rowsum_s, slots_s.at[me], swap_send.at[hop - 1], swap_recv.at[hop - 1],
                 (column, lax.rem(me + hop, tp_size)),
             )
             for hop in range(1, tp_size)
@@ -474,9 +516,9 @@
             copy.start()
         for copy in copies:
             copy.wait()
-        total = slots[0]
+        total = slots_s[0]
         for at in range(1, tp_size):
-            total = total + slots[at]
+            total = total + slots_s[at]
         turn_s[...] = jnp.zeros(turn_s.shape, F32)
         scale = lax.rsqrt(total[:, 0:1, :] / total_inner + EPSILON)
         turn_s[:, 0:1, :] = scale
@@ -485,16 +527,15 @@
             stats_out[group * GROUP : (group + 1) * GROUP, :] = jnp.transpose(turn_s[group])
 
 
-def backward_kernel(
-    gate_ref, value_ref, before_ref, mixed_ref, grad_ref, bc_ref, stepin_ref, cums_ref, held_ref,
-    stats_ref, gate_w, value_w, step_w, taps_ref, bias_ref, rate_ref, skip_ref, gain_ref,
-    cols_ref, seg_ref,
+def backward_step(
+    g, j, groups, blocks, gate_ref, value_ref, before_ref, mixed_ref,
+    bc_ref, stepin_ref, cums_ref, held_ref,
+    gate_w, value_w, step_w, taps_ref, bias_ref, rate_ref, skip_ref, gain_ref, cols_ref, seg_ref,
     branch_out, lowgate_out, lowvalue_out, lowstep_out, gbc_out, gin_out, small_out, sums_out,
-    vbuf, gcbuf, gram_s, dgram, b_s, c_t, step_s, ent_s, fade_s, cums_s, cums_t, keep_s, grad_state,
-    gin, gb_s, gc_s, u_s, v_s, fin_s, small_s, sums_s,
+    vbuf, gcbuf, gram_s, dgram, b_s, c_t, step_s, ent_s, fade_s, cums_s, cums_t, keep_s,
+    grad_state, gin, gb_s, gc_s, u_s, v_s, fin_s, small_s, sums_s, branch_s, stats_ref,
 ):
-    g, j = pl.program_id(0), pl.program_id(1)
-    groups, blocks = pl.num_programs(0), pl.num_programs(1)
+    group = groups - 1 - g
     nblocks = grad_state.shape[0]
     cols = cols_ref[...]
     at_row, at_col = iota((GROUP, GROUP), 0), iota((GROUP, GROUP), 1)
@@ -531,10 +572,11 @@
         fin_s[...] = jnp.zeros(fin_s.shape, F32)
 
     at = pl.multiple_of(j * BLOCK, BLOCK)
-    gate, mixed, grad = gate_ref[...].astype(F32), mixed_ref[...], grad_ref[...].astype(F32)
+    gate, mixed = gate_ref[...].astype(F32), mixed_ref[...]
+    grad = branch_s[group, :, pl.ds(at, BLOCK)].astype(F32)
     gain, skip, taps = gain_ref[...], skip_ref[...], taps_ref[...]
-    scale = stats_ref[:, 0:1]
-    inner = stats_ref[:, 1:2]
+    stats = stats_ref[pl.ds(pl.multiple_of(group * GROUP, GROUP), GROUP), :]
+    scale, inner = stats[:, 0:1], stats[:, 1:2]
     sig = jax.nn.sigmoid(gate)
     act = gate * sig
     gated = mixed * act
@@ -720,72 +762,46 @@
     )
 
 
-def branch_call(cotan, out_w, gate_raw, mixed, gain, tp_size):
-    length, model = cotan.shape
-    inner = out_w.shape[0]
-    groups = length // GROUP
-    rows_of = lambda width: pl.BlockSpec((GROUP, width), lambda i: (i, 0))
-    full = lambda dims, **extra: pl.BlockSpec(dims, lambda i: (0, 0), **extra)
-    return pl.pallas_call(
-        partial(branch_kernel, tp_size, inner * tp_size),
-        grid=(groups,),
-        in_specs=[
-            rows_of(model), full(out_w.shape, pipeline_mode=pl.Buffered(1)),
-            rows_of(inner), rows_of(inner), full(gain.shape),
-        ],
-        out_specs=[rows_of(inner), full((length, 128))],
-        out_shape=[shape((length, inner), BF16), shape((length, 128))],
-        scratch_shapes=[
-            pltpu.VMEM((groups, 8, GROUP), F32),
-            pltpu.VMEM((tp_size, groups, 8, GROUP), F32),
-            pltpu.VMEM((groups, 128, GROUP), F32),
-            pltpu.SemaphoreType.DMA((tp_size - 1,)),
-            pltpu.SemaphoreType.DMA((tp_size - 1,)),
-        ],
-        compiler_params=pltpu.CompilerParams(
-            collective_id=3, has_side_effects=True, vmem_limit_bytes=50 << 20
-        ),
-        cost_estimate=pl.CostEstimate(
-            flops=2 * length * model * inner, bytes_accessed=20 << 20, transcendentals=0
-        ),
-        name="branch_gradient",
-    )(cotan, out_w, gate_raw, mixed, gain)
-
-
-def backward_call(saved, grad_branch, stats, weights, vectors, gain, cols, seg_line, hosted, pace, collective):
+def backward_call(saved, cotan, weights, vectors, gain, cols, seg_line, hosted, pace, collective):
     gate_raw, value_raw, mixed, bc, _, step_in, cums, held, _ = saved
-    gate_w, value_w, step_w = weights
+    gate_w, value_w, step_w, out_w = weights
     taps, bias, rate, skip = vectors
     length, inner = gate_raw.shape
-    model = gate_w.shape[0]
+    model, tp_size = gate_w.shape[0], hosted.size
     specs, shapes = hosted.outs()
     groups, blocks = length // GROUP, inner // BLOCK
+    assert groups == blocks
     last = groups - 1
-    wide = pl.BlockSpec((GROUP, BLOCK), lambda g, j: (last - g, j))
-    line = lambda rows: pl.BlockSpec((rows, BLOCK), lambda g, j: (0, j))
-    rows_of = lambda width: pl.BlockSpec((GROUP, width), lambda g, j: (last - g, 0))
+    row = lambda g: last - jnp.maximum(g - 1, 0)
+    column = lambda g, j: jnp.where(g == 0, 0, j)
+    wide = pl.BlockSpec((GROUP, BLOCK), lambda g, j: (row(g), column(g, j)))
+    line = lambda rows: pl.BlockSpec((rows, BLOCK), lambda g, j: (0, column(g, j)))
+    rows_of = lambda width: pl.BlockSpec((GROUP, width), lambda g, j: (row(g), 0))
+    first = lambda width: pl.BlockSpec((GROUP, width), lambda g, j: (jnp.where(g == 0, j, last), 0))
     steps = GROUP // HALO
     before = pl.BlockSpec(
-        (HALO, BLOCK), lambda g, j: (jnp.maximum((last - g) * steps - 1, 0), j)
+        (HALO, BLOCK), lambda g, j: (jnp.maximum(row(g) * steps - 1, 0), column(g, j))
     )
     return pl.pallas_call(
-        hosted.wrap(backward_kernel, BACKWARD_INS, BACKWARD_OUTS, pace),
-        grid=(groups, blocks),
+        hosted.wrap(partial(backward_kernel, tp_size), BACKWARD_INS, BACKWARD_OUTS, pace),
+        grid=(groups + 1, blocks),
         in_specs=[
-            wide, wide, before, wide, wide, rows_of(2 * STATE), rows_of(128), rows_of(128),
-            pl.BlockSpec((1, STATE, BLOCK), lambda g, j: (last - g, 0, j)),
-            rows_of(128), whole(gate_w), whole(value_w), whole(step_w),
+            first(model), whole(out_w), first(inner), first(inner), whole(gain),
+            wide, wide, before, wide, rows_of(2 * STATE), rows_of(128), rows_of(128),
+            pl.BlockSpec((1, STATE, BLOCK), lambda g, j: (row(g), 0, column(g, j))),
+            whole(gate_w), whole(value_w), whole(step_w),
             line(CONV), line(1), whole(rate), line(1), line(1),
-            rows_of(cols.shape[1]), pl.BlockSpec((1, GROUP), lambda g, j: (0, last - g)),
+            rows_of(cols.shape[1]), pl.BlockSpec((1, GROUP), lambda g, j: (0, row(g))),
         ] + hosted.in_specs(),
         out_specs=[
             wide, wide, wide, rows_of(128), rows_of(2 * STATE),
             rows_of(model), pl.BlockSpec((8, inner), lambda g, j: (0, 0)), pl.BlockSpec((8, 128), lambda g, j: (0, 0)),
+            pl.BlockSpec((length, 128), lambda g, j: (0, 0)),
         ] + specs,
         out_shape=[
             shape((length, inner), BF16), shape((length, inner), BF16), shape((length, inner), BF16),
             shape((length, 128), BF16), shape((length, 2 * STATE), BF16),
-            shape((length, model), BF16), shape((8, inner)), shape((8, 128)),
+            shape((length, model), BF16), shape((8, inner)), shape((8, 128)), shape((length, 128)),
         ] + shapes,
         scratch_shapes=[
             pltpu.VMEM((GROUP + HALO, BLOCK), F32),
@@ -809,6 +825,12 @@
             pltpu.VMEM((8, 128), F32),
             pltpu.VMEM((blocks, 8, BLOCK), F32),
             pltpu.VMEM((8, 128), F32),
+            pltpu.VMEM((groups, GROUP, inner), BF16),
+            pltpu.VMEM((groups, 8, GROUP), F32),
+            pltpu.VMEM((tp_size, groups, 8, GROUP), F32),
+            pltpu.VMEM((groups, 128, GROUP), F32),
+            pltpu.SemaphoreType.DMA((tp_size - 1,)),
+            pltpu.SemaphoreType.DMA((tp_size - 1,)),
         ] + hosted.scratch(),
         compiler_params=params(collective),
         cost_estimate=pl.CostEstimate(
@@ -816,7 +838,8 @@
         ),
         name="ssd_backward",
     )(
-        gate_raw, value_raw, value_raw, mixed, grad_branch, bc, step_in, cums, held, stats,
+        cotan, out_w, gate_raw, mixed, gain,
+        gate_raw, value_raw, value_raw, mixed, bc, step_in, cums, held,
         gate_w, value_w, step_w, taps, bias, rate, skip, gain, cols, seg_line, *hosted.operands(),
     )
 
@@ -1670,9 +1693,11 @@
     taps, bias = conv_value, conv_value_bias[None, :]
     staps, sbias = conv_state, conv_state_bias[None, :]
 
-    rows_float = hidden_in[:, 0].astype(F32)
-    inv_root = lax.rsqrt(jnp.mean(rows_float * rows_float, axis=-1, keepdims=True) + EPSILON)
-    input_rows = (rows_float * inv_root * norm_gain).astype(BF16)
+    input_rows = []
+    for at in range(micro):
+        rows_float = hidden_in[at, 0].astype(F32)
+        inv_root = lax.rsqrt(jnp.mean(rows_float * rows_float, axis=-1, keepdims=True) + EPSILON)
+        input_rows.append((rows_float * inv_root * norm_gain).astype(BF16))
 
     def gather_tp(values, *after):
         values = lax.optimization_barrier((values,) + after)[0]
@@ -1698,7 +1723,8 @@
     vectors = (taps, bias, staps, sbias, step_bias_line, rate, skip)
     columns = [document_columns(segment_ids[at, 0]) for at in range(micro)]
     seg_lines = [segment_ids[at, 0].astype(F32)[None, :] for at in range(micro)]
-    quick, slow = [0, 7, 15, 15, 15], [0, 5, 10, 15, 15]
+    quick = [0, 3, 7, 11, 14, 15, 15, 15, 15, 15]
+    paces = {4: [0, 3, 4, 6, 9, 12, 15, 17, 19, 19], 5: [4, 6, 9, 12, 14, 17, 19, 19]}
 
     def forward(at, hosted):
         return forward_call(
@@ -1706,12 +1732,12 @@
         )
 
     def backward(at, hosted, collective):
-        grad_branch, stats = branch_call(cotans[at], out_w, saved[at][0], saved[at][2], gain, tp_size)
-        scales.append(stats)
-        return backward_call(
-            saved[at], grad_branch, stats, (gate_w, value_w, step_w), (taps, bias, rate, skip),
-            gain, columns[at], seg_lines[at], hosted, slow, collective,
-        )
+        done = backward_call(
+            saved[at], cotans[at], (gate_w, value_w, step_w, out_w), (taps, bias, rate, skip),
+            gain, columns[at], seg_lines[at], hosted, paces[collective], collective,
+        )
+        scales.append(done[8])
+        return done
 
     scales, produced, summed = [], [], []
     saved = [forward(0, Hosted(tp_size))]

time: 647 us -> 634 us (0.980); the launches traced: 644 us -> 624 us
  Pallas kernels: 578 us -> 564 us
    pallas_call x4 -> x2, Pallas kernels: 219 us -> 206 us  [backward_call(): pl.pallas_call(hosted.wrap(partial(backward_kernel, tp_size), BACKWARD_IN...]
  transfers between devices with their start and end apart: 4 -> 4, of which waited for: 1 -> 1; matrix products, arithmetic and copies ran while one was open for 2% -> 2% of each run, Pallas kernels for 52% -> 54%
where the time goes in v4:
time: 634 us; the launch traced here: 624 us
  Pallas kernels  564 us (89%)
  waiting for transfers between devices  21.6 us (3%)
  local copies, waits for them, and re-layouts  17.8 us (3%)
  between operations  14.5 us (2%)
    pallas_call x2, Pallas kernels, backward_call(): pl.pallas_call(hosted.wrap(partial(backward_kernel, tp_size), BACKWARD_IN...  206 us
    pallas_call x2, Pallas kernels, forward_call(): pl.pallas_call(hosted.wrap(forward_kernel, FORWARD_INS, FORWARD_OUTS, pac...  158 us
    pallas_call x1, Pallas kernels, tail_call(): pl.pallas_call(partial(tail_kernel, chips, tp_size, micro, widths), grid=...  95 us
    pallas_call x1, Pallas kernels, gather_call(): pl.pallas_call(partial(gather_kernel, count, pieces), in_specs=[pl.BlockS...  84.4 us
    all_gather x2, waiting for transfers between devices, gather_tp(): return lax.all_gather(values, 'tp', axis=0, tiled=True)  21.5 us
  transfers between devices with their start and end apart: 4, of which 1 were waited for; matrix products, arithmetic and copies ran while one was open for 2% of the time, Pallas kernels for 54%

profile of v4, /device:TPU:0, one launch (start us, length us, event | category | flops | bytes accessed | tf_op | source)
XLA Modules:
  0.0 623.9 jit_solution(13383561602174713866)
XLA Ops:
  7.2 0.0 copy-start.4
  7.2 0.0 all-gather.3.cloned.1.call-start
  7.2 2.2 fusion.3
  9.4 0.0 copy-start.13
  9.5 1.9 fusion.5
  11.3 0.0 all-gather.3.cloned.1.call-update
  11.3 0.0 copy-start.16
  11.3 0.0 all-gather.5.cloned.1.call-start
  11.4 0.1 copy.77
  11.5 0.6 pad.57.refs_3_
  12.2 84.4 %gather_weights.1 = (bf16[2048,1024]{1,0:T(8,128)(2,1)}, bf16[2048,1024]{1,0:T(8,128)(2,1)}, bf16[2048,256]{1,0:T(8,128)(2,1)}, bf16[2048,128]{1,0:T(8,128)(2,1)}, bf16[1024,2048]{1,0:T(8,128)(2,1)}) custom-call(bf16[256,1024]{1,0:T(8,128)(2,1)} %refs_0_.1, bf16[256,1024]{1,0:T(8,128)(2,1)} %refs_1_.1, bf16[256,256]{1,0:T(8,128)(2,1)} %refs_2_.1, ...), custom_call_target="tpu_custom_call" | custom-call | bytes 262144000 | tf_op jit(solution)/shard_map/gather_weights/pallas_call | solution.py:923
  96.6 0.0 all-gather.3.cloned.1.call-done.in_ref.refs_0_
  96.7 0.0 all-gather.5.cloned.1.call-update
  96.7 0.0 all-reduce.18.cloned.1.call-start
  96.7 0.0 copy-done.12
  96.7 0.6 convert_bitcast_fusion
  97.4 0.1 slice.80
  97.4 0.1 slice.81
  97.5 0.1 slice.89
  97.6 0.1 slice.90
  97.7 0.1 pad_add_fusion
  97.8 0.1 broadcast_bitcast_fusion.5
  97.9 0.1 broadcast_bitcast_fusion.2
  98.0 0.1 broadcast_bitcast_fusion.4
  98.0 0.1 broadcast_bitcast_fusion.1
  98.1 0.1 compare_convert_fusion.4
  98.2 0.1 broadcast_bitcast_fusion
  98.3 0.1 fusion.18
  98.4 0.1 stack.132
  98.5 1.0 copy.78.cols_ref.refs_21_
  99.5 0.1 broadcast_in_dim.55
  99.6 0.7 broadcast_in_dim_reshape.3.skip_ref.refs_11_.refs_19_
  100.3 0.1 broadcast_bitcast_fusion.3
  100.3 0.1 fusion.24
  100.4 0.1 stack.119
  100.5 1.0 copy.79.refs_12_.refs_21_
  101.5 0.5 pad_bitcast_fusion
  102.1 1.5 slice_bitcast_fusion
  103.5 53.1 %ssd_forward.2 = (bf16[1024,1024]{1,0:T(8,128)(2,1)}, f32[1024,1024]{1,0:T(8,128)}, f32[1024,1024]{1,0:T(8,128)}, bf16[1024,256]{1,0:T(8,128)(2,1)}, f32[1024,25...) custom-call(bf16[1024,2048]{1,0:T(8,128)(2,1)} %all-gather.3.cloned., ...), custom_call_target="tpu_custom_call" | custom-call | flops 15032385536 | bytes 41943040 | tf_op jit(solution)/shard_map/ssd_forward/pallas_call | solution.py:721
  156.7 21.5 %all-gather.5.cloned.1.call-done.refs_0_.refs_1_ = bf16[1024,2048]{1,0:T(8,128)(2,1)} async-done(((bf16[256,2048]{1,0:T(8,128)(2,1)}), bf16[1024,2048]{1,0:T(8,128)(2,1)}) %all-gather.5.cloned.1.call-update) | async-done | bytes 4194320 | tf_op jit(solution)/shard_map/all_gather | solution.py:1704
  178.2 105.2 %ssd_forward.3 = (bf16[1024,1024]{1,0:T(8,128)(2,1)}, f32[1024,1024]{1,0:T(8,128)}, f32[1024,1024]{1,0:T(8,128)}, bf16[1024,256]{1,0:T(8,128)(2,1)}, f32[1024,25...) custom-call(bf16[1024,2048]{1,0:T(8,128)(2,1)} %all-gather.5.cloned., ...), custom_call_target="tpu_custom_call" | custom-call | flops 15032385536 | bytes 41943040 | tf_op jit(solution)/shard_map/ssd_forward/pallas_call | solution.py:721
  283.4 105.3 %ssd_backward.2 = (bf16[1024,1024]{1,0:T(8,128)(2,1)}, bf16[1024,1024]{1,0:T(8,128)(2,1)}, bf16[1024,1024]{1,0:T(8,128)(2,1)}, bf16[1024,128]{1,0:T(8,128)(2,1)}...) custom-call(bf16[1024,2048]{1,0:T(8,128)(2,1)} %get-tuple-element.89, ...), custom_call_target="tpu_custom_call" | custom-call | flops 12884901888 | bytes 62914560 | tf_op jit(solution)/shard_map/ssd_backward/pallas_call | solution.py:785
  388.7 0.0 all-reduce.18.cloned.1.call-update
  388.7 0.0 reduce-scatter.2.cloned.1.call-start
  388.8 100.8 %ssd_backward.3 = (bf16[1024,1024]{1,0:T(8,128)(2,1)}, bf16[1024,1024]{1,0:T(8,128)(2,1)}, bf16[1024,1024]{1,0:T(8,128)(2,1)}, bf16[1024,128]{1,0:T(8,128)(2,1)}...) custom-call(bf16[1024,2048]{1,0:T(8,128)(2,1)} %get-tuple-element.98, ...), custom_call_target="tpu_custom_call" | custom-call | flops 12884901888 | bytes 62914560 | tf_op jit(solution)/shard_map/ssd_backward/pallas_call | solution.py:785
  489.7 0.0 reduce-scatter.2.cloned.1.call-update
  489.7 1.3 copy.82.refs_16_
  491.0 0.0 copy-done.10
  491.1 0.6 select_maximum_fusion.refs_19_
  491.7 0.9 dynamic-slice_bitcast_fusion
  492.6 0.9 dynamic-slice_bitcast_fusion.1
  493.6 0.0 all-reduce.18.cloned.1.call-done.refs_12_
  493.6 95.0 %weight_gradients.1 = (f32[256,1024]{1,0:T(8,128)}, f32[256,1024]{1,0:T(8,128)}, f32[256,128]{1,0:T(8,128)}, f32[1024,256]{1,0:T(8,128)}, f32[256,256]{1,0:T(8,1...) custom-call(bf16[1024,2048]{1,0:T(8,128)(2,1)} %all-gather.3.cloned.1.call-done.in_ref.refs_0_, ...), custom_call_target="tpu_custom_call" | custom-call | flops 26843545600 | bytes 262144000 | tf_op jit(solution)/shard_map/weight_gradients/pallas_call | solution.py:1431
  588.6 1.6 copy.85
  590.2 1.8 small_gradients.1
  592.0 1.2 copy-done.1
  593.3 0.9 copy-done.2
  594.2 8.1 %finish_rows.1 = (bf16[2,256,2048]{2,1,0:T(8,128)(2,1)}, bf16[2,256,2048]{2,1,0:T(8,128)(2,1)}, f32[8,256]{1,0:T(8,128)S(1)}) custom-call(f32[256,2048]{1,0:T(8,128)} %get-tuple-element.107.sum0, bf16[256,2048]{1,0:T(8,128)(2,1)S(1)} %copy-done.1, bf16[2,256,256]{2,1,0:T(8,128)(2,1)S(1)} %copy-done.2, bf16[2048,256]{1,0:T(8,128)(2,1)S(1)} %copy-done, ...), custom_call_target="tpu_custom_call" | custom-call | flops 1073741824 | bytes 18874368 | tf_op jit(solution)/shard_map/finish_rows/pallas_call | solution.py:1530
  602.3 10.3 %gain_sum.1 = f32[8,256]{1,0:T(8,128)S(1)} custom-call(f32[8,256]{1,0:T(8,128)S(1)} %get-tuple-element.132.part), custom_call_target="tpu_custom_call" | custom-call | bytes 1048576 | tf_op jit(solution)/shard_map/gain_sum/pallas_call | solution.py:1589
  612.7 0.6 copy.92
  613.3 1.0 copy.98
  614.2 1.0 copy.99
  615.2 0.7 copy.100
  615.9 1.0 copy.101
  (45 shorter events, 0.2 us)
Async XLA Ops:
  7.2 2.2 copy-start.4
  7.2 2.2 copy-start.3
  7.2 89.5 %all-gather.3.cloned.1.call-start = ((), (), s32[]{:S(2)}) async-start(), calls=%async_computation.1 | async-start | bytes 5242880 | tf_op jit(solution)/shard_map/all_gather | solution.py:1704
  9.4 2.0 copy-start.13
  11.3 85.4 %copy-start.12 = (s32[2,1,1024]{2,1,0:T(1,128)S(1)}, s32[2,1,1024]{2,1,0:T(1,128)}, u32[]{:S(2)}) copy-start(s32[2,1,1024]{2,1,0:T(1,128)} %param.18) | copy-start | bytes 24580
  11.3 88.2 %copy-start.16 = (f32[16]{0:T(128)S(1)}, f32[16]{0:T(128)}, u32[]{:S(2)}) copy-start(f32[16]{0:T(128)} %param.31) | copy-start | bytes 196
  11.3 166.8 %all-gather.5.cloned.1.call-start = ((), (), s32[]{:S(2)}) async-start(), calls=%async_computation.2 | async-start | bytes 5242880 | tf_op jit(solution)/shard_map/all_gather | solution.py:1704
  12.2 89.4 %copy-start.18 = (f32[16]{0:T(128)S(1)}, f32[16]{0:T(128)}, u32[]{:S(2)}) copy-start(f32[16]{0:T(128)} %param.30) | copy-start | bytes 196
  12.2 89.4 %copy-start.17 = (f32[16]{0:T(128)S(1)}, f32[16]{0:T(128)}, u32[]{:S(2)}) copy-start(f32[16]{0:T(128)} %param.29) | copy-start | bytes 196
  12.2 89.9 %copy-start.5 = (bf16[2,1,256,2048]{3,2,1,0:T(8,128)(2,1)S(1)}, bf16[2,1,256,2048]{3,2,1,0:T(8,128)(2,1)}, u32[]{:S(2)}) copy-start(bf16[2,1,256,2048]{3,2,1,0:T(8,128)(2,1)} %param.19) | copy-start | bytes 6291460
  96.7 396.9 %all-reduce.18.cloned.1.call-start = ((), (), s32[]{:S(2)}) async-start(), calls=%async_computation.4 | async-start | bytes 1048576 | tf_op jit(solution)/shard_map/psum | solution.py:1751
  388.7 203.3 %reduce-scatter.2.cloned.1.call-start = ((), (), s32[]{:S(2)}) async-start(), calls=%async_computation.3 | async-start | bytes 5242880 | tf_op jit(solution)/shard_map/reduce_scatter | solution.py:1708
  489.6 1.4 copy-start.10
  489.6 1.4 copy-start.11
  489.6 1.4 copy-start.14
  489.7 1.4 copy-start.15
  493.6 98.4 %copy-start = (bf16[2048,256]{1,0:T(8,128)(2,1)S(1)}, bf16[2048,256]{1,0:T(8,128)(2,1)}, u32[]{:S(2)}) copy-start(bf16[2048,256]{1,0:T(8,128)(2,1)} %get-tuple-element.86.state_w.refs_3_) | copy-start | bytes 3145732
  592.0 1.2 copy-start.1
  593.3 0.9 copy-start.2
  594.2 19.0 %copy-start.8 = (f32[256,1024]{1,0:T(8,128)S(1)}, f32[256,1024]{1,0:T(8,128)}, u32[]{:S(2)}) copy-start(f32[256,1024]{1,0:T(8,128)} %get-tuple-element.251) | copy-start | bytes 3145732
  602.3 11.9 %copy-start.7 = (f32[256,1024]{1,0:T(8,128)S(1)}, f32[256,1024]{1,0:T(8,128)}, u32[]{:S(2)}) copy-start(f32[256,1024]{1,0:T(8,128)} %get-tuple-element.252) | copy-start | bytes 3145732
  613.3 1.9 copy-start.9
  613.3 2.7 copy-start.6
Sparse Core Ops, SparseCore 0:
  11.5 83.4 all-gather.2
  97.1 81.0 all-gather.4
  388.8 45.1 all-reduce.17
  489.8 96.0 reduce-scatter.1

commit v5 on v4

--- a/solution.py
+++ b/solution.py
@@ -29,6 +29,14 @@
     return jnp.dot(former, latter, preferred_element_type=F32, precision=precision)
 
 
+def head_sums(values, place):
+    high = values.astype(BF16)
+    rest = values - high.astype(F32)
+    middle = rest.astype(BF16)
+    low = (rest - middle.astype(F32)).astype(BF16)
+    return mm(high, place) + (mm(middle, place) + mm(low, place))
+
+
 def mm_nt(former, latter):
     return lax.dot_general(
         former, latter, (((1,), (1,)), ((), ())), preferred_element_type=F32
@@ -278,7 +286,7 @@
                     self.sending(flow, hop, part).wait_send()
 
 
-def run_line(step, steps, scatter, gather, out):
+def run_line(step, steps, scatter, gather, out, early):
     size = (scatter or gather).size
     first = 1 if scatter and gather else 0
     actions = [[] for _ in range(PARTS * (size + first))]
@@ -294,6 +302,8 @@
     if scatter:
         actions[0].insert(0, scatter.begin)
     for at in sorted(set(steps)):
+        if (at == 0) != early:
+            continue
         todo = [action for when, each in zip(steps, actions) if when == at for action in each]
 
         @pl.when(step == at)
@@ -333,32 +343,57 @@
             needed += LineGather.scratch(self.size)
         return needed
 
-    def wrap(self, body, ins, outs, pace):
+    def wrap(self, body, ins, outs, pace, resident):
         has_scatter, has_gather = self.scatter is not None, self.gather is not None
         hosts = has_scatter + has_gather
-        size, spare = self.size, len(self.scratch())
-        if not hosts:
-            return body
+        size, spare, kept = self.size, len(self.scratch()), len(resident) + 1
 
         def kernel(*refs):
+            refs, stored = refs[: len(refs) - kept], refs[len(refs) - kept :]
+            tail = refs[len(refs) - spare :]
             sources, targets = refs[ins : ins + hosts], refs[ins + hosts + outs : ins + outs + 2 * hosts]
-            tail = refs[len(refs) - spare :]
             step = pl.program_id(0) * pl.num_programs(1) + pl.program_id(1)
             me, column = lax.axis_index("tp"), lax.axis_index("fsdp")
+            operands = list(refs[:ins])
+            loads = []
+            for at, (which, _, need) in enumerate(resident):
+                copy = pltpu.make_async_copy(operands[which], stored[at], stored[-1].at[at])
+                operands[which] = stored[at]
+                loads.append((copy, need))
 
             @pl.when(step == 0)
             def _():
-                greet([(column, lax.rem(me + hop, size)) for hop in range(1, size)])
+                for copy, _ in loads:
+                    copy.start()
+                if hosts:
+                    greet([(column, lax.rem(me + hop, size)) for hop in range(1, size)])
+
+            if hosts:
+                scatter = LineScatter(size, sources[0], *tail[:7]) if has_scatter else None
+                gather = LineGather(size, sources[-1], targets[-1], *tail[-3:]) if has_gather else None
+                run_line(step, pace, scatter, gather, targets[0], True)
+            for when in sorted(set(need for _, need in loads)):
+
+                @pl.when(step == when)
+                def _():
+                    for copy, need in loads:
+                        if need == when:
+                            copy.wait()
 
             body(
-                *refs[:ins], *refs[ins + hosts : ins + hosts + outs],
+                *operands, *refs[ins + hosts : ins + hosts + outs],
                 *refs[ins + outs + 2 * hosts : len(refs) - spare],
             )
-            scatter = LineScatter(size, sources[0], *tail[:7]) if has_scatter else None
-            gather = LineGather(size, sources[-1], targets[-1], *tail[-3:]) if has_gather else None
-            run_line(step, pace, scatter, gather, targets[0])
+            if hosts:
+                run_line(step, pace, scatter, gather, targets[0], False)
 
         return kernel
+
+
+def resident_scratch(resident):
+    return [pltpu.VMEM(array.shape, array.dtype) for _, array, _ in resident] + [
+        pltpu.SemaphoreType.DMA((len(resident),))
+    ]
 
 
 def forward_kernel(
@@ -470,8 +505,13 @@
     def _():
         row_sums(
             tp_size, cot_ref, out_w, gate_rows, mixed_rows, gain_row,
-            branch_s, rowsum_s, slots_s, turn_s, swap_send, swap_recv, stats_out,
-        )
+            branch_s, rowsum_s, slots_s, swap_send, swap_recv,
+        )
+
+    scales = partial(
+        row_scales, tp_size, gain_row.shape[1] * tp_size, rowsum_s, slots_s, turn_s, swap_send,
+        swap_recv, stats_out,
+    )
 
     @pl.when(g >= 0)
     def _():
@@ -481,17 +521,16 @@
             gate_w, value_w, step_w, taps_ref, bias_ref, rate_ref, skip_ref, gain_ref, cols_ref, seg_ref,
             branch_out, lowgate_out, lowvalue_out, lowstep_out, gbc_out, gin_out, small_out, sums_out,
             vbuf, gcbuf, gram_s, dgram, b_s, c_t, step_s, ent_s, fade_s, cums_s, cums_t, keep_s,
-            grad_state, gin, gb_s, gc_s, u_s, v_s, fin_s, small_s, sums_s, branch_s, stats_out,
+            grad_state, gin, gb_s, gc_s, u_s, v_s, fin_s, small_s, sums_s, branch_s, stats_out, scales,
         )
 
 
 def row_sums(
     tp_size, cot_ref, out_w, gate_rows, mixed_rows, gain_row,
-    branch_s, rowsum_s, slots_s, turn_s, swap_send, swap_recv, stats_out,
+    branch_s, rowsum_s, slots_s, swap_send, swap_recv,
 ):
     step, groups = pl.program_id(1), pl.num_programs(1)
     me, column = lax.axis_index("tp"), lax.axis_index("fsdp")
-    total_inner = gain_row.shape[1] * tp_size
     grad = mm_nt(cot_ref[...], out_w[...])
     branch_s[step] = grad.astype(BF16)
     gate = gate_rows[...].astype(F32)
@@ -505,26 +544,33 @@
     @pl.when(step == groups - 1)
     def _():
         slots_s[me] = rowsum_s[...]
-        copies = [
-            remote_copy(
-                rowsum_s, slots_s.at[me], swap_send.at[hop - 1], swap_recv.at[hop - 1],
-                (column, lax.rem(me + hop, tp_size)),
-            )
-            for hop in range(1, tp_size)
-        ]
-        for copy in copies:
+        for copy in row_swaps(tp_size, rowsum_s, slots_s, swap_send, swap_recv):
             copy.start()
-        for copy in copies:
-            copy.wait()
-        total = slots_s[0]
-        for at in range(1, tp_size):
-            total = total + slots_s[at]
-        turn_s[...] = jnp.zeros(turn_s.shape, F32)
-        scale = lax.rsqrt(total[:, 0:1, :] / total_inner + EPSILON)
-        turn_s[:, 0:1, :] = scale
-        turn_s[:, 1:2, :] = scale * scale * scale * (total[:, 1:2, :] / total_inner)
-        for group in range(turn_s.shape[0]):
-            stats_out[group * GROUP : (group + 1) * GROUP, :] = jnp.transpose(turn_s[group])
+
+
+def row_swaps(tp_size, rowsum_s, slots_s, swap_send, swap_recv):
+    me, column = lax.axis_index("tp"), lax.axis_index("fsdp")
+    return [
+        remote_copy(
+            rowsum_s, slots_s.at[me], swap_send.at[hop - 1], swap_recv.at[hop - 1],
+            (column, lax.rem(me + hop, tp_size)),
+        )
+        for hop in range(1, tp_size)
+    ]
+
+
+def row_scales(tp_size, total_inner, rowsum_s, slots_s, turn_s, swap_send, swap_recv, stats_out):
+    for copy in row_swaps(tp_size, rowsum_s, slots_s, swap_send, swap_recv):
+        copy.wait()
+    total = slots_s[0]
+    for at in range(1, tp_size):
+        total = total + slots_s[at]
+    turn_s[...] = jnp.zeros(turn_s.shape, F32)
+    scale = lax.rsqrt(total[:, 0:1, :] / total_inner + EPSILON)
+    turn_s[:, 0:1, :] = scale
+    turn_s[:, 1:2, :] = scale * scale * scale * (total[:, 1:2, :] / total_inner)
+    for group in range(turn_s.shape[0]):
+        stats_out[group * GROUP : (group + 1) * GROUP, :] = jnp.transpose(turn_s[group])
 
 
 def backward_step(
@@ -533,7 +579,7 @@
     gate_w, value_w, step_w, taps_ref, bias_ref, rate_ref, skip_ref, gain_ref, cols_ref, seg_ref,
     branch_out, lowgate_out, lowvalue_out, lowstep_out, gbc_out, gin_out, small_out, sums_out,
     vbuf, gcbuf, gram_s, dgram, b_s, c_t, step_s, ent_s, fade_s, cums_s, cums_t, keep_s,
-    grad_state, gin, gb_s, gc_s, u_s, v_s, fin_s, small_s, sums_s, branch_s, stats_ref,
+    grad_state, gin, gb_s, gc_s, u_s, v_s, fin_s, small_s, sums_s, branch_s, stats_ref, scales,
 ):
     group = groups - 1 - g
     nblocks = grad_state.shape[0]
@@ -570,6 +616,10 @@
         u_s[...] = jnp.zeros(u_s.shape, F32)
         v_s[...] = jnp.zeros(v_s.shape, F32)
         fin_s[...] = jnp.zeros(fin_s.shape, F32)
+
+    @pl.when((g == 0) & (j == 0))
+    def _():
+        scales()
 
     at = pl.multiple_of(j * BLOCK, BLOCK)
     gate, mixed = gate_ref[...].astype(F32), mixed_ref[...]
@@ -639,10 +689,11 @@
     through = jnp.concatenate([top, bottom], axis=0) + faded
     column = scaled_float * through
     final = kept + jnp.sum(scaled_float * faded, axis=0, keepdims=True)
-    place = (iota((BLOCK, 128), 1) == j * PER_BLOCK + iota((BLOCK, 128), 0) // HEAD_DIM).astype(F32)
-    u_s[...] += mm(grad_scan_float * scanned - column, place, PRECISE)
-    v_s[...] += mm(column, place, PRECISE)
-    fin_s[...] += mm(jnp.broadcast_to(final, (8, BLOCK)), place, PRECISE)
+    place = iota((BLOCK, 128), 1) == j * PER_BLOCK + iota((BLOCK, 128), 0) // HEAD_DIM
+    place = place.astype(F32).astype(BF16)
+    u_s[...] += head_sums(grad_scan_float * scanned - column, place)
+    v_s[...] += head_sums(column, place)
+    fin_s[...] += head_sums(jnp.broadcast_to(final, (8, BLOCK)), place)
 
     grad_conv = (step_wide * through + skip * grad_mixed) * slope
     after = gcbuf.at[j]
@@ -718,14 +769,16 @@
     line = lambda rows: pl.BlockSpec((rows, BLOCK), lambda g, j: (0, j))
     rows_of = lambda width: pl.BlockSpec((GROUP, width), lambda g, j: (g, 0))
     specs, shapes = hosted.outs()
+    hbm = pl.BlockSpec(memory_space=pl.ANY)
+    resident = [(1, gate_w, 0), (2, value_w, 0), (3, state_w, 0), (4, step_w, 0), (14, out_w, 0)]
     return pl.pallas_call(
-        hosted.wrap(forward_kernel, FORWARD_INS, FORWARD_OUTS, pace),
+        hosted.wrap(forward_kernel, FORWARD_INS, FORWARD_OUTS, pace, resident),
         grid=(groups, blocks),
         in_specs=[
-            rows_of(model), whole(gate_w), whole(value_w), whole(state_w), whole(step_w),
+            rows_of(model), hbm, hbm, hbm, hbm,
             line(CONV), line(1), whole(staps), whole(sbias), whole(step_bias), whole(rate), line(1),
             rows_of(cols.shape[1]), pl.BlockSpec((1, GROUP), lambda g, j: (0, g)),
-            whole(out_w), line(1),
+            hbm, line(1),
         ] + hosted.in_specs(),
         out_specs=[
             wide, wide, wide, rows_of(2 * STATE), rows_of(2 * STATE), rows_of(128), rows_of(128),
@@ -750,7 +803,7 @@
             pltpu.VMEM((blocks, 8, 128), F32),
             pltpu.VMEM((blocks, STATE, BLOCK), F32),
             pltpu.VMEM((GROUP, model), F32),
-        ] + hosted.scratch(),
+        ] + hosted.scratch() + resident_scratch(resident),
         compiler_params=params(2 if hosted.operands() else None),
         cost_estimate=pl.CostEstimate(
             flops=2 * length * model * (3 * inner + 512), bytes_accessed=40 << 20, transcendentals=0
@@ -772,6 +825,8 @@
     groups, blocks = length // GROUP, inner // BLOCK
     assert groups == blocks
     last = groups - 1
+    hbm = pl.BlockSpec(memory_space=pl.ANY)
+    resident = [(1, out_w, 0), (13, gate_w, blocks), (14, value_w, blocks), (15, step_w, blocks)]
     row = lambda g: last - jnp.maximum(g - 1, 0)
     column = lambda g, j: jnp.where(g == 0, 0, j)
     wide = pl.BlockSpec((GROUP, BLOCK), lambda g, j: (row(g), column(g, j)))
@@ -783,13 +838,13 @@
         (HALO, BLOCK), lambda g, j: (jnp.maximum(row(g) * steps - 1, 0), column(g, j))
     )
     return pl.pallas_call(
-        hosted.wrap(partial(backward_kernel, tp_size), BACKWARD_INS, BACKWARD_OUTS, pace),
+        hosted.wrap(partial(backward_kernel, tp_size), BACKWARD_INS, BACKWARD_OUTS, pace, resident),
         grid=(groups + 1, blocks),
         in_specs=[
-            first(model), whole(out_w), first(inner), first(inner), whole(gain),
+            first(model), hbm, first(inner), first(inner), whole(gain),
             wide, wide, before, wide, rows_of(2 * STATE), rows_of(128), rows_of(128),
             pl.BlockSpec((1, STATE, BLOCK), lambda g, j: (row(g), 0, column(g, j))),
-            whole(gate_w), whole(value_w), whole(step_w),
+            hbm, hbm, hbm,
             line(CONV), line(1), whole(rate), line(1), line(1),
             rows_of(cols.shape[1]), pl.BlockSpec((1, GROUP), lambda g, j: (0, row(g))),
         ] + hosted.in_specs(),
@@ -831,7 +886,7 @@
             pltpu.VMEM((groups, 128, GROUP), F32),
             pltpu.SemaphoreType.DMA((tp_size - 1,)),
             pltpu.SemaphoreType.DMA((tp_size - 1,)),
-        ] + hosted.scratch(),
+        ] + hosted.scratch() + resident_scratch(resident),
         compiler_params=params(collective),
         cost_estimate=pl.CostEstimate(
             flops=6 * length * model * inner, bytes_accessed=60 << 20, transcendentals=0
@@ -1724,7 +1779,7 @@
     columns = [document_columns(segment_ids[at, 0]) for at in range(micro)]
     seg_lines = [segment_ids[at, 0].astype(F32)[None, :] for at in range(micro)]
     quick = [0, 3, 7, 11, 14, 15, 15, 15, 15, 15]
-    paces = {4: [0, 3, 4, 6, 9, 12, 15, 17, 19, 19], 5: [4, 6, 9, 12, 14, 17, 19, 19]}
+    paces = {4: [0, 3, 4, 6, 9, 12, 15, 17, 19, 19], 5: [0, 4, 4, 7, 10, 13, 18, 19]}
 
     def forward(at, hosted):
         return forward_call(

time: 634 us -> 624 us (0.984)
  Pallas kernels: 564 us -> 554 us
    pallas_call x2, Pallas kernels: 206 us -> 200 us  [backward_call(): pl.pallas_call(hosted.wrap(partial(backward_kernel, tp_size), BACKWARD_IN...]
where the time goes in v5:
time: 624 us; the launch traced here: 614 us
  Pallas kernels  554 us (89%)
  waiting for transfers between devices  21.2 us (3%)
  local copies, waits for them, and re-layouts  17.8 us (3%)
  between operations  14.5 us (2%)
    pallas_call x2, Pallas kernels, backward_call(): pl.pallas_call(hosted.wrap(partial(backward_kernel, tp_size), BACKWARD_IN...  200 us
    pallas_call x2, Pallas kernels, forward_call(): pl.pallas_call(hosted.wrap(forward_kernel, FORWARD_INS, FORWARD_OUTS, pac...  154 us
    pallas_call x1, Pallas kernels, tail_call(): pl.pallas_call(partial(tail_kernel, chips, tp_size, micro, widths), grid=...  96.5 us
    pallas_call x1, Pallas kernels, gather_call(): pl.pallas_call(partial(gather_kernel, count, pieces), in_specs=[pl.BlockS...  84.4 us
    all_gather x2, waiting for transfers between devices, gather_tp(): return lax.all_gather(values, 'tp', axis=0, tiled=True)  21.1 us
  transfers between devices with their start and end apart: 4, of which 1 were waited for; matrix products, arithmetic and copies ran while one was open for 2% of the time, Pallas kernels for 54%

profile of v5, /device:TPU:0, one launch (start us, length us, event | category | flops | bytes accessed | tf_op | source)
XLA Modules:
  0.0 613.7 jit_solution(11899159475159551096)
XLA Ops:
  7.2 0.0 copy-start.4
  7.2 0.0 copy-start.3
  7.2 0.0 all-gather.3.cloned.1.call-start
  7.2 2.2 fusion.3
  9.4 0.0 copy-start.13
  9.5 1.9 fusion.5
  11.3 0.0 all-gather.3.cloned.1.call-update
  11.3 0.0 copy-start.16
  11.3 0.0 all-gather.5.cloned.1.call-start
  11.4 0.1 copy.77
  11.5 0.6 pad.57.refs_3_
  12.2 84.4 %gather_weights.1 = (bf16[2048,1024]{1,0:T(8,128)(2,1)}, bf16[2048,1024]{1,0:T(8,128)(2,1)}, bf16[2048,256]{1,0:T(8,128)(2,1)}, bf16[2048,128]{1,0:T(8,128)(2,1)}, bf16[1024,2048]{1,0:T(8,128)(2,1)}) custom-call(bf16[256,1024]{1,0:T(8,128)(2,1)} %refs_0_.1, bf16[256,1024]{1,0:T(8,128)(2,1)} %refs_1_.1, bf16[256,256]{1,0:T(8,128)(2,1)} %refs_2_.1, ...), custom_call_target="tpu_custom_call" | custom-call | bytes 262144000 | tf_op jit(solution)/shard_map/gather_weights/pallas_call | solution.py:978
  96.6 0.0 all-gather.3.cloned.1.call-done.refs_0_
  96.7 0.0 all-gather.5.cloned.1.call-update
  96.7 0.0 all-reduce.18.cloned.1.call-start
  96.7 0.6 convert_bitcast_fusion
  97.4 0.1 slice.80
  97.4 0.1 slice.81
  97.5 0.1 slice.89
  97.6 0.1 slice.90
  97.7 0.1 pad_add_fusion
  97.8 0.1 broadcast_bitcast_fusion.5
  97.9 0.1 broadcast_bitcast_fusion.2
  98.0 0.1 broadcast_bitcast_fusion.4
  98.0 0.1 broadcast_bitcast_fusion.1
  98.1 0.1 compare_convert_fusion.4
  98.2 0.1 broadcast_bitcast_fusion
  98.3 0.1 fusion.18
  98.4 0.1 stack.132
  98.5 1.0 copy.78.refs_12_.refs_21_
  99.5 0.0 copy-done.16
  99.5 0.1 broadcast_in_dim.55
  99.6 0.7 broadcast_in_dim_reshape.3.refs_11_.refs_19_
  100.3 0.1 broadcast_bitcast_fusion.3
  100.3 0.1 fusion.24
  100.4 0.1 stack.119
  100.5 1.0 copy.79.refs_12_.refs_21_
  101.5 0.5 pad_bitcast_fusion
  102.1 1.5 slice_bitcast_fusion
  103.5 53.6 %ssd_forward.2 = (bf16[1024,1024]{1,0:T(8,128)(2,1)}, f32[1024,1024]{1,0:T(8,128)}, f32[1024,1024]{1,0:T(8,128)}, bf16[1024,256]{1,0:T(8,128)(2,1)}, f32[1024,25...) custom-call(bf16[1024,2048]{1,0:T(8,128)(2,1)} %all-gather.3.cloned., ...), custom_call_target="tpu_custom_call" | custom-call | flops 15032385536 | bytes 41943040 | tf_op jit(solution)/shard_map/ssd_forward/pallas_call | solution.py:774
  157.1 21.1 %all-gather.5.cloned.1.call-done.refs_0_.refs_1_ = bf16[1024,2048]{1,0:T(8,128)(2,1)} async-done(((bf16[256,2048]{1,0:T(8,128)(2,1)}), bf16[1024,2048]{1,0:T(8,128)(2,1)}) %all-gather.5.cloned.1.call-update) | async-done | bytes 4194320 | tf_op jit(solution)/shard_map/all_gather | solution.py:1759
  178.2 100.1 %ssd_forward.3 = (bf16[1024,1024]{1,0:T(8,128)(2,1)}, f32[1024,1024]{1,0:T(8,128)}, f32[1024,1024]{1,0:T(8,128)}, bf16[1024,256]{1,0:T(8,128)(2,1)}, f32[1024,25...) custom-call(bf16[1024,2048]{1,0:T(8,128)(2,1)} %all-gather.5.cloned., ...), custom_call_target="tpu_custom_call" | custom-call | flops 15032385536 | bytes 41943040 | tf_op jit(solution)/shard_map/ssd_forward/pallas_call | solution.py:774
  278.3 101.6 %ssd_backward.2 = (bf16[1024,1024]{1,0:T(8,128)(2,1)}, bf16[1024,1024]{1,0:T(8,128)(2,1)}, bf16[1024,1024]{1,0:T(8,128)(2,1)}, bf16[1024,128]{1,0:T(8,128)(2,1)}...) custom-call(bf16[1024,2048]{1,0:T(8,128)(2,1)} %get-tuple-element.89, ...), custom_call_target="tpu_custom_call" | custom-call | flops 12884901888 | bytes 62914560 | tf_op jit(solution)/shard_map/ssd_backward/pallas_call | solution.py:840
  379.9 0.0 all-reduce.18.cloned.1.call-update
  379.9 0.0 reduce-scatter.2.cloned.1.call-start
  380.0 97.9 %ssd_backward.3 = (bf16[1024,1024]{1,0:T(8,128)(2,1)}, bf16[1024,1024]{1,0:T(8,128)(2,1)}, bf16[1024,1024]{1,0:T(8,128)(2,1)}, bf16[1024,128]{1,0:T(8,128)(2,1)}...) custom-call(bf16[1024,2048]{1,0:T(8,128)(2,1)} %get-tuple-element.98, ...), custom_call_target="tpu_custom_call" | custom-call | flops 12884901888 | bytes 62914560 | tf_op jit(solution)/shard_map/ssd_backward/pallas_call | solution.py:840
  478.0 0.0 reduce-scatter.2.cloned.1.call-update
  478.0 1.3 copy.82.refs_16_
  479.4 0.6 select_maximum_fusion.refs_19_
  480.0 0.9 dynamic-slice_bitcast_fusion
  480.9 0.9 dynamic-slice_bitcast_fusion.1
  481.9 0.0 all-reduce.18.cloned.1.call-done.refs_12_
  481.9 96.5 %weight_gradients.1 = (f32[256,1024]{1,0:T(8,128)}, f32[256,1024]{1,0:T(8,128)}, f32[256,128]{1,0:T(8,128)}, f32[1024,256]{1,0:T(8,128)}, f32[256,256]{1,0:T(8,1...) custom-call(bf16[1024,2048]{1,0:T(8,128)(2,1)} %all-gather.3.cloned.1.call-done.refs_0_, ...), custom_call_target="tpu_custom_call" | custom-call | flops 26843545600 | bytes 262144000 | tf_op jit(solution)/shard_map/weight_gradients/pallas_call | solution.py:1486
  578.4 1.6 copy.85
  580.0 1.8 small_gradients.1
  581.8 1.2 copy-done.1
  583.1 0.9 copy-done.2
  584.0 8.1 %finish_rows.1 = (bf16[2,256,2048]{2,1,0:T(8,128)(2,1)}, bf16[2,256,2048]{2,1,0:T(8,128)(2,1)}, f32[8,256]{1,0:T(8,128)S(1)}) custom-call(f32[256,2048]{1,0:T(8,128)} %get-tuple-element.107.sum0, bf16[256,2048]{1,0:T(8,128)(2,1)S(1)} %copy-done.1, bf16[2,256,256]{2,1,0:T(8,128)(2,1)S(1)} %copy-done.2, bf16[2048,256]{1,0:T(8,128)(2,1)S(1)} %copy-done, ...), custom_call_target="tpu_custom_call" | custom-call | flops 1073741824 | bytes 18874368 | tf_op jit(solution)/shard_map/finish_rows/pallas_call | solution.py:1585
  592.1 10.4 %gain_sum.1 = f32[8,256]{1,0:T(8,128)S(1)} custom-call(f32[8,256]{1,0:T(8,128)S(1)} %get-tuple-element.132.part), custom_call_target="tpu_custom_call" | custom-call | bytes 1048576 | tf_op jit(solution)/shard_map/gain_sum/pallas_call | solution.py:1644
  602.5 0.6 copy.92
  603.1 1.0 copy.98
  604.1 1.0 copy.99
  605.1 0.7 copy.100
  605.8 1.0 copy.101
  (45 shorter events, 0.2 us)
Async XLA Ops:
  7.2 2.2 copy-start.4
  7.2 2.2 copy-start.3
  7.2 89.5 %all-gather.3.cloned.1.call-start = ((), (), s32[]{:S(2)}) async-start(), calls=%async_computation.1 | async-start | bytes 5242880 | tf_op jit(solution)/shard_map/all_gather | solution.py:1759
  9.4 2.0 copy-start.13
  11.3 85.4 %copy-start.12 = (s32[2,1,1024]{2,1,0:T(1,128)S(1)}, s32[2,1,1024]{2,1,0:T(1,128)}, u32[]{:S(2)}) copy-start(s32[2,1,1024]{2,1,0:T(1,128)} %param.18) | copy-start | bytes 24580
  11.3 88.2 %copy-start.16 = (f32[16]{0:T(128)S(1)}, f32[16]{0:T(128)}, u32[]{:S(2)}) copy-start(f32[16]{0:T(128)} %param.31) | copy-start | bytes 196
  11.3 166.8 %all-gather.5.cloned.1.call-start = ((), (), s32[]{:S(2)}) async-start(), calls=%async_computation.2 | async-start | bytes 5242880 | tf_op jit(solution)/shard_map/all_gather | solution.py:1759
  12.2 89.4 %copy-start.18 = (f32[16]{0:T(128)S(1)}, f32[16]{0:T(128)}, u32[]{:S(2)}) copy-start(f32[16]{0:T(128)} %param.30) | copy-start | bytes 196
  12.2 89.4 %copy-start.17 = (f32[16]{0:T(128)S(1)}, f32[16]{0:T(128)}, u32[]{:S(2)}) copy-start(f32[16]{0:T(128)} %param.29) | copy-start | bytes 196
  12.2 89.9 %copy-start.5 = (bf16[2,1,256,2048]{3,2,1,0:T(8,128)(2,1)S(1)}, bf16[2,1,256,2048]{3,2,1,0:T(8,128)(2,1)}, u32[]{:S(2)}) copy-start(bf16[2,1,256,2048]{3,2,1,0:T(8,128)(2,1)} %param.19) | copy-start | bytes 6291460
  96.7 385.2 %all-reduce.18.cloned.1.call-start = ((), (), s32[]{:S(2)}) async-start(), calls=%async_computation.4 | async-start | bytes 1048576 | tf_op jit(solution)/shard_map/psum | solution.py:1806
  379.9 201.9 %reduce-scatter.2.cloned.1.call-start = ((), (), s32[]{:S(2)}) async-start(), calls=%async_computation.3 | async-start | bytes 5242880 | tf_op jit(solution)/shard_map/reduce_scatter | solution.py:1763
  477.9 1.4 copy-start.10
  478.0 1.4 copy-start.11
  478.0 1.4 copy-start.14
  478.0 1.4 copy-start.15
  481.9 99.9 %copy-start = (bf16[2048,256]{1,0:T(8,128)(2,1)S(1)}, bf16[2048,256]{1,0:T(8,128)(2,1)}, u32[]{:S(2)}) copy-start(bf16[2048,256]{1,0:T(8,128)(2,1)} %get-tuple-element.86.refs_3_.state_w) | copy-start | bytes 3145732
  581.8 1.2 copy-start.1
  583.0 0.9 copy-start.2
  584.0 19.1 %copy-start.8 = (f32[256,1024]{1,0:T(8,128)S(1)}, f32[256,1024]{1,0:T(8,128)}, u32[]{:S(2)}) copy-start(f32[256,1024]{1,0:T(8,128)} %get-tuple-element.251) | copy-start | bytes 3145732
  592.1 12.0 %copy-start.7 = (f32[256,1024]{1,0:T(8,128)S(1)}, f32[256,1024]{1,0:T(8,128)}, u32[]{:S(2)}) copy-start(f32[256,1024]{1,0:T(8,128)} %get-tuple-element.252) | copy-start | bytes 3145732
  603.1 1.9 copy-start.9
  603.1 2.7 copy-start.6
Sparse Core Ops, SparseCore 0:
  11.5 83.4 all-gather.2
  97.1 81.0 all-gather.4
  380.1 48.8 all-reduce.17
  478.1 97.5 reduce-scatter.1

commit v6 on v5

--- a/solution.py
+++ b/solution.py
@@ -496,7 +496,7 @@
     branch_out, lowgate_out, lowvalue_out, lowstep_out, gbc_out, gin_out, small_out, sums_out, stats_out,
     vbuf, gcbuf, gram_s, dgram, b_s, c_t, step_s, ent_s, fade_s, cums_s, cums_t, keep_s, grad_state,
     gin, gb_s, gc_s, u_s, v_s, fin_s, small_s, sums_s,
-    branch_s, rowsum_s, slots_s, turn_s, swap_send, swap_recv,
+    branch_s, rowsum_s, slots_s, turn_s, stats_s, swap_send, swap_recv,
 ):
     g, j = pl.program_id(0) - 1, pl.program_id(1)
     groups, blocks = pl.num_programs(0) - 1, pl.num_programs(1)
@@ -510,7 +510,7 @@
 
     scales = partial(
         row_scales, tp_size, gain_row.shape[1] * tp_size, rowsum_s, slots_s, turn_s, swap_send,
-        swap_recv, stats_out,
+        swap_recv, stats_s, stats_out,
     )
 
     @pl.when(g >= 0)
@@ -521,7 +521,7 @@
             gate_w, value_w, step_w, taps_ref, bias_ref, rate_ref, skip_ref, gain_ref, cols_ref, seg_ref,
             branch_out, lowgate_out, lowvalue_out, lowstep_out, gbc_out, gin_out, small_out, sums_out,
             vbuf, gcbuf, gram_s, dgram, b_s, c_t, step_s, ent_s, fade_s, cums_s, cums_t, keep_s,
-            grad_state, gin, gb_s, gc_s, u_s, v_s, fin_s, small_s, sums_s, branch_s, stats_out, scales,
+            grad_state, gin, gb_s, gc_s, u_s, v_s, fin_s, small_s, sums_s, branch_s, stats_s, scales,
         )
 
 
@@ -559,7 +559,7 @@
     ]
 
 
-def row_scales(tp_size, total_inner, rowsum_s, slots_s, turn_s, swap_send, swap_recv, stats_out):
+def row_scales(tp_size, total_inner, rowsum_s, slots_s, turn_s, swap_send, swap_recv, stats_s, stats_out):
     for copy in row_swaps(tp_size, rowsum_s, slots_s, swap_send, swap_recv):
         copy.wait()
     total = slots_s[0]
@@ -570,7 +570,9 @@
     turn_s[:, 0:1, :] = scale
     turn_s[:, 1:2, :] = scale * scale * scale * (total[:, 1:2, :] / total_inner)
     for group in range(turn_s.shape[0]):
-        stats_out[group * GROUP : (group + 1) * GROUP, :] = jnp.transpose(turn_s[group])
+        stats_s[group * GROUP : (group + 1) * GROUP, :] = jnp.transpose(turn_s[group])
+    rows = stats_out.shape[0]
+    stats_out[...] = stats_s[pl.ds(pl.multiple_of(lax.axis_index("tp") * rows, rows), rows), :]
 
 
 def backward_step(
@@ -851,12 +853,13 @@
         out_specs=[
             wide, wide, wide, rows_of(128), rows_of(2 * STATE),
             rows_of(model), pl.BlockSpec((8, inner), lambda g, j: (0, 0)), pl.BlockSpec((8, 128), lambda g, j: (0, 0)),
-            pl.BlockSpec((length, 128), lambda g, j: (0, 0)),
+            pl.BlockSpec((length // tp_size, 128), lambda g, j: (0, 0)),
         ] + specs,
         out_shape=[
             shape((length, inner), BF16), shape((length, inner), BF16), shape((length, inner), BF16),
             shape((length, 128), BF16), shape((length, 2 * STATE), BF16),
-            shape((length, model), BF16), shape((8, inner)), shape((8, 128)), shape((length, 128)),
+            shape((length, model), BF16), shape((8, inner)), shape((8, 128)),
+            shape((length // tp_size, 128)),
         ] + shapes,
         scratch_shapes=[
             pltpu.VMEM((GROUP + HALO, BLOCK), F32),
@@ -884,6 +887,7 @@
             pltpu.VMEM((groups, 8, GROUP), F32),
             pltpu.VMEM((tp_size, groups, 8, GROUP), F32),
             pltpu.VMEM((groups, 128, GROUP), F32),
+            pltpu.VMEM((length, 128), F32),
             pltpu.SemaphoreType.DMA((tp_size - 1,)),
             pltpu.SemaphoreType.DMA((tp_size - 1,)),
         ] + hosted.scratch() + resident_scratch(resident),
@@ -1140,16 +1144,23 @@
 
 def tail_kernel(chips, tp_size, micro, widths, *refs):
     columns, lows, parts, raws = refs[:4], refs[4:12], refs[12:14], refs[14:16]
-    cols_ref, staps_ref, sbias_ref, pack = refs[16:20]
-    outs, state_out, pack_out, ssum_out, low_out = refs[20:24], refs[24], refs[25], refs[26], refs[27]
+    cols_ref, staps_ref, sbias_ref = refs[16:19]
+    pieces = refs[19:23]
+    outs, state_out, pack_out, ssum_out, low_out = refs[23:27], refs[27], refs[28], refs[29], refs[30]
     (
         cols_s, give, took, mine, came, passed, total_s, kept_s,
         sgive, stook, smine, scame, stotal, skept_s,
-        pack_took, pack_sum, pack_slots, ssum, ssum_took, ssum_sum, ssum_slots,
+        pack, pack_took, pack_sum, pack_slots, ssum, ssum_took, ssum_sum, ssum_slots,
         raw_s, own_s, slots_s, whole_s, sum_s, low_s, vbuf, gcbuf,
         cols_sem, give_sem, took_sem, send_sem, recv_sem, sgive_sem, stook_sem, ssend_sem, srecv_sem,
         pass_sem, pack_sem, ssum_sem, raw_sem, own_sem, part_send, part_recv, whole_send, whole_recv,
-    ) = refs[28:]
+        *stored, low_sem,
+    ) = refs[31:]
+    loads = [
+        pltpu.make_async_copy(low, kept, low_sem.at[at])
+        for at, (low, kept) in enumerate(zip(lows, stored))
+    ]
+    lows = stored
     step, steps = pl.program_id(0), pl.num_programs(0)
     me, line = lax.axis_index("fsdp"), lax.axis_index("tp")
     count = 2 * chips
@@ -1270,6 +1281,11 @@
         )
         for hop in range(1, tp_size):
             handing(hop).start()
+        for load in loads:
+            load.start()
+        pack[0:8, :] = pieces[0][...] + pieces[1][...]
+        pack[8:16, :] = jnp.zeros((8, pack.shape[1]), F32)
+        pack[8:16, 0:128] = pieces[2][...] + pieces[3][...]
         pack_pass.start()
 
     @pl.when(step + 1 < count)
@@ -1304,6 +1320,12 @@
     def _():
         at = 0
         for which, width in enumerate(widths):
+
+            @pl.when(step == 0)
+            def _():
+                loads[2 * which].wait()
+                loads[2 * which + 1].wait()
+
             give[hop, :, at : at + width] = tile(which).astype(BF16)
             at += width
         giving(hop).start()
@@ -1470,24 +1492,24 @@
             sgiving(other).wait_send()
 
 
-def tail_call(count, tp_size, inputs, cotans, lows, parts, raws, cols, staps, sbias, pack):
+def tail_call(count, tp_size, inputs, cotans, lows, parts, raws, cols, staps, sbias, pieces):
     micro, length = len(inputs), inputs[0].shape[0]
     chips = count // 2
     order = [low[which] for which in range(4) for low in lows]
     widths = [low.shape[1] for low in order[::2]]
     total, narrow = sum(widths), 2 * STATE
+    packed = (16, pieces[0].shape[1])
     hbm = pl.BlockSpec(memory_space=pl.ANY)
     full = lambda array: pl.BlockSpec(array.shape, lambda i: (0,) * array.ndim, pipeline_mode=pl.Buffered(1))
     out_dims = [(BLOCK, width) for width in widths[:3]] + [(widths[3], BLOCK), (BLOCK, narrow)]
     out_shapes = [shape(dims) for dims in out_dims] + [
-        shape(pack.shape), shape((8, narrow)), shape((micro, GROUP, narrow), BF16)
+        shape(packed), shape((8, narrow)), shape((micro, GROUP, narrow), BF16)
     ]
     dma = lambda *dims: pltpu.SemaphoreType.DMA(dims)
     return pl.pallas_call(
         partial(tail_kernel, chips, tp_size, micro, widths),
         grid=(2 * count,),
-        in_specs=[hbm] * 4 + [full(low) for low in order] + [hbm] * 4
-        + [full(cols), full(staps), full(sbias), full(pack)],
+        in_specs=[hbm] * 16 + [full(each) for each in (cols, staps, sbias) + pieces],
         out_specs=[full(each) for each in out_shapes],
         out_shape=out_shapes,
         scratch_shapes=[
@@ -1505,9 +1527,10 @@
             pltpu.VMEM((chips - 1, BLOCK, narrow), BF16),
             pltpu.VMEM((BLOCK, narrow), F32),
             pltpu.VMEM((BLOCK, narrow), F32),
-            pltpu.VMEM(pack.shape, F32),
-            pltpu.VMEM(pack.shape, F32),
-            pltpu.VMEM((chips,) + pack.shape, F32),
+            pltpu.VMEM(packed, F32),
+            pltpu.VMEM(packed, F32),
+            pltpu.VMEM(packed, F32),
+            pltpu.VMEM((chips,) + packed, F32),
             pltpu.VMEM((8, narrow), F32),
             pltpu.VMEM((8, narrow), F32),
             pltpu.VMEM((8, narrow), F32),
@@ -1524,7 +1547,7 @@
             dma(chips), dma(chips), dma(chips - 1), dma(chips - 1),
             dma(2, 2), dma(2, chips), dma(2, chips), dma(micro), dma(micro),
             dma(tp_size - 1), dma(tp_size - 1), dma(tp_size - 1), dma(tp_size - 1),
-        ],
+        ] + [pltpu.VMEM(low.shape, BF16) for low in order] + [dma(len(order))],
         compiler_params=pltpu.CompilerParams(
             collective_id=6, has_side_effects=True, vmem_limit_bytes=62 << 20
         ),
@@ -1532,18 +1555,18 @@
             flops=4 * length * BLOCK * count * total, bytes_accessed=250 << 20, transcendentals=0
         ),
         name="weight_gradients",
-    )(*inputs, *cotans, *order, *parts, *raws, cols, staps, sbias, pack)
+    )(*inputs, *cotans, *order, *parts, *raws, cols, staps, sbias, *pieces)
 
 
 def rows_kernel(
-    sum0, sum1, low_ref, state_w, rows_ref, cot_ref, gain_ref, made0, made1, scale_ref,
+    sum0, sum1, low_ref, state_w, rows_ref, cot_ref, gain_ref, made0, made1, scale0, scale1,
     hidden_out, block_out, gain_out,
 ):
     step = pl.program_id(0)
     half = pl.num_programs(0) // 2
     gain = gain_ref[...]
 
-    def work(summed, made):
+    def work(summed, made, scale_ref):
         grad = summed[...].astype(F32) + mm_nt(low_ref[0], state_w[...])
         rows = rows_ref[0].astype(F32)
         inv_root = lax.rsqrt(jnp.mean(rows * rows, axis=1, keepdims=True) + EPSILON)
@@ -1552,7 +1575,7 @@
         inner = jnp.mean(normed * rows, axis=1, keepdims=True)
         back = inv_root * normed - rows * (inv_root * inv_root * inv_root * inner)
         hidden_out[0] = (cot_ref[0].astype(F32) + back).astype(BF16)
-        block_out[0] = (rows + made[...] * scale_ref[0][:, 0:1]).astype(BF16)
+        block_out[0] = (rows + made[...] * scale_ref[:, 0:1]).astype(BF16)
         width = gain_out.shape[1]
         for at in range(gain_out.shape[0]):
             piece = part[:, at * width : (at + 1) * width]
@@ -1567,11 +1590,11 @@
 
     @pl.when(step < half)
     def _():
-        work(sum0, made0)
+        work(sum0, made0, scale0)
 
     @pl.when(step >= half)
     def _():
-        work(sum1, made1)
+        work(sum1, made1, scale1)
 
 
 def rows_call(sums, lows, state_w, rows, cotan, gain, made, scales):
@@ -1579,22 +1602,23 @@
     tiles = 2
     tile = length // tiles
     both = lambda width: pl.BlockSpec((1, tile, width), lambda i: (i // tiles, i % tiles, 0))
-    former = pl.BlockSpec((tile, model), lambda i: (jnp.minimum(i, tiles - 1), 0))
-    latter = pl.BlockSpec((tile, model), lambda i: (jnp.maximum(i - tiles, 0), 0))
+    former_of = lambda width: pl.BlockSpec((tile, width), lambda i: (jnp.minimum(i, tiles - 1), 0))
+    latter_of = lambda width: pl.BlockSpec((tile, width), lambda i: (jnp.maximum(i - tiles, 0), 0))
+    former, latter = former_of(model), latter_of(model)
     full = lambda dims: pl.BlockSpec(dims, lambda i: (0, 0))
     return pl.pallas_call(
         rows_kernel,
         grid=(micro * tiles,),
         in_specs=[
             former, latter, both(2 * STATE), full(state_w.shape), both(model), both(model),
-            full(gain.shape), former, latter, both(128),
+            full(gain.shape), former, latter, former_of(128), latter_of(128),
         ],
         out_specs=[both(model), both(model), full((8, model // 8))],
         out_shape=[shape(rows.shape, BF16), shape(rows.shape, BF16), shape((8, model // 8))],
         compiler_params=pltpu.CompilerParams(vmem_limit_bytes=50 << 20),
         cost_estimate=pl.CostEstimate(flops=1 << 30, bytes_accessed=18 << 20, transcendentals=0),
         name="finish_rows",
-    )(*sums, lows, state_w, rows, cotan, gain, *made, scales)
+    )(*sums, lows, state_w, rows, cotan, gain, *made, *scales)
 
 
 def gain_kernel(
@@ -1808,14 +1832,11 @@
     summed = [gin_sum, scatter_tp(latter[5])]
     lows = [[each[1], each[2], each[3], each[0]] for each in (former, latter)]
     parts, raws = (early, latter[4]), [each[4] for each in saved]
-    inner_here = proj_gate.shape[1]
-    pack = jnp.concatenate(
-        [former[6] + latter[6], jnp.pad(former[7] + latter[7], ((0, 0), (0, inner_here - 128)))], axis=0
-    )
+    pieces = (former[6], latter[6], former[7], latter[7])
     if aligned and fsdp_size == 8 and model // fsdp_size == BLOCK:
         grad_gate, grad_value, grad_step, grad_out, grad_state, pack, state_sum, mine = tail_call(
             fsdp_size, tp_size, inputs, cotans, lows, parts, raws, jnp.concatenate(columns, axis=0),
-            staps, sbias, pack,
+            staps, sbias, pieces,
         )
     else:
         mine, state_sum = [], 0.0
@@ -1837,14 +1858,13 @@
         grad_gate, grad_value, grad_state, grad_step, grad_out = scatter_call(
             fsdp_size, (grad_gate, grad_value, grad_state, grad_step, grad_out), axes
         )
+        narrow = jnp.pad(pieces[2] + pieces[3], ((0, 0), (0, proj_gate.shape[1] - 128)))
+        pack = jnp.concatenate([pieces[0] + pieces[1], narrow], axis=0)
         pack, state_sum = lax.psum((pack, state_sum), "fsdp")
     grad_step = grad_step[:, :heads]
-    my_scales = jnp.stack(
-        [lax.dynamic_slice_in_dim(each, me * rows_here, rows_here, axis=0) for each in scales]
-    )
     grad_hidden, block_rows, gain_part = rows_call(
         summed, mine, state_w, hidden_in[:, 0], cotangent[:, 0], norm_gain[None, :],
-        produced, my_scales,
+        produced, scales,
     )
     gain_total = gain_call(tp_size, fsdp_size, gain_part)
     grad_gain, grad_skip, grad_conv, grad_bias, grad_sconv, grad_sbias, grad_in, grad_decay = (

time: 624 us -> 620 us (level)
  transfers between devices with their start and end apart: 4 -> 4, of which waited for: 1 -> 1; matrix products, arithmetic and copies ran while one was open for 2% -> 2% of each run, Pallas kernels for 54% -> 55%
where the time goes in v6:
time: 620 us; the launch traced here: 610 us
  Pallas kernels  554 us (89%)
  waiting for transfers between devices  21.2 us (3%)
  local copies, waits for them, and re-layouts  15.9 us (3%)
  between operations  14.4 us (2%)
    pallas_call x2, Pallas kernels, backward_call(): pl.pallas_call(hosted.wrap(partial(backward_kernel, tp_size), BACKWARD_IN...  199 us
    pallas_call x2, Pallas kernels, forward_call(): pl.pallas_call(hosted.wrap(forward_kernel, FORWARD_INS, FORWARD_OUTS, pac...  154 us
    pallas_call x1, Pallas kernels, tail_call(): pl.pallas_call(partial(tail_kernel, chips, tp_size, micro, widths), grid=...  96 us
    pallas_call x1, Pallas kernels, gather_call(): pl.pallas_call(partial(gather_kernel, count, pieces), in_specs=[pl.BlockS...  84.4 us
    all_gather x2, waiting for transfers between devices, gather_tp(): return lax.all_gather(values, 'tp', axis=0, tiled=True)  21.1 us
  transfers between devices with their start and end apart: 4, of which 1 were waited for; matrix products, arithmetic and copies ran while one was open for 2% of the time, Pallas kernels for 55%

profile of v6, /device:TPU:0, one launch (start us, length us, event | category | flops | bytes accessed | tf_op | source)
XLA Modules:
  0.0 610.4 jit_solution(531902370010855843)
XLA Ops:
  7.2 0.0 copy-start.6
  7.2 0.0 copy-start.5
  7.2 0.0 all-gather.3.cloned.1.call-start
  7.2 2.2 fusion.3
  9.4 0.0 copy-done.6
  9.4 0.0 copy-done.5
  9.4 0.0 copy-start.13
  9.5 1.9 fusion.5
  11.3 0.0 all-gather.3.cloned.1.call-update
  11.3 0.0 copy-start.14
  11.3 0.0 all-gather.5.cloned.1.call-start
  11.4 0.1 copy.77
  11.5 0.6 pad.53.refs_3_
  12.2 84.4 %gather_weights.1 = (bf16[2048,1024]{1,0:T(8,128)(2,1)}, bf16[2048,1024]{1,0:T(8,128)(2,1)}, bf16[2048,256]{1,0:T(8,128)(2,1)}, bf16[2048,128]{1,0:T(8,128)(2,1)}, bf16[1024,2048]{1,0:T(8,128)(2,1)}) custom-call(bf16[256,1024]{1,0:T(8,128)(2,1)} %refs_0_.1, bf16[256,1024]{1,0:T(8,128)(2,1)} %refs_1_.1, bf16[256,256]{1,0:T(8,128)(2,1)} %refs_2_.1, ...), custom_call_target="tpu_custom_call" | custom-call | bytes 262144000 | tf_op jit(solution)/shard_map/gather_weights/pallas_call | solution.py:982
  96.6 0.0 all-gather.3.cloned.1.call-done.refs_0_
  96.7 0.0 all-gather.5.cloned.1.call-update
  96.7 0.0 all-reduce.17.cloned.1.call-start
  96.7 0.0 copy-done.12
  96.7 0.6 convert_bitcast_fusion
  97.4 0.1 slice.80
  97.4 0.1 slice.81
  97.5 0.1 slice.89
  97.6 0.1 slice.90
  97.7 0.1 pad_add_fusion
  97.8 0.1 broadcast_bitcast_fusion.5
  97.9 0.1 broadcast_bitcast_fusion.2
  98.0 0.1 broadcast_bitcast_fusion.4
  98.0 0.1 broadcast_bitcast_fusion.1
  98.1 0.1 compare_convert_fusion.4
  98.2 0.1 broadcast_bitcast_fusion
  98.3 0.1 fusion.18
  98.4 0.1 stack.123
  98.5 1.0 copy.78.refs_12_.refs_21_
  99.5 0.1 broadcast_in_dim.55
  99.6 0.7 broadcast_in_dim_reshape.3.refs_11_.refs_19_
  100.2 0.1 broadcast_bitcast_fusion.3
  100.3 0.1 fusion.24
  100.4 0.1 stack.110
  100.5 1.0 copy.79.refs_12_.refs_21_
  101.5 0.0 copy-done.16
  101.5 0.5 pad_bitcast_fusion
  102.1 1.5 slice_bitcast_fusion
  103.5 53.6 %ssd_forward.2 = (bf16[1024,1024]{1,0:T(8,128)(2,1)}, f32[1024,1024]{1,0:T(8,128)}, f32[1024,1024]{1,0:T(8,128)}, bf16[1024,256]{1,0:T(8,128)(2,1)}, f32[1024,25...) custom-call(bf16[1024,2048]{1,0:T(8,128)(2,1)} %all-gather.3.cloned., ...), custom_call_target="tpu_custom_call" | custom-call | flops 15032385536 | bytes 41943040 | tf_op jit(solution)/shard_map/ssd_forward/pallas_call | solution.py:776
  157.1 21.1 %all-gather.5.cloned.1.call-done.refs_0_.refs_1_ = bf16[1024,2048]{1,0:T(8,128)(2,1)} async-done(((bf16[256,2048]{1,0:T(8,128)(2,1)}), bf16[1024,2048]{1,0:T(8,128)(2,1)}) %all-gather.5.cloned.1.call-update) | async-done | bytes 4194320 | tf_op jit(solution)/shard_map/all_gather | solution.py:1783
  178.2 100.1 %ssd_forward.3 = (bf16[1024,1024]{1,0:T(8,128)(2,1)}, f32[1024,1024]{1,0:T(8,128)}, f32[1024,1024]{1,0:T(8,128)}, bf16[1024,256]{1,0:T(8,128)(2,1)}, f32[1024,25...) custom-call(bf16[1024,2048]{1,0:T(8,128)(2,1)} %all-gather.5.cloned., ...), custom_call_target="tpu_custom_call" | custom-call | flops 15032385536 | bytes 41943040 | tf_op jit(solution)/shard_map/ssd_forward/pallas_call | solution.py:776
  278.3 101.3 %ssd_backward.2 = (bf16[1024,1024]{1,0:T(8,128)(2,1)}, bf16[1024,1024]{1,0:T(8,128)(2,1)}, bf16[1024,1024]{1,0:T(8,128)(2,1)}, bf16[1024,128]{1,0:T(8,128)(2,1)}...) custom-call(bf16[1024,2048]{1,0:T(8,128)(2,1)} %get-tuple-element.89, ...), custom_call_target="tpu_custom_call" | custom-call | flops 12884901888 | bytes 62914560 | tf_op jit(solution)/shard_map/ssd_backward/pallas_call | solution.py:842
  379.6 0.0 all-reduce.17.cloned.1.call-update
  379.7 0.0 reduce-scatter.2.cloned.1.call-start
  379.7 97.9 %ssd_backward.3 = (bf16[1024,1024]{1,0:T(8,128)(2,1)}, bf16[1024,1024]{1,0:T(8,128)(2,1)}, bf16[1024,1024]{1,0:T(8,128)(2,1)}, bf16[1024,128]{1,0:T(8,128)(2,1)}...) custom-call(bf16[1024,2048]{1,0:T(8,128)(2,1)} %get-tuple-element.98, ...), custom_call_target="tpu_custom_call" | custom-call | flops 12884901888 | bytes 62914560 | tf_op jit(solution)/shard_map/ssd_backward/pallas_call | solution.py:842
  477.6 0.0 reduce-scatter.2.cloned.1.call-update
  477.6 1.3 copy.82.refs_16_
  479.0 96.0 %weight_gradients.1 = (f32[256,1024]{1,0:T(8,128)}, f32[256,1024]{1,0:T(8,128)}, f32[256,128]{1,0:T(8,128)}, f32[1024,256]{1,0:T(8,128)}, f32[256,256]{1,0:T(8,1...) custom-call(bf16[1024,2048]{1,0:T(8,128)(2,1)} %all-gather.3.cloned.1.call-done.refs_0_, ...), custom_call_target="tpu_custom_call" | custom-call | flops 26843545600 | bytes 262144000 | tf_op jit(solution)/shard_map/weight_gradients/pallas_call | solution.py:1509
  575.0 1.6 copy.85
  576.6 1.8 small_gradients.1
  578.4 1.2 copy-done.1
  579.6 0.9 copy-done.2
  580.6 8.1 %finish_rows.1 = (bf16[2,256,2048]{2,1,0:T(8,128)(2,1)}, bf16[2,256,2048]{2,1,0:T(8,128)(2,1)}, f32[8,256]{1,0:T(8,128)S(1)}) custom-call(f32[256,2048]{1,0:T(8,128)} %get-tuple-element.107.sum0, bf16[256,2048]{1,0:T(8,128)(2,1)S(1)} %copy-done.1, bf16[2,256,256]{2,1,0:T(8,128)(2,1)S(1)} %copy-done.2, bf16[2048,256]{1,0:T(8,128)(2,1)S(1)} %copy-done, ...), custom_call_target="tpu_custom_call" | custom-call | flops 1073741824 | bytes 18874368 | tf_op jit(solution)/shard_map/finish_rows/pallas_call | solution.py:1609
  588.7 10.5 %gain_sum.1 = f32[8,256]{1,0:T(8,128)S(1)} custom-call(f32[8,256]{1,0:T(8,128)S(1)} %get-tuple-element.132.part), custom_call_target="tpu_custom_call" | custom-call | bytes 1048576 | tf_op jit(solution)/shard_map/gain_sum/pallas_call | solution.py:1668
  599.2 0.6 copy.92
  599.8 1.0 copy.98
  600.8 1.0 copy.99
  601.8 0.7 copy.100
  602.5 0.0 copy-done.8
  602.5 1.0 copy.101
  (35 shorter events, 0.1 us)
Async XLA Ops:
  7.2 2.2 copy-start.6
  7.2 2.2 copy-start.5
  7.2 89.5 %all-gather.3.cloned.1.call-start = ((), (), s32[]{:S(2)}) async-start(), calls=%async_computation.1 | async-start | bytes 5242880 | tf_op jit(solution)/shard_map/all_gather | solution.py:1783
  9.4 2.0 copy-start.13
  11.3 85.4 %copy-start.12 = (s32[2,1,1024]{2,1,0:T(1,128)S(1)}, s32[2,1,1024]{2,1,0:T(1,128)}, u32[]{:S(2)}) copy-start(s32[2,1,1024]{2,1,0:T(1,128)} %param.18) | copy-start | bytes 24580
  11.3 88.2 %copy-start.14 = (f32[16]{0:T(128)S(1)}, f32[16]{0:T(128)}, u32[]{:S(2)}) copy-start(f32[16]{0:T(128)} %param.31) | copy-start | bytes 196
  11.3 166.8 %all-gather.5.cloned.1.call-start = ((), (), s32[]{:S(2)}) async-start(), calls=%async_computation.2 | async-start | bytes 5242880 | tf_op jit(solution)/shard_map/all_gather | solution.py:1783
  12.2 89.4 %copy-start.16 = (f32[16]{0:T(128)S(1)}, f32[16]{0:T(128)}, u32[]{:S(2)}) copy-start(f32[16]{0:T(128)} %param.30) | copy-start | bytes 196
  12.2 89.4 %copy-start.15 = (f32[16]{0:T(128)S(1)}, f32[16]{0:T(128)}, u32[]{:S(2)}) copy-start(f32[16]{0:T(128)} %param.29) | copy-start | bytes 196
  12.2 89.9 %copy-start.7 = (bf16[2,1,256,2048]{3,2,1,0:T(8,128)(2,1)S(1)}, bf16[2,1,256,2048]{3,2,1,0:T(8,128)(2,1)}, u32[]{:S(2)}) copy-start(bf16[2,1,256,2048]{3,2,1,0:T(8,128)(2,1)} %param.19) | copy-start | bytes 6291460
  96.7 382.3 %all-reduce.17.cloned.1.call-start = ((), (), s32[]{:S(2)}) async-start(), calls=%async_computation.4 | async-start | bytes 1048576 | tf_op jit(solution)/shard_map/psum | solution.py:1830
  379.7 198.7 %reduce-scatter.2.cloned.1.call-start = ((), (), s32[]{:S(2)}) async-start(), calls=%async_computation.3 | async-start | bytes 5242880 | tf_op jit(solution)/shard_map/reduce_scatter | solution.py:1787
  479.0 99.4 %copy-start = (bf16[2048,256]{1,0:T(8,128)(2,1)S(1)}, bf16[2048,256]{1,0:T(8,128)(2,1)}, u32[]{:S(2)}) copy-start(bf16[2048,256]{1,0:T(8,128)(2,1)} %get-tuple-element.86.refs_3_.state_w) | copy-start | bytes 3145732
  479.0 99.4 %copy-start.3 = (f32[256,128]{1,0:T(8,128)S(1)}, f32[256,128]{1,0:T(8,128)}, u32[]{:S(2)}) copy-start(f32[256,128]{1,0:T(8,128)} %get-tuple-element.128.scale0) | copy-start | bytes 393220
  479.0 99.5 %copy-start.4 = (f32[256,128]{1,0:T(8,128)S(1)}, f32[256,128]{1,0:T(8,128)}, u32[]{:S(2)}) copy-start(f32[256,128]{1,0:T(8,128)} %get-tuple-element.129.scale1) | copy-start | bytes 393220
  578.4 1.2 copy-start.1
  579.6 0.9 copy-start.2
  580.6 19.2 %copy-start.10 = (f32[256,1024]{1,0:T(8,128)S(1)}, f32[256,1024]{1,0:T(8,128)}, u32[]{:S(2)}) copy-start(f32[256,1024]{1,0:T(8,128)} %get-tuple-element.251) | copy-start | bytes 3145732
  588.7 12.1 %copy-start.9 = (f32[256,1024]{1,0:T(8,128)S(1)}, f32[256,1024]{1,0:T(8,128)}, u32[]{:S(2)}) copy-start(f32[256,1024]{1,0:T(8,128)} %get-tuple-element.252) | copy-start | bytes 3145732
  599.8 1.9 copy-start.11
  599.8 2.7 copy-start.8
Sparse Core Ops, SparseCore 0:
  11.5 83.4 all-gather.2
  97.1 81.0 all-gather.4
  379.8 48.7 all-reduce.16
  477.7 95.0 reduce-scatter.1

commit v7 on v6

--- a/solution.py
+++ b/solution.py
@@ -18,7 +18,7 @@
 INNER = 4096
 EPSILON = 1e-05
 PRECISE = lax.Precision.HIGHEST
-PARTS = 2
+PARTS = 4
 FORWARD_INS, FORWARD_OUTS = 16, 9
 BACKWARD_INS, BACKWARD_OUTS = 23, 9
 F32 = jnp.float32
@@ -1802,8 +1802,11 @@
     vectors = (taps, bias, staps, sbias, step_bias_line, rate, skip)
     columns = [document_columns(segment_ids[at, 0]) for at in range(micro)]
     seg_lines = [segment_ids[at, 0].astype(F32)[None, :] for at in range(micro)]
-    quick = [0, 3, 7, 11, 14, 15, 15, 15, 15, 15]
-    paces = {4: [0, 3, 4, 6, 9, 12, 15, 17, 19, 19], 5: [0, 4, 4, 7, 10, 13, 18, 19]}
+    quick = [0, 2, 4, 6, 7, 9, 11, 13, 14] + [15] * 11
+    paces = {
+        4: [0, 1, 3, 4, 4, 5, 6, 8, 9, 11, 12, 13, 15, 16, 17, 18, 19, 19, 19, 19],
+        5: [0, 0, 4, 4, 4, 5, 7, 8, 10, 11, 13, 14, 17, 18, 19, 19],
+    }
 
     def forward(at, hosted):
         return forward_call(

time: 620 us -> 623 us (level)
  transfers between devices with their start and end apart: 4 -> 4, of which waited for: 1 -> 1; matrix products, arithmetic and copies ran while one was open for 2% -> 2% of each run, Pallas kernels for 55% -> 54%
where the time goes in v7:
time: 623 us; the launch traced here: 613 us
  Pallas kernels  556 us (89%)
  waiting for transfers between devices  21.2 us (3%)
  local copies, waits for them, and re-layouts  15.9 us (3%)
  between operations  14.2 us (2%)
    pallas_call x2, Pallas kernels, backward_call(): pl.pallas_call(hosted.wrap(partial(backward_kernel, tp_size), BACKWARD_IN...  199 us
    pallas_call x2, Pallas kernels, forward_call(): pl.pallas_call(hosted.wrap(forward_kernel, FORWARD_INS, FORWARD_OUTS, pac...  158 us
    pallas_call x1, Pallas kernels, tail_call(): pl.pallas_call(partial(tail_kernel, chips, tp_size, micro, widths), grid=...  93.2 us
    pallas_call x1, Pallas kernels, gather_call(): pl.pallas_call(partial(gather_kernel, count, pieces), in_specs=[pl.BlockS...  84.4 us
    all_gather x2, waiting for transfers between devices, gather_tp(): return lax.all_gather(values, 'tp', axis=0, tiled=True)  21.1 us
  transfers between devices with their start and end apart: 4, of which 1 were waited for; matrix products, arithmetic and copies ran while one was open for 2% of the time, Pallas kernels for 54%

profile of v7, /device:TPU:0, one launch (start us, length us, event | category | flops | bytes accessed | tf_op | source)
XLA Modules:
  0.0 612.5 jit_solution(12406787805174470357)
XLA Ops:
  7.2 0.0 copy-start.6
  7.2 0.0 copy-start.5
  7.2 0.0 all-gather.3.cloned.1.call-start
  7.2 2.2 fusion.3
  9.4 0.0 copy-done.6
  9.4 0.0 copy-done.5
  9.4 0.0 copy-start.13
  9.5 1.9 fusion.5
  11.3 0.0 all-gather.3.cloned.1.call-update
  11.3 0.0 copy-start.14
  11.3 0.0 all-gather.5.cloned.1.call-start
  11.4 0.0 copy-done.13
  11.4 0.1 copy.77
  11.5 0.6 pad.53.refs_3_
  12.2 84.4 %gather_weights.1 = (bf16[2048,1024]{1,0:T(8,128)(2,1)}, bf16[2048,1024]{1,0:T(8,128)(2,1)}, bf16[2048,256]{1,0:T(8,128)(2,1)}, bf16[2048,128]{1,0:T(8,128)(2,1)}, bf16[1024,2048]{1,0:T(8,128)(2,1)}) custom-call(bf16[256,1024]{1,0:T(8,128)(2,1)} %refs_0_.1, bf16[256,1024]{1,0:T(8,128)(2,1)} %refs_1_.1, bf16[256,256]{1,0:T(8,128)(2,1)} %refs_2_.1, ...), custom_call_target="tpu_custom_call" | custom-call | bytes 262144000 | tf_op jit(solution)/shard_map/gather_weights/pallas_call | solution.py:982
  96.6 0.0 all-gather.3.cloned.1.call-done.refs_0_
  96.7 0.0 all-gather.5.cloned.1.call-update
  96.7 0.0 all-reduce.17.cloned.1.call-start
  96.7 0.6 convert_bitcast_fusion
  97.4 0.1 slice.80
  97.4 0.1 slice.81
  97.5 0.1 slice.89
  97.6 0.1 slice.90
  97.7 0.1 pad_add_fusion
  97.8 0.1 broadcast_bitcast_fusion.5
  97.9 0.1 broadcast_bitcast_fusion.2
  98.0 0.1 broadcast_bitcast_fusion.4
  98.0 0.1 broadcast_bitcast_fusion.1
  98.1 0.1 compare_convert_fusion.4
  98.2 0.1 broadcast_bitcast_fusion
  98.3 0.1 fusion.18
  98.4 0.1 stack.123
  98.5 1.0 copy.78.refs_12_.refs_21_
  99.5 0.1 broadcast_in_dim.55
  99.6 0.7 broadcast_in_dim_reshape.3.refs_11_.refs_19_
  100.2 0.1 broadcast_bitcast_fusion.3
  100.3 0.1 fusion.24
  100.4 0.1 stack.110
  100.5 1.0 copy.79.refs_12_.refs_21_
  101.5 0.5 pad_bitcast_fusion
  102.1 0.0 copy-done.7
  102.1 1.5 slice_bitcast_fusion
  103.5 53.6 %ssd_forward.2 = (bf16[1024,1024]{1,0:T(8,128)(2,1)}, f32[1024,1024]{1,0:T(8,128)}, f32[1024,1024]{1,0:T(8,128)}, bf16[1024,256]{1,0:T(8,128)(2,1)}, f32[1024,25...) custom-call(bf16[1024,2048]{1,0:T(8,128)(2,1)} %all-gather.3.cloned., ...), custom_call_target="tpu_custom_call" | custom-call | flops 15032385536 | bytes 41943040 | tf_op jit(solution)/shard_map/ssd_forward/pallas_call | solution.py:776
  157.1 21.1 %all-gather.5.cloned.1.call-done.refs_0_.refs_1_ = bf16[1024,2048]{1,0:T(8,128)(2,1)} async-done(((bf16[256,2048]{1,0:T(8,128)(2,1)}), bf16[1024,2048]{1,0:T(8,128)(2,1)}) %all-gather.5.cloned.1.call-update) | async-done | bytes 4194320 | tf_op jit(solution)/shard_map/all_gather | solution.py:1783
  178.2 104.6 %ssd_forward.3 = (bf16[1024,1024]{1,0:T(8,128)(2,1)}, f32[1024,1024]{1,0:T(8,128)}, f32[1024,1024]{1,0:T(8,128)}, bf16[1024,256]{1,0:T(8,128)(2,1)}, f32[1024,25...) custom-call(bf16[1024,2048]{1,0:T(8,128)(2,1)} %all-gather.5.cloned., ...), custom_call_target="tpu_custom_call" | custom-call | flops 15032385536 | bytes 41943040 | tf_op jit(solution)/shard_map/ssd_forward/pallas_call | solution.py:776
  282.8 101.6 %ssd_backward.2 = (bf16[1024,1024]{1,0:T(8,128)(2,1)}, bf16[1024,1024]{1,0:T(8,128)(2,1)}, bf16[1024,1024]{1,0:T(8,128)(2,1)}, bf16[1024,128]{1,0:T(8,128)(2,1)}...) custom-call(bf16[1024,2048]{1,0:T(8,128)(2,1)} %get-tuple-element.89, ...), custom_call_target="tpu_custom_call" | custom-call | flops 12884901888 | bytes 62914560 | tf_op jit(solution)/shard_map/ssd_backward/pallas_call | solution.py:842
  384.5 0.0 all-reduce.17.cloned.1.call-update
  384.5 0.0 reduce-scatter.2.cloned.1.call-start
  384.5 97.8 %ssd_backward.3 = (bf16[1024,1024]{1,0:T(8,128)(2,1)}, bf16[1024,1024]{1,0:T(8,128)(2,1)}, bf16[1024,1024]{1,0:T(8,128)(2,1)}, bf16[1024,128]{1,0:T(8,128)(2,1)}...) custom-call(bf16[1024,2048]{1,0:T(8,128)(2,1)} %get-tuple-element.98, ...), custom_call_target="tpu_custom_call" | custom-call | flops 12884901888 | bytes 62914560 | tf_op jit(solution)/shard_map/ssd_backward/pallas_call | solution.py:842
  482.4 0.0 reduce-scatter.2.cloned.1.call-update
  482.4 1.3 copy.82.refs_16_
  483.7 93.2 %weight_gradients.1 = (f32[256,1024]{1,0:T(8,128)}, f32[256,1024]{1,0:T(8,128)}, f32[256,128]{1,0:T(8,128)}, f32[1024,256]{1,0:T(8,128)}, f32[256,256]{1,0:T(8,1...) custom-call(bf16[1024,2048]{1,0:T(8,128)(2,1)} %all-gather.3.cloned.1.call-done.refs_0_, ...), custom_call_target="tpu_custom_call" | custom-call | flops 26843545600 | bytes 262144000 | tf_op jit(solution)/shard_map/weight_gradients/pallas_call | solution.py:1509
  576.9 1.6 copy.85
  578.5 1.8 small_gradients.1
  580.4 1.2 copy-done.1
  581.6 0.9 copy-done.2
  582.6 8.1 %finish_rows.1 = (bf16[2,256,2048]{2,1,0:T(8,128)(2,1)}, bf16[2,256,2048]{2,1,0:T(8,128)(2,1)}, f32[8,256]{1,0:T(8,128)S(1)}) custom-call(f32[256,2048]{1,0:T(8,128)} %get-tuple-element.107.sum0, bf16[256,2048]{1,0:T(8,128)(2,1)S(1)} %copy-done.1, bf16[2,256,256]{2,1,0:T(8,128)(2,1)S(1)} %copy-done.2, bf16[2048,256]{1,0:T(8,128)(2,1)S(1)} %copy-done, ...), custom_call_target="tpu_custom_call" | custom-call | flops 1073741824 | bytes 18874368 | tf_op jit(solution)/shard_map/finish_rows/pallas_call | solution.py:1609
  590.6 11.0 %gain_sum.1 = f32[8,256]{1,0:T(8,128)S(1)} custom-call(f32[8,256]{1,0:T(8,128)S(1)} %get-tuple-element.132.part), custom_call_target="tpu_custom_call" | custom-call | bytes 1048576 | tf_op jit(solution)/shard_map/gain_sum/pallas_call | solution.py:1668
  601.6 0.6 copy.92
  602.2 1.0 copy.98
  603.2 1.0 copy.99
  604.1 0.0 copy-done.11
  604.1 0.7 copy.100
  604.9 1.0 copy.101
  (35 shorter events, 0.1 us)
Async XLA Ops:
  7.2 2.2 copy-start.6
  7.2 2.2 copy-start.5
  7.2 89.5 %all-gather.3.cloned.1.call-start = ((), (), s32[]{:S(2)}) async-start(), calls=%async_computation.1 | async-start | bytes 5242880 | tf_op jit(solution)/shard_map/all_gather | solution.py:1783
  9.4 2.0 copy-start.13
  11.3 85.4 %copy-start.12 = (s32[2,1,1024]{2,1,0:T(1,128)S(1)}, s32[2,1,1024]{2,1,0:T(1,128)}, u32[]{:S(2)}) copy-start(s32[2,1,1024]{2,1,0:T(1,128)} %param.18) | copy-start | bytes 24580
  11.3 88.2 %copy-start.14 = (f32[16]{0:T(128)S(1)}, f32[16]{0:T(128)}, u32[]{:S(2)}) copy-start(f32[16]{0:T(128)} %param.31) | copy-start | bytes 196
  11.3 166.8 %all-gather.5.cloned.1.call-start = ((), (), s32[]{:S(2)}) async-start(), calls=%async_computation.2 | async-start | bytes 5242880 | tf_op jit(solution)/shard_map/all_gather | solution.py:1783
  12.2 89.4 %copy-start.16 = (f32[16]{0:T(128)S(1)}, f32[16]{0:T(128)}, u32[]{:S(2)}) copy-start(f32[16]{0:T(128)} %param.30) | copy-start | bytes 196
  12.2 89.4 %copy-start.15 = (f32[16]{0:T(128)S(1)}, f32[16]{0:T(128)}, u32[]{:S(2)}) copy-start(f32[16]{0:T(128)} %param.29) | copy-start | bytes 196
  12.2 89.9 %copy-start.7 = (bf16[2,1,256,2048]{3,2,1,0:T(8,128)(2,1)S(1)}, bf16[2,1,256,2048]{3,2,1,0:T(8,128)(2,1)}, u32[]{:S(2)}) copy-start(bf16[2,1,256,2048]{3,2,1,0:T(8,128)(2,1)} %param.19) | copy-start | bytes 6291460
  96.7 387.0 %all-reduce.17.cloned.1.call-start = ((), (), s32[]{:S(2)}) async-start(), calls=%async_computation.4 | async-start | bytes 1048576 | tf_op jit(solution)/shard_map/psum | solution.py:1833
  384.5 195.9 %reduce-scatter.2.cloned.1.call-start = ((), (), s32[]{:S(2)}) async-start(), calls=%async_computation.3 | async-start | bytes 5242880 | tf_op jit(solution)/shard_map/reduce_scatter | solution.py:1787
  483.7 96.6 %copy-start = (bf16[2048,256]{1,0:T(8,128)(2,1)S(1)}, bf16[2048,256]{1,0:T(8,128)(2,1)}, u32[]{:S(2)}) copy-start(bf16[2048,256]{1,0:T(8,128)(2,1)} %get-tuple-element.86.refs_3_.state_w) | copy-start | bytes 3145732
  483.7 96.7 %copy-start.3 = (f32[256,128]{1,0:T(8,128)S(1)}, f32[256,128]{1,0:T(8,128)}, u32[]{:S(2)}) copy-start(f32[256,128]{1,0:T(8,128)} %get-tuple-element.128.scale0) | copy-start | bytes 393220
  483.7 96.7 %copy-start.4 = (f32[256,128]{1,0:T(8,128)S(1)}, f32[256,128]{1,0:T(8,128)}, u32[]{:S(2)}) copy-start(f32[256,128]{1,0:T(8,128)} %get-tuple-element.129.scale1) | copy-start | bytes 393220
  580.4 1.2 copy-start.1
  581.6 0.9 copy-start.2
  582.6 19.6 %copy-start.10 = (f32[256,1024]{1,0:T(8,128)S(1)}, f32[256,1024]{1,0:T(8,128)}, u32[]{:S(2)}) copy-start(f32[256,1024]{1,0:T(8,128)} %get-tuple-element.251) | copy-start | bytes 3145732
  590.6 12.5 %copy-start.9 = (f32[256,1024]{1,0:T(8,128)S(1)}, f32[256,1024]{1,0:T(8,128)}, u32[]{:S(2)}) copy-start(f32[256,1024]{1,0:T(8,128)} %get-tuple-element.252) | copy-start | bytes 3145732
  602.2 1.9 copy-start.11
  602.2 2.7 copy-start.8
Sparse Core Ops, SparseCore 0:
  11.5 83.4 all-gather.2
  97.1 81.0 all-gather.4
  384.6 48.5 all-reduce.16
  482.5 93.6 reduce-scatter.1
